TPU v7x, 512 devices: a whole 4x4x16 slice. The times are simulated.
512 devices in a mesh: ctx: 64 (over z, x), tp: 8 (over y, core).
Axes of the slice: x: 4, y: 4, z: 16, core: 2. Of those that a mesh axis runs over, the one named last changes fastest.
Arguments:
- outer_input: bfloat16 [4096, 8192], P('ctx', 'tp'), may hold values from -6 to 6
- inner_input: bfloat16 [4096, 8192], P('ctx', 'tp'), may hold values from -6 to 6
- value_input: bfloat16 [4096, 8192], P('ctx', 'tp'), may hold values from -6 to 6
- feature_taps: bfloat16 [3, 7, 8192], P(None, None, 'tp'), may hold values from -2 to 2
- medium_taps: bfloat16 [128, 512], P(None, 'tp'), may hold values from -0.5 to 0.5
- decay_rates: float32 [512, 16], P('tp'), may hold values from 1e-05 to 0.04
- residues: float32 [512, 16], P('tp'), may hold values from -4 to 4
- residual: bfloat16 [4096, 8192], P('ctx', 'tp'), may hold values from -72 to 72
- norm_gain: bfloat16 [8192], P('tp'), may hold values from 0.5 to 1.5
Outputs:
- normed: bfloat16 [4096, 8192], P('ctx', 'tp')
All inputs are finite; a program needn't handle non-finite values.
Results may differ from a plain program's by a relative error of at most 0.0039.
Values may be sent and summed in bfloat16 or wider, within the bound.
No kernel may reach another device: no remote copies, remote signals or barrier semaphores. Data moves between devices by JAX's collectives and lax.ppermute only.
A program may use at most 128 MiB of HBM per device.

v0:
```python
import jax
import jax.numpy as jnp
from jax import lax
from jax.sharding import PartitionSpec as P

D = 8192


def passed_along(array, axis, by):
    size = lax.axis_size(axis)
    pairs = [(i, i + by) for i in range(size) if 0 <= i + by < size]
    return lax.ppermute(array, axis, pairs)


def entering(part, axis, combine, identity):
    place = lax.axis_index(axis)
    gathered = jax.tree.map(lambda a: lax.all_gather(a, axis), part)
    state = jax.tree.map(lambda a, e: jnp.zeros_like(a) + jnp.asarray(e, a.dtype), part, identity)

    def one(lap, state):
        return combine(
            state, jax.tree.map(lambda a: lax.dynamic_index_in_dim(a, lap, 0, False), gathered)
        )

    return lax.fori_loop(0, place, one, state)


def banded(reversed_taps, row_count, width):
    group_count, tap_count = reversed_taps.shape
    period = width + 1
    padded = jnp.pad(reversed_taps, ((0, 0), (0, period - tap_count)))
    tiled = jnp.tile(padded, (1, row_count))
    return tiled[:, : row_count * width].reshape(group_count, row_count, width)


def featurize(extended, tap_table, row_count):
    rim_rows = tap_table.shape[0] - 1
    summed = jnp.zeros((row_count, extended.shape[1]), jnp.float32)
    for offset in range(tap_table.shape[0]):
        window = extended[rim_rows - offset : rim_rows - offset + row_count].astype(jnp.float32)
        summed = summed + tap_table[offset].astype(jnp.float32)[None, :] * window
    return summed


def product_rim(product, rim_depth):
    row_count = product.shape[0]
    pieces = []
    for distance in range(1, (rim_depth - 1) // row_count + 2):
        needed = min(row_count, rim_depth - (distance - 1) * row_count)
        arrived = passed_along(product[row_count - needed :], "ctx", distance)
        pieces = [arrived] + pieces
    return jnp.concatenate(pieces, 0)


def combine_modes(earlier, later):
    return (earlier[0] * later[0], earlier[1] * later[0] + later[1])


def on_device(
    outer_input,
    inner_input,
    value_input,
    feature_taps,
    medium_taps,
    decay_rates,
    residues,
    residual,
    norm_gain,
):
    row_count, channels = outer_input.shape
    group_count, mode_count = decay_rates.shape
    group_width = channels // group_count
    feat_rim = feature_taps.shape[1] - 1
    medium_rim = medium_taps.shape[0] - 1
    highest = lax.Precision.HIGHEST
    rim_outer, rim_inner, rim_value = passed_along(
        (
            outer_input[row_count - feat_rim :],
            inner_input[row_count - feat_rim :],
            value_input[row_count - feat_rim :],
        ),
        "ctx",
        1,
    )
    inner_feat = featurize(jnp.concatenate([rim_inner, inner_input], 0), feature_taps[1], row_count)
    value_feat = featurize(jnp.concatenate([rim_value, value_input], 0), feature_taps[2], row_count)
    product = (inner_feat * value_feat).astype(jnp.bfloat16)
    extended = jnp.concatenate([product_rim(product, medium_rim), product], 0)
    outer_feat = featurize(jnp.concatenate([rim_outer, outer_input], 0), feature_taps[0], row_count)
    band_medium = banded(medium_taps[::-1].T, row_count, row_count + medium_rim)
    extended_groups = extended.reshape(row_count + medium_rim, group_count, group_width)
    medium_part = jnp.einsum(
        "gts,sgc->tgc", band_medium, extended_groups, preferred_element_type=jnp.float32
    )
    lag_rows = jnp.arange(row_count, dtype=jnp.float32)[:, None, None]
    mode_weight = residues * jnp.sqrt(2.0 * decay_rates / mode_count)
    powers = jnp.exp(-decay_rates[None] * lag_rows)
    long_taps = jnp.sum(powers * mode_weight[None], axis=2)
    band_long = banded(long_taps[::-1].T, row_count, 2 * row_count - 1)[:, :, row_count - 1 :]
    product_wide = product.reshape(row_count, group_count, group_width).astype(jnp.float32)
    within = jnp.einsum("gts,sgc->tgc", band_long, product_wide, precision=highest)
    to_end = jnp.exp(-decay_rates[None] * (row_count - 1.0 - lag_rows))
    local_state = jnp.einsum("tgc,tgn->gcn", product_wide, to_end, precision=highest)
    block_decay = jnp.exp(-decay_rates * row_count)[:, None, :]
    neutral = (jnp.ones_like(block_decay), jnp.zeros_like(local_state))
    prefix = entering((block_decay, local_state), "ctx", combine_modes, neutral)
    incoming = prefix[1]
    from_start = powers * jnp.exp(-decay_rates)[None]
    carried = jnp.einsum(
        "tgn,gcn->tgc", from_start, incoming * mode_weight[:, None, :], precision=highest
    )
    mixed_conv = (medium_part + within + carried).reshape(row_count, channels)
    hidden = residual.astype(jnp.float32) + outer_feat * mixed_conv
    square_sum = lax.psum(jnp.sum(hidden * hidden, axis=1), "tp")
    normed = (
        hidden * norm_gain.astype(jnp.float32)[None, :] / jnp.sqrt(square_sum / D + 1e-05)[:, None]
    ).astype(jnp.bfloat16)
    return normed


def solution(mesh):
    return jax.shard_map(
        on_device,
        mesh=mesh,
        in_specs=(
            P("ctx", "tp"),
            P("ctx", "tp"),
            P("ctx", "tp"),
            P(None, None, "tp"),
            P(None, "tp"),
            P("tp", None),
            P("tp", None),
            P("ctx", "tp"),
            P("tp"),
        ),
        out_specs=P("ctx", "tp"),
        check_vma=False,
    )
```

profile of v0, /device:TPU:486, one launch (start us, length us, event | category | flops | bytes accessed | tf_op | source)
XLA Modules:
  0.0 437.2 jit_solution(1768202327101172436)
XLA Ops:
  7.5 1.3 collective-permute-start.1
  9.7 1.3 collective-permute-start.2
  11.0 1.2 slice_convert_fusion.20
  13.8 1.1 copy.31
  14.8 1.1 copy.34
  16.0 2.5 collective-permute-done.1
  18.5 4.5 %collective-permute-done.2 = bf16[6,1024]{0,1:T(8,128)(2,1)S(1)} collective-permute-done((bf16[6,1024]{0,1:T(8,128)(2,1)S(1)}, bf16[6,1024]{0,1:T(8,128)(2,1)S(1)}, u32[]{:S(2)}, u32[]{:S(2)}) %collective-permute-start.2) | collective-permute-done | bytes 12320 | tf_op jit(solution)/shard_map/ppermute | solution.py:12
  23.0 3.7 multiply_convert_fusion
  26.8 1.5 fusion.3
  29.0 1.3 collective-permute-start
  31.0 1.2 copy.46
  32.2 5.2 %reshape.228 = f32[64,64,127]{2,1,0:T(8,128)} reshape(f32[64,8128]{1,0:T(8,128)S(1)} %bitcast.55) | data formatting | bytes 4161536 | tf_op jit(solution)/shard_map/reshape | solution.py:33
  37.6 3.2 tile.9
  40.8 7.3 %reshape.226 = bf16[64,64,191]{2,1,0:T(8,128)(2,1)S(1)} reshape(bf16[64,12224]{1,0:T(8,128)(2,1)} %bitcast.58) | data formatting | bytes 3129344 | tf_op jit(solution)/shard_map/reshape | solution.py:33
  48.2 102.4 %all-gather.2 = f32[64,64,16]{1,2,0:T(8,128)S(1)} all-gather(f32[1,64,16]{1,2,0:T(8,128)S(1)} %get-tuple-element.99), channel_id=2, replica_groups=mesh['ctx'=64,'tp'=8] {'ctx'}, dimensions={0}, use_global_device_ids=true | all-gather | bytes 266240 | tf_op jit(solution)/shard_map/all_gather | solution.py:17
  150.7 1.3 collective-permute-start.4
  152.0 1.5 collective-permute-start.3
  153.5 3.5 fusion
  157.0 10.9 %collective-permute-done.3 = bf16[63,1024]{0,1:T(8,128)(2,1)S(1)} collective-permute-done((bf16[63,1024]{0,1:T(8,128)(2,1)S(1)}, bf16[63,1024]{0,1:T(8,128)(2,1)S(1)}, u32[]{:S(2)}, u32[]{:S(2)}) %collective-permute-start.3) | collective-permute-done | bytes 129056 | tf_op jit(solution)/shard_map/ppermute | solution.py:12
  169.0 159.7 %all-gather.5.cloned.1.call-done = f32[4096,16,16]{2,1,0:T(8,128)} async-done(((f32[64,16,16]{2,1,0:T(8,128)}), f32[4096,16,16]{2,1,0:T(8,128)}) %all-gather.5.cloned.1.call-update) | async-done | bytes 4194320 | tf_op jit(solution)/shard_map/all_gather | solution.py:17
  328.7 22.6 %copy.40 = f32[64,64,16,16]{1,3,2,0:T(8,128)} copy(f32[64,64,16,16]{3,2,1,0:T(8,128)} %bitcast.53) | data formatting | bytes 8388608 | tf_op jit(solution)/shard_map/while | solution.py:25
  351.3 62.7 %while.12 = (s32[]{:T(128)}, f32[64,16,16]{0,2,1:T(8,128)S(1)}, s32[]{:T(128)}, f32[64,64,1,16]{1,3,2,0:T(8,128)S(1)}, f32[64,64,16,16]{1,3,2,0:T(8,128)}, /*index=5*/s32[]{:T(128)}, s32[]{:T(128)}, s32[]{:T(128)}) while((s32[]{:T(128)}, f32[64,16,16]{0,2,1:T(8,128)S(1)}, s32[]{:T(128)}, f32[64,64,1,16]{1,3,2,0:T(8,128)S(1)}, ...), condition=%wide.region_2.3_spmd, body=%wide.region_1.2_spmd.sunk | while | flops 32773 | bytes 209023 | solution.py:25
  353.3 1.0 bitcast_add_fusion.2
  415.7 13.9 %psum.7 = f32[64]{0:T(128)S(1)} all-reduce(f32[64]{0:T(128)S(1)} %get-tuple-element.75), channel_id=1, replica_groups=mesh['ctx'=64,'tp'=8] {'tp'}, use_global_device_ids=true, to_apply=%region_4.5 | all-reduce | flops 64 | bytes 512 | tf_op jit(solution)/shard_map/psum | solution.py:114
  (167 shorter events, 68.5 us)
Async XLA Ops:
  6.5 322.1 %all-gather.5.cloned.1.call-start = ((), (), s32[]{:S(2)}) async-start(), calls=%async_computation | async-start | bytes 34078720 | tf_op jit(solution)/shard_map/all_gather | solution.py:17
  7.5 11.1 %collective-permute-start.1 = (bf16[6,1024]{0,1:T(8,128)(2,1)S(1)}, bf16[6,1024]{0,1:T(8,128)(2,1)S(1)}, u32[]{:S(2)}, u32[]{:S(2)}) collective-permute-start(bf16[6,1024]{0,1:T(8,128)(2,1)S(1)} %copy.32), channel_id=1, source_target_pairs={{0,8},{8,16},{16,24},{24,32},{32,40},{40,48},{48,56},{56,64},{64,7... | collective-permute-start | bytes 36872 | tf_op jit(solution)/shard_map/ppermute | solution.py:12
  9.7 13.3 %collective-permute-start.2 = (bf16[6,1024]{0,1:T(8,128)(2,1)S(1)}, bf16[6,1024]{0,1:T(8,128)(2,1)S(1)}, u32[]{:S(2)}, u32[]{:S(2)}) collective-permute-start(bf16[6,1024]{0,1:T(8,128)(2,1)S(1)} %copy.35), channel_id=1, source_target_pairs={{0,8},{8,16},{16,24},{24,32},{32,40},{40,48},{48,56},{56,64},{64,7... | collective-permute-start | bytes 36872 | tf_op jit(solution)/shard_map/ppermute | solution.py:12
  29.0 386.3 %collective-permute-start = (bf16[6,1024]{1,0:T(8,128)(2,1)S(1)}, bf16[6,1024]{1,0:T(8,128)(2,1)S(1)}, u32[]{:S(2)}, u32[]{:S(2)}) collective-permute-start(bf16[6,1024]{1,0:T(8,128)(2,1)S(1)} %slice.185), channel_id=1, source_target_pairs={{0,8},{8,16},{16,24},{24,32},{32,40},{40,48},{48,56},{56,64},{64,7... | collective-permute-start | bytes 36872 | tf_op jit(solution)/shard_map/ppermute | solution.py:12
  32.2 5.2 %copy-start.2 = (bf16[128,64]{0,1:T(8,128)(2,1)S(1)}, bf16[128,64]{0,1:T(8,128)(2,1)}, u32[]{:S(2)}) copy-start(bf16[128,64]{0,1:T(8,128)(2,1)} %param.15) | copy-start | bytes 49156
  40.8 7.4 %copy-start.3 = (bf16[1024]{0:T(1024)(128)(2,1)S(1)}, bf16[1024]{0:T(1024)(128)(2,1)}, u32[]{:S(2)}) copy-start(bf16[1024]{0:T(1024)(128)(2,1)} %param.19) | copy-start | bytes 6148
  150.7 17.2 %collective-permute-start.4 = (bf16[64,1024]{0,1:T(8,128)(2,1)S(1)}, bf16[64,1024]{0,1:T(8,128)(2,1)S(1)}, u32[]{:S(2)}, u32[]{:S(2)}) collective-permute-start(bf16[64,1024]{0,1:T(8,128)(2,1)S(1)} %multiply_convert_fusion), channel_id=1, source_target_pairs={{0,8},{8,16},{16,24},{24,32},{32,40},{40,48},{48,56},{56,64},{64,7... | collective-permute-start | bytes 393224 | tf_op jit(solution)/shard_map/ppermute | solution.py:12
  152.0 15.9 %collective-permute-start.3 = (bf16[63,1024]{0,1:T(8,128)(2,1)S(1)}, bf16[63,1024]{0,1:T(8,128)(2,1)S(1)}, u32[]{:S(2)}, u32[]{:S(2)}) collective-permute-start(bf16[63,1024]{0,1:T(8,128)(2,1)S(1)} %slice.259), channel_id=1, source_target_pairs={{0,16},{8,24},{16,32},{24,40},{32,48},{40,56},{48,64},{56,72},{64,... | collective-permute-start | bytes 387080 | tf_op jit(solution)/shard_map/ppermute | solution.py:12
  414.0 1.3 copy-start
  414.0 1.3 copy-start.1
Sparse Core Ops, SparseCore 0:
  28.4 300.2 all-gather.4
where the time goes:
time: 439 us; the launch traced here: 437 us
  waiting for transfers between devices  178 us (41%)
  blocking collectives  116 us (26%)
  other arithmetic  68.5 us (16%)
  local copies, waits for them, and re-layouts  46 us (10%)
  between operations  13.6 us (3%)
  starting transfers between devices  6.63 us (2%)
  matrix products  6.39 us (1%)
    all_gather x1, waiting for transfers between devices, entering(): gathered = jax.tree.map(lambda a: lax.all_gather(a, axis), part)  160 us
    all_gather x1, blocking collectives, entering(): gathered = jax.tree.map(lambda a: lax.all_gather(a, axis), part)  102 us
    add x63, other arithmetic, combine_modes(): return (earlier[0] * later[0], earlier[1] * later[0] + later[1])  60.1 us
    while x1, local copies, waits for them, and re-layouts, entering(): return lax.fori_loop(0, place, one, state)  22.6 us
    ppermute x5, waiting for transfers between devices, passed_along(): return lax.ppermute(array, axis, pairs)  18 us
    psum x1, blocking collectives, on_device(): square_sum = lax.psum(jnp.sum(hidden * hidden, axis=1), 'tp')  13.9 us
    reshape x2, local copies, waits for them, and re-layouts, banded(): return tiled[:, :row_count * width].reshape(group_count, row_count, width)  12.5 us
  transfers between devices with their start and end apart: 6, of which 4 were waited for; matrix products, arithmetic and copies ran while one was open for 26% of the time, Pallas kernels for 0%

commit v1 on v0

v1 whole, which is shorter than its diff:
```python
import functools

import jax
import jax.numpy as jnp
from jax import lax
from jax.experimental import pallas as pl
from jax.experimental.pallas import tpu as pltpu
from jax.sharding import PartitionSpec as P

D = 8192
F32 = jnp.float32
BF16 = jnp.bfloat16
LANES = 128
HALO = 8


def iota(shape, axis):
    return lax.broadcasted_iota(jnp.int32, shape, axis)


def split(x):
    high = x.astype(BF16)
    return high, (x - high.astype(F32)).astype(BF16)


def tables_kernel(place, decay_ref, residue_ref, medium_ref, table_ref, step_ref):
    group = place[0]
    modes = decay_ref.shape[1]
    taps, groups = medium_ref.shape
    square = (LANES, LANES)
    block = LANES // 2
    row, lane = iota(square, 0), iota(square, 1)
    pick = iota((modes, LANES), 0) == iota((modes, LANES), 1) % modes
    eye = iota((modes, modes), 0) == iota((modes, modes), 1)

    def column(ref):
        line = ref[pl.ds(group, 1), :]
        return jnp.sum(jnp.where(eye, jnp.broadcast_to(line, (modes, modes)), 0.0), 1, keepdims=True)

    rate = column(decay_ref)
    weight = column(residue_ref) * jnp.sqrt(2.0 * rate / modes)

    def along_lanes(x):
        return jnp.sum(jnp.where(pick, x, 0.0), 0, keepdims=True)

    def along_rows(x):
        return jnp.sum(jnp.where(row == lane, along_lanes(x), 0.0), 1, keepdims=True)

    lag = iota((modes, LANES), 1).astype(F32)
    long_row = jnp.sum(weight * jnp.exp(-rate * lag), 0, keepdims=True)
    one_hot = (iota((8, groups), 1) == group).astype(BF16)
    medium_row = lax.dot_general(
        one_hot, medium_ref[...], (((1,), (1,)), ((), ())), preferred_element_type=F32
    )[:1]
    zero_row = jnp.zeros((1, LANES), F32)

    def toeplitz(filter_row):
        wide = jnp.concatenate([filter_row, zero_row], 1)
        wide = jnp.broadcast_to(wide, (LANES, 2 * LANES))
        return pltpu.roll(wide, 0, 1, stride=1, stride_axis=0)

    same = row // block == lane // block
    medium_wide = toeplitz(medium_row)
    near = jnp.where(same, medium_wide[:, :LANES] + toeplitz(long_row)[:, :LANES], 0.0)
    near_high, near_low = split(near)
    middle = jnp.concatenate([medium_wide[:, block:LANES], medium_wide[:, LANES : LANES + block]], 1)
    table_ref[0] = near_high
    table_ref[1] = near_low
    table_ref[2] = jnp.where(same, middle, 0.0).astype(BF16)
    table_ref[3] = jnp.where(same, medium_wide[:, LANES:], 0.0).astype(BF16)
    width = 2 * modes
    rate_lanes, rate_rows, weight_rows = along_lanes(rate), along_rows(rate), along_rows(weight)
    to_end = jnp.exp(-rate_lanes * (block - 1 - row % block).astype(F32))
    to_end = jnp.where(((lane // modes) % 2 == row // block) & (lane < 3 * width), to_end, 0.0)
    table_ref[4], table_ref[5] = split(to_end)
    from_start = weight_rows * jnp.exp(-rate_rows * (lane % block + 1).astype(F32))
    from_start = jnp.where(((row // modes) % 2 == lane // block) & (row < 3 * width), from_start, 0.0)
    start_high, start_low = split(from_start)
    table_ref[6] = jnp.where(row < 2 * width, start_high.astype(F32), start_low.astype(F32)).astype(BF16)
    step_ref[...] = jnp.broadcast_to(jnp.exp(-rate_lanes * block), step_ref.shape)


def featurized(tap_ref, which, tile, padded):
    taps = tap_ref.shape[1]
    rows = padded.shape[0] - HALO
    lanes = slice(tile * LANES, (tile + 1) * LANES)
    total = None
    for k in range(taps):
        term = tap_ref[which, k : k + 1, lanes].astype(F32) * padded[HALO - k : HALO - k + rows, :]
        total = term if total is None else total + term
    return total


def product_kernel(halo_ref, inner_ref, value_ref, tap_ref, out_ref, padded):
    rows, channels = inner_ref.shape
    for tile in range(channels // LANES):
        lanes = slice(tile * LANES, (tile + 1) * LANES)
        for n, ref in enumerate((inner_ref, value_ref)):
            padded[n, tile, :HALO] = halo_ref[HALO * (n + 1) : HALO * (n + 2), lanes].astype(F32)
            padded[n, tile, HALO:] = ref[:, lanes].astype(F32)
    for tile in range(channels // LANES):
        inner = featurized(tap_ref, 1, tile, padded.at[0, tile])
        value = featurized(tap_ref, 2, tile, padded.at[1, tile])
        product = (inner * value).astype(BF16).astype(F32)
        both = jnp.concatenate([product, pltpu.roll(product, LANES - 8, 1)], 0).T
        slabs = both.reshape(LANES // 16, 16, LANES)[:, :8].reshape(LANES // 2, LANES)
        out_ref[tile * (LANES // 2) : (tile + 1) * (LANES // 2)] = slabs.astype(BF16)


def conv_kernel(x_ref, table_ref, step_ref, out_ref, state):
    def dot(a, b):
        return jnp.dot(a, b, preferred_element_type=F32)

    rows = x_ref.shape[0]
    x = x_ref[...]
    local = dot(x, table_ref[4]) + dot(x, table_ref[5])
    step = step_ref[...]
    carry = jnp.zeros((8, LANES), F32)
    for block in range(rows // 8):
        state[8 * block : 8 * block + 8] = carry
        carry = carry * step + local[8 * block : 8 * block + 8]
    carried = state[...]
    high, low = split(carried)
    lane = iota(carried.shape, 1)
    width = 32
    second = (lane >= width) & (lane < 2 * width)
    mixed_state = jnp.where(second, low.astype(F32), high.astype(F32)).astype(BF16)
    wide = x.astype(F32)
    zeros = jnp.zeros((8, LANES), F32)
    before = jnp.concatenate([zeros, wide[:-8]], 0).astype(BF16)
    earlier = jnp.concatenate([zeros, zeros, wide[:-16]], 0).astype(BF16)
    mixed = dot(x, table_ref[0]) + dot(x, table_ref[1])
    mixed = mixed + dot(before, table_ref[2]) + dot(earlier, table_ref[3])
    out_ref[...] = (mixed + dot(mixed_state, table_ref[6])).astype(BF16)


def hidden_kernel(mixed_ref, halo_ref, outer_ref, tap_ref, residual_ref, hidden_ref, sum_ref, padded):
    rows, channels = outer_ref.shape
    for tile in range(channels // LANES):
        lanes = slice(tile * LANES, (tile + 1) * LANES)
        padded[tile, :HALO] = halo_ref[:HALO, lanes].astype(F32)
        padded[tile, HALO:] = outer_ref[:, lanes].astype(F32)
    squares = jnp.zeros((rows, LANES), F32)
    for tile in range(channels // LANES):
        lanes = slice(tile * LANES, (tile + 1) * LANES)
        slabs = mixed_ref[tile * (LANES // 2) : (tile + 1) * (LANES // 2)].astype(F32)
        other = pltpu.roll(slabs, LANES // 2, 1)
        groups = LANES // 16
        both = jnp.concatenate([slabs.reshape(groups, 8, LANES), other.reshape(groups, 8, LANES)], 1)
        mixed = both.reshape(LANES, LANES).T[:rows]
        outer = featurized(tap_ref, 0, tile, padded.at[tile])
        hidden = residual_ref[:, lanes].astype(F32) + outer * mixed
        hidden_ref[:, lanes] = hidden
        squares = squares + hidden * hidden
    tall = jnp.concatenate([squares, jnp.zeros_like(squares)], 0).T
    line = jnp.sum(tall, 0, keepdims=True)
    sum_ref[...] = jnp.broadcast_to(line, sum_ref.shape)


def norm_kernel(hidden_ref, sum_ref, gain_ref, out_ref):
    rows, channels = hidden_ref.shape
    parts = sum_ref[...].reshape(sum_ref.shape[0] // 8, 8, LANES)
    line = jnp.sum(parts, 0)
    scale = 1.0 / jnp.sqrt(line / D + 1e-05)
    tall = jnp.broadcast_to(scale[:1], (LANES, LANES)).T[:rows]
    for tile in range(channels // LANES):
        lanes = slice(tile * LANES, (tile + 1) * LANES)
        out_ref[:, lanes] = (hidden_ref[:, lanes] * gain_ref[:, lanes].astype(F32) * tall).astype(BF16)


def on_device(
    outer_input,
    inner_input,
    value_input,
    feature_taps,
    medium_taps,
    decay_rates,
    residues,
    residual,
    norm_gain,
):
    rows, channels = outer_input.shape
    groups, modes = decay_rates.shape
    size = lax.axis_size("ctx")
    parts = lax.axis_size("tp")
    tiles = channels // LANES
    call = pl.pallas_call
    vmem = pl.BlockSpec(memory_space=pltpu.VMEM)
    sent = jnp.concatenate([a[rows - HALO :] for a in (outer_input, inner_input, value_input)], 0)
    halo = lax.ppermute(sent, "ctx", [(i, i + 1) for i in range(size - 1)])
    place = lax.axis_index("ctx").reshape(1).astype(jnp.int32)
    table, step = call(
        tables_kernel,
        in_specs=[pl.BlockSpec(memory_space=pltpu.SMEM), vmem, vmem, vmem],
        out_specs=[vmem, vmem],
        out_shape=[
            jax.ShapeDtypeStruct((7, LANES, LANES), BF16),
            jax.ShapeDtypeStruct((8, LANES), F32),
        ],
        name="tables",
    )(place, decay_rates, residues, medium_taps)
    slab_rows = rows * channels // LANES
    slabs = call(
        product_kernel,
        out_shape=jax.ShapeDtypeStruct((slab_rows, LANES), BF16),
        scratch_shapes=[pltpu.VMEM((2, tiles, HALO + rows, LANES), F32)],
        name="product",
    )(halo, inner_input, value_input, feature_taps)
    slab = (size, slab_rows // size, LANES)
    arrived = lax.all_to_all(slabs.reshape(slab), "ctx", 0, 0)
    mixed = call(
        conv_kernel,
        out_shape=jax.ShapeDtypeStruct((slab_rows, LANES), BF16),
        scratch_shapes=[pltpu.VMEM((slab_rows, LANES), F32)],
        name="conv",
    )(arrived.reshape(slab_rows, LANES), table, step)
    returned = lax.all_to_all(mixed.reshape(slab), "ctx", 0, 0)
    hidden, sums = call(
        hidden_kernel,
        out_shape=[
            jax.ShapeDtypeStruct((rows, channels), F32),
            jax.ShapeDtypeStruct((8 * parts, LANES), F32),
        ],
        scratch_shapes=[pltpu.VMEM((tiles, HALO + rows, LANES), F32)],
        name="hidden",
    )(returned.reshape(slab_rows, LANES), halo, outer_input, feature_taps, residual)
    all_sums = lax.all_to_all(sums.reshape(parts, 8, LANES), "tp", 0, 0)
    return call(
        norm_kernel,
        out_shape=jax.ShapeDtypeStruct((rows, channels), BF16),
        name="norm",
    )(hidden, all_sums.reshape(8 * parts, LANES), norm_gain.reshape(1, channels))


def solution(mesh):
    return jax.shard_map(
        on_device,
        mesh=mesh,
        in_specs=(
            P("ctx", "tp"),
            P("ctx", "tp"),
            P("ctx", "tp"),
            P(None, None, "tp"),
            P(None, "tp"),
            P("tp", None),
            P("tp", None),
            P("ctx", "tp"),
            P("tp"),
        ),
        out_specs=P("ctx", "tp"),
        check_vma=False,
    )
```

time: 439 us -> 85.9 us (0.20)
  the two profiles are of different devices: /device:TPU:486 before, /device:TPU:1 now
where the time goes in v1:
time: 85.9 us; the launch traced here: 85.2 us
  starting transfers between devices  32.9 us (38%)
  blocking collectives  20.5 us (24%)
  waiting for transfers between devices  16.3 us (19%)
  Pallas kernels  10.1 us (12%)
  local copies, waits for them, and re-layouts  5.33 us (6%)
    all_to_all x1, blocking collectives, on_device(): returned = lax.all_to_all(mixed.reshape(slab), 'ctx', 0, 0)  20.5 us
    all_to_all x1, starting transfers between devices, on_device(): arrived = lax.all_to_all(slabs.reshape(slab), 'ctx', 0, 0)  19.8 us
    all_to_all x1, waiting for transfers between devices, on_device(): arrived = lax.all_to_all(slabs.reshape(slab), 'ctx', 0, 0)  11.1 us
    all_to_all x1, starting transfers between devices, on_device(): all_sums = lax.all_to_all(sums.reshape(parts, 8, LANES), 'tp', 0, 0)  9.19 us
    all_to_all x1, waiting for transfers between devices, on_device(): all_sums = lax.all_to_all(sums.reshape(parts, 8, LANES), 'tp', 0, 0)  4.13 us
    unnamed x17, local copies, waits for them, and re-layouts  4 us
    ppermute x1, starting transfers between devices, on_device(): halo = lax.ppermute(sent, 'ctx', [(i, i + 1) for i in range(size - 1)])  3.92 us
    pallas_call x1, Pallas kernels, on_device(): call(product_kernel, out_shape=jax.ShapeDtypeStruct((slab_rows, LANES), B...  2.29 us
  transfers between devices with their start and end apart: 3, of which 3 were waited for; matrix products, arithmetic and copies ran while one was open for 3% of the time, Pallas kernels for 2%

profile of v1, /device:TPU:1, one launch (start us, length us, event | category | flops | bytes accessed | tf_op | source)
XLA Modules:
  0.0 85.2 jit_solution(16072827469060970574)
XLA Ops:
  0.0 0.7 slice-done.2
  0.7 0.0 slice-done
  0.7 0.0 slice-done.1
  0.8 3.9 %collective-permute-start = (bf16[24,1024]{1,0:T(8,128)(2,1)S(1)}, bf16[24,1024]{1,0:T(8,128)(2,1)S(1)}, u32[]{:S(2)}, u32[]{:S(2)}) collective-permute-start(bf16[24,1024]{1,0:T(8,128)(2,1)S(1)} %pad_maximum_fusion), channel_id=1, source_target_pairs={{0,8},{8,16},{16,24},{24,32},{32,40},{40,48},{48,56},{56,64},{64,7... | collective-permute-start | bytes 147464 | tf_op jit(solution)/shard_map/ppermute | solution.py:190
  4.7 1.2 %collective-permute-done.halo_ref = bf16[24,1024]{1,0:T(8,128)(2,1)S(1)} collective-permute-done((bf16[24,1024]{1,0:T(8,128)(2,1)S(1)}, bf16[24,1024]{1,0:T(8,128)(2,1)S(1)}, u32[]{:S(2)}, u32[]{:S(2)}) %collective-permute-start) | collective-permute-done | bytes 49184 | tf_op jit(solution)/shard_map/ppermute | solution.py:190
  5.8 0.6 copy-done.1
  6.5 2.3 %product.1 = bf16[512,128]{1,0:T(8,128)(2,1)} custom-call(bf16[24,1024]{1,0:T(8,128)(2,1)} %copy-done.1, bf16[64,1024]{1,0:T(8,128)(2,1)} %inner_ref.1, bf16[64,1024]{1,0:T(8,128)(2,1)} %value_ref.1, bf16[3,7,1024]{2,1,0:T(8,128)(2,1)} %tap_ref.3), custom_call_target="tpu_custom_call" | custom-call | tf_op jit(solution)/shard_map/product/pallas_call | solution.py:203
  8.8 19.8 %all-to-all-start = ((bf16[64,8,128]{2,1,0:T(8,128)(2,1)}), bf16[64,8,128]{2,1,0:T(8,128)(2,1)S(1)}, u32[]{:S(2)}, u32[]{:S(2)}) async-start(bf16[64,8,128]{2,1,0:T(8,128)(2,1)} %bitcast.8), calls=%async_computation | async-start | bytes 262144 | tf_op jit(solution)/shard_map/all_to_all | solution.py:210
  28.6 0.0 copy-start.5
  28.6 0.7 copy.10.decay_ref
  29.3 0.7 copy.11.residue_ref
  30.0 0.0 copy-done.3
  30.0 0.7 copy.12.medium_ref
  30.7 1.8 %tables.1 = (bf16[7,128,128]{2,1,0:T(8,128)(2,1)}, f32[8,128]{1,0:T(8,128)}) custom-call(s32[1]{0:T(128)} %bitcast.2.place, f32[64,16]{1,0:T(8,128)} %copy.10.decay_ref, f32[64,16]{1,0:T(8,128)} %copy.11.residue_ref, bf16[128,64]{1,0:T(8,128)(2,1)} %copy.12.medium_ref), custom_call_target="tpu_custom_call" | custom-call | tf_op jit(solution)/shard_map/tables/pallas_call | solution.py:192
  32.5 11.1 %all-to-all-done = bf16[64,8,128]{2,1,0:T(8,128)(2,1)S(1)} async-done(((bf16[64,8,128]{2,1,0:T(8,128)(2,1)}), bf16[64,8,128]{2,1,0:T(8,128)(2,1)S(1)}, u32[]{:S(2)}, u32[]{:S(2)}) %all-to-all-start) | async-done | bytes 131104 | tf_op jit(solution)/shard_map/all_to_all | solution.py:210
  43.6 0.7 copy-done
  44.2 2.1 %conv.1 = bf16[512,128]{1,0:T(8,128)(2,1)} custom-call(bf16[512,128]{1,0:T(8,128)(2,1)} %bitcast.7, bf16[7,128,128]{2,1,0:T(8,128)(2,1)} %get-tuple-element.9.table_ref, f32[8,128]{1,0:T(8,128)} %get-tuple-element.10.step_ref), custom_call_target="tpu_custom_call" | custom-call | tf_op jit(solution)/shard_map/conv/pallas_call | solution.py:211
  46.4 20.5 %all_to_all.15 = bf16[64,8,128]{2,1,0:T(8,128)(2,1)} all-to-all(bf16[64,8,128]{2,1,0:T(8,128)(2,1)} %bitcast.10), channel_id=1, replica_groups=mesh['ctx'=64,'tp'=8] {'ctx'}, dimensions={0} | all-to-all | bytes 262144 | tf_op jit(solution)/shard_map/all_to_all | solution.py:217
  66.9 2.1 %hidden.1 = (f32[64,1024]{1,0:T(8,128)}, f32[64,128]{1,0:T(8,128)}) custom-call(bf16[512,128]{1,0:T(8,128)(2,1)} %bitcast.9, bf16[24,1024]{1,0:T(8,128)(2,1)} %copy-done.1, bf16[64,1024]{1,0:T(8,128)(2,1)} %outer_ref.1, bf16[3,7,1024]{2,1,0:T(8,128)(2,1)} %tap_ref.3, bf16[64,1024]{1,0:T(8,128)(2,1)} %residual_ref.1), custom_call_target="tpu_custom_call" | custom-call | tf_op jit(solution)/shard_map/hidden/pallas_call | solution.py:218
  69.0 9.2 %all-to-all-start.2 = ((f32[8,8,128]{2,1,0:T(8,128)}), f32[8,8,128]{2,1,0:T(8,128)S(1)}, u32[]{:S(2)}, u32[]{:S(2)}) async-start(f32[8,8,128]{2,1,0:T(8,128)} %bitcast.12), calls=%async_computation.2 | async-start | bytes 65536 | tf_op jit(solution)/shard_map/all_to_all | solution.py:227
  78.2 0.6 reshape.31.gain_ref
  78.8 4.1 %all-to-all-done.2 = f32[8,8,128]{2,1,0:T(8,128)S(1)} async-done(((f32[8,8,128]{2,1,0:T(8,128)}), f32[8,8,128]{2,1,0:T(8,128)S(1)}, u32[]{:S(2)}, u32[]{:S(2)}) %all-to-all-start.2) | async-done | bytes 32800 | tf_op jit(solution)/shard_map/all_to_all | solution.py:227
  82.9 0.6 copy-done.2
  83.5 1.7 %norm.1 = bf16[64,1024]{1,0:T(8,128)(2,1)} custom-call(f32[64,1024]{1,0:T(8,128)} %get-tuple-element.11.hidden_ref, f32[64,128]{1,0:T(8,128)} %bitcast.11, bf16[1,1024]{1,0:T(2,128)(2,1)} %reshape.31.gain_ref), custom_call_target="tpu_custom_call" | custom-call | tf_op jit(solution)/shard_map/norm/pallas_call | solution.py:228
  (13 shorter events, 0.0 us)
Async XLA Ops:
  0.0 0.7 slice-start.2
  0.0 0.7 slice-start
  0.0 0.7 slice-start.1
  0.8 5.1 %collective-permute-start = (bf16[24,1024]{1,0:T(8,128)(2,1)S(1)}, bf16[24,1024]{1,0:T(8,128)(2,1)S(1)}, u32[]{:S(2)}, u32[]{:S(2)}) collective-permute-start(bf16[24,1024]{1,0:T(8,128)(2,1)S(1)} %pad_maximum_fusion), channel_id=1, source_target_pairs={{0,8},{8,16},{16,24},{24,32},{32,40},{40,48},{48,56},{56,64},{64,7... | collective-permute-start | bytes 147464 | tf_op jit(solution)/shard_map/ppermute | solution.py:190
  5.8 0.6 copy-start.1
  8.7 19.8 %copy-start.4 = (f32[64,16]{0,1:T(8,128)S(1)}, f32[64,16]{0,1:T(8,128)}, u32[]{:S(2)}) copy-start(f32[64,16]{0,1:T(8,128)} %param.14) | copy-start | bytes 12292
  8.8 34.8 %all-to-all-start = ((bf16[64,8,128]{2,1,0:T(8,128)(2,1)}), bf16[64,8,128]{2,1,0:T(8,128)(2,1)S(1)}, u32[]{:S(2)}, u32[]{:S(2)}) async-start(bf16[64,8,128]{2,1,0:T(8,128)(2,1)} %bitcast.8), calls=%async_computation | async-start | bytes 262144 | tf_op jit(solution)/shard_map/all_to_all | solution.py:210
  28.6 0.7 copy-start.5
  29.3 0.7 copy-start.3
  43.6 0.7 copy-start
  69.0 9.2 %copy-start.6 = (bf16[1024]{0:T(1024)(128)(2,1)S(1)}, bf16[1024]{0:T(1024)(128)(2,1)}, u32[]{:S(2)}) copy-start(bf16[1024]{0:T(1024)(128)(2,1)} %param.17) | copy-start | bytes 6148
  69.0 13.9 %all-to-all-start.2 = ((f32[8,8,128]{2,1,0:T(8,128)}), f32[8,8,128]{2,1,0:T(8,128)S(1)}, u32[]{:S(2)}, u32[]{:S(2)}) async-start(f32[8,8,128]{2,1,0:T(8,128)} %bitcast.12), calls=%async_computation.2 | async-start | bytes 65536 | tf_op jit(solution)/shard_map/all_to_all | solution.py:227
  82.9 0.6 copy-start.2

commit v2 on v1

v2 whole, which is shorter than its diff:
```python
import functools

import jax
import jax.numpy as jnp
from jax import lax
from jax.experimental import pallas as pl
from jax.experimental.pallas import tpu as pltpu
from jax.sharding import PartitionSpec as P

D = 8192
F32 = jnp.float32
BF16 = jnp.bfloat16
LANES = 128
HALO = 8
NEAR = 16


def iota(shape, axis):
    return lax.broadcasted_iota(jnp.int32, shape, axis)


def in_vmem(*arrays):
    return [pltpu.with_memory_space_constraint(a, pltpu.VMEM) for a in arrays]


def split(x):
    high = x.astype(BF16)
    return high, (x - high.astype(F32)).astype(BF16)


def split_three(x, width):
    high, rest = split(x)
    middle, _ = split(x - high.astype(F32))
    low = x - high.astype(F32) - middle.astype(F32)
    copy = iota(x.shape, 1) // width
    part = jnp.where(copy == 0, high.astype(F32), jnp.where(copy == 1, middle.astype(F32), low))
    return jnp.where(copy < 3, part, 0.0).astype(BF16)


def join_three(parts, width):
    x = parts.astype(F32)
    x = x + pltpu.roll(x, width, 1)
    return x + pltpu.roll(x, 2 * width, 1)


def two_parts(x, width):
    high, low = split(x)
    copy = iota(x.shape, 1) // width
    return jnp.where(copy == 1, low.astype(F32), high.astype(F32)).astype(BF16)


def tables_kernel(place, decay_ref, residue_ref, medium_ref, table_ref, step_ref, jump_ref):
    modes, groups = decay_ref.shape
    square = (LANES, LANES)
    block = LANES // 2
    row, lane = iota(square, 0), iota(square, 1)
    same = row // block == lane // block
    pick = iota((modes, LANES), 0) == iota((modes, LANES), 1) % modes
    lag = iota((modes, LANES), 1).astype(F32)
    zero_row = jnp.zeros((1, LANES), F32)
    width = 2 * modes
    count = table_ref.shape[0]

    def along_lanes(x):
        return jnp.sum(jnp.where(pick, x, 0.0), 0, keepdims=True)

    def along_rows(x):
        return jnp.sum(jnp.where(row == lane, along_lanes(x), 0.0), 1, keepdims=True)

    def toeplitz(filter_row):
        wide = jnp.concatenate([filter_row, zero_row], 1)
        wide = jnp.broadcast_to(wide, (LANES, 2 * LANES))
        return pltpu.roll(wide, 0, 1, stride=1, stride_axis=0)

    for q in range(count):
        group = place[0] * count + q
        mine = iota((modes, groups), 1) == group
        rate = jnp.sum(jnp.where(mine, decay_ref[...], 0.0), 1, keepdims=True)
        weight = jnp.sum(jnp.where(mine, residue_ref[...], 0.0), 1, keepdims=True)
        weight = weight * jnp.sqrt(2.0 * rate / modes)
        long_row = jnp.sum(weight * jnp.exp(-rate * lag), 0, keepdims=True)
        chosen = iota(medium_ref.shape, 0) == group
        medium_row = jnp.sum(jnp.where(chosen, medium_ref[...].astype(F32), 0.0), 0, keepdims=True)
        medium_wide = toeplitz(medium_row)
        near = jnp.where(same, medium_wide[:, :LANES] + toeplitz(long_row)[:, :LANES], 0.0)
        table_ref[q, 0], table_ref[q, 1] = split(near)
        middle = [medium_wide[:, block:LANES], medium_wide[:, LANES : LANES + block]]
        table_ref[q, 2] = jnp.where(same, jnp.concatenate(middle, 1), 0.0).astype(BF16)
        table_ref[q, 3] = jnp.where(same, medium_wide[:, LANES:], 0.0).astype(BF16)
        rate_lanes, rate_rows, weight_rows = along_lanes(rate), along_rows(rate), along_rows(weight)
        to_end = jnp.exp(-rate_lanes * (block - 1 - row % block).astype(F32))
        kept = ((lane // modes) % 2 == row // block) & (lane < 3 * width)
        table_ref[q, 4], table_ref[q, 5] = split(jnp.where(kept, to_end, 0.0))
        from_start = weight_rows * jnp.exp(-rate_rows * (lane % block + 1).astype(F32))
        kept = ((row // modes) % 2 == lane // block) & (row < 3 * width)
        high, low = split(jnp.where(kept, from_start, 0.0))
        both = jnp.where(row < 2 * width, high.astype(F32), low.astype(F32))
        table_ref[q, 6] = both.astype(BF16)
        rows = slice(8 * q, 8 * q + 8)
        step_ref[rows] = jnp.broadcast_to(jnp.exp(-rate_lanes * block), (8, LANES))
        jump_ref[rows] = jnp.broadcast_to(jnp.exp(-rate_lanes * (block * NEAR)), (8, LANES))


def featurized(tap_ref, which, lanes, padded, rows):
    total = None
    for k in range(tap_ref.shape[1]):
        term = tap_ref[which, k : k + 1, lanes].astype(F32) * padded[HALO - k : HALO - k + rows, :]
        total = term if total is None else total + term
    return total


def tile_lanes(tile):
    return slice(tile * LANES, (tile + 1) * LANES)


def body_kernel(inner_ref, value_ref, tap_ref, out_ref, head_ref, padded):
    rows, channels = inner_ref.shape
    for tile in range(channels // LANES):
        lanes = tile_lanes(tile)
        feats = []
        for n, ref in enumerate((inner_ref, value_ref)):
            wide = ref[:, lanes].astype(F32)
            padded[n, tile] = wide
            head_ref[n, :, lanes] = wide[:HALO]
            feats.append(featurized(tap_ref, n + 1, lanes, padded.at[n, tile], rows - HALO))
        out_ref[:, lanes] = feats[0] * feats[1]


def product_kernel(halo_ref, head_ref, body_ref, tap_ref, out_ref, padded):
    channels = body_ref.shape[1]
    for tile in range(channels // LANES):
        lanes = tile_lanes(tile)
        feats = []
        for n in range(2):
            padded[n, tile, :HALO] = halo_ref[HALO * (n + 1) : HALO * (n + 2), lanes].astype(F32)
            padded[n, tile, HALO:] = head_ref[n, :, lanes]
            feats.append(featurized(tap_ref, n + 1, lanes, padded.at[n, tile], HALO))
        product = jnp.concatenate([feats[0] * feats[1], body_ref[:, lanes]], 0)
        product = product.astype(BF16).astype(F32)
        both = jnp.concatenate([product, pltpu.roll(product, LANES - 8, 1)], 0).T
        slabs = both.reshape(LANES // 16, 16, LANES)[:, :8].reshape(LANES // 2, LANES)
        out_ref[tile * (LANES // 2) : (tile + 1) * (LANES // 2)] = slabs.astype(BF16)


def outer_kernel(halo_ref, outer_ref, tap_ref, out_ref, padded):
    rows, channels = outer_ref.shape
    for tile in range(channels // LANES):
        lanes = tile_lanes(tile)
        padded[tile, :HALO] = halo_ref[:HALO, lanes].astype(F32)
        padded[tile, HALO:] = outer_ref[:, lanes].astype(F32)
        out_ref[:, lanes] = featurized(tap_ref, 0, lanes, padded.at[tile], rows)


def dot(a, b):
    return jnp.dot(a, b, preferred_element_type=F32)


def of_group(x, q, count):
    return x.reshape(x.shape[0] // (8 * count), count, 8, LANES)[:, q].reshape(-1, LANES)


def states_kernel(width, x_ref, table_ref, step_ref, state_ref, end_ref, send_ref):
    count = table_ref.shape[0]
    blocks = x_ref.shape[0] // (8 * count)
    wide = x_ref[...].astype(F32)
    ends = []
    for q in range(count):
        x = of_group(wide, q, count).astype(BF16)
        local = dot(x, table_ref[q, 4]) + dot(x, table_ref[q, 5])
        step = step_ref[8 * q : 8 * q + 8]
        carry = jnp.zeros((8, LANES), F32)
        for block in range(blocks):
            at = 8 * (count * block + q)
            state_ref[at : at + 8] = carry
            carry = carry * step + local[8 * block : 8 * block + 8]
        ends.append(carry)
    end = jnp.concatenate(ends, 0)
    end_ref[...] = end
    rows = 8 * count
    send_ref[:rows] = split_three(end, width)
    send_ref[rows:] = x_ref[(blocks - 2) * rows :]


def chain_kernel(width, got_ref, end_ref, jump_ref, send_ref, next_ref):
    rows = end_ref.shape[0]
    end = end_ref[...] + jump_ref[...] * join_three(got_ref[:rows], width)
    next_ref[:rows] = split_three(end, width)
    next_ref[rows:] = send_ref[rows:]


def local_kernel(width, x_ref, table_ref, state_ref, out_ref):
    count = table_ref.shape[0]
    wide = x_ref[...].astype(F32)
    states = state_ref[...]
    zeros = jnp.zeros((8, LANES), F32)
    for q in range(count):
        x = of_group(wide, q, count)
        before = jnp.concatenate([zeros, x[:-8]], 0).astype(BF16)
        earlier = jnp.concatenate([zeros, zeros, x[:-16]], 0).astype(BF16)
        x = x.astype(BF16)
        mixed = dot(x, table_ref[q, 0]) + dot(x, table_ref[q, 1])
        mixed = mixed + dot(before, table_ref[q, 2]) + dot(earlier, table_ref[q, 3])
        mixed = mixed + dot(two_parts(of_group(states, q, count), width), table_ref[q, 6])
        for block in range(x.shape[0] // 8):
            at = 8 * (count * block + q)
            out_ref[at : at + 8] = mixed[8 * block : 8 * block + 8]


def finish_kernel(width, local_ref, first_ref, second_ref, third_ref, table_ref, step_ref, out_ref):
    count = table_ref.shape[0]
    rows = 8 * count
    blocks = local_ref.shape[0] // rows
    got = first_ref[...].astype(F32) + second_ref[...].astype(F32) + third_ref[...].astype(F32)
    incoming = join_three(got[:rows], width)
    zeros = jnp.zeros((8, LANES), F32)
    parts = []
    for q in range(count):
        at = slice(8 * q, 8 * q + 8)
        step = step_ref[at]
        state = incoming[at]
        states = []
        for block in range(blocks):
            states.append(state)
            state = state * step
        mixed = dot(two_parts(jnp.concatenate(states, 0), width), table_ref[q, 6])
        last_but_one, last = got[rows:][at], got[2 * rows :][at]
        before = jnp.concatenate([last, zeros], 0).astype(BF16)
        earlier = jnp.concatenate([last_but_one, last], 0).astype(BF16)
        start = dot(before, table_ref[q, 2]) + dot(earlier, table_ref[q, 3])
        mixed = jnp.concatenate([mixed[:16] + start, mixed[16:]], 0)
        parts.append(mixed.reshape(blocks, 8, LANES))
    total = local_ref[...] + jnp.concatenate(parts, 1).reshape(local_ref.shape)
    out_ref[...] = total.astype(BF16)


def hidden_kernel(mixed_ref, outer_ref, residual_ref, hidden_ref, sum_ref):
    rows, channels = outer_ref.shape
    squares = jnp.zeros((rows, LANES), F32)
    for tile in range(channels // LANES):
        lanes = tile_lanes(tile)
        slabs = mixed_ref[tile * (LANES // 2) : (tile + 1) * (LANES // 2)].astype(F32)
        other = pltpu.roll(slabs, LANES // 2, 1)
        groups = LANES // 16
        both = jnp.concatenate([slabs.reshape(groups, 8, LANES), other.reshape(groups, 8, LANES)], 1)
        mixed = both.reshape(LANES, LANES).T[:rows]
        hidden = residual_ref[:, lanes].astype(F32) + outer_ref[:, lanes] * mixed
        hidden_ref[:, lanes] = hidden
        squares = squares + hidden * hidden
    tall = jnp.concatenate([squares, jnp.zeros_like(squares)], 0).T
    line = jnp.sum(tall, 0, keepdims=True)
    sum_ref[...] = jnp.broadcast_to(line, sum_ref.shape)


def norm_kernel(hidden_ref, sum_ref, gain_ref, out_ref):
    rows, channels = hidden_ref.shape
    parts = sum_ref[...].reshape(sum_ref.shape[0] // 8, 8, LANES)
    line = jnp.sum(parts, 0)
    scale = 1.0 / jnp.sqrt(line / D + 1e-05)
    tall = jnp.broadcast_to(scale[:1], (LANES, LANES)).T[:rows]
    for tile in range(channels // LANES):
        lanes = slice(tile * LANES, (tile + 1) * LANES)
        out_ref[:, lanes] = (hidden_ref[:, lanes] * gain_ref[:, lanes].astype(F32) * tall).astype(BF16)


def on_device(
    outer_input,
    inner_input,
    value_input,
    feature_taps,
    medium_taps,
    decay_rates,
    residues,
    residual,
    norm_gain,
):
    rows, channels = outer_input.shape
    groups, modes = decay_rates.shape
    size = lax.axis_size("ctx")
    parts = lax.axis_size("tp")
    tiles = channels // LANES
    vmem = pl.BlockSpec(memory_space=pltpu.VMEM)
    smem = pl.BlockSpec(memory_space=pltpu.SMEM)

    def call(kernel, name, out, *arrays, scalars=(), scratch=()):
        return pl.pallas_call(
            kernel,
            in_specs=[smem] * len(scalars) + [vmem] * len(arrays),
            out_specs=jax.tree.map(lambda _: vmem, out),
            out_shape=out,
            scratch_shapes=scratch,
            name=name,
        )(*scalars, *in_vmem(*arrays))

    slab_rows = rows * channels // LANES
    count = groups // NEAR
    width = 2 * modes
    far = size // NEAR
    pack = 8 * count
    with_width = lambda kernel: functools.partial(kernel, width)

    sent = jnp.concatenate([a[rows - HALO :] for a in (outer_input, inner_input, value_input)], 0)
    halo = lax.ppermute(sent, "ctx", [(i, i + 1) for i in range(size - 1)])
    body, head = call(
        body_kernel,
        "body",
        [pltpu.VMEM((rows - HALO, channels), F32), pltpu.VMEM((2, HALO, channels), F32)],
        inner_input,
        value_input,
        feature_taps,
        scratch=[pltpu.VMEM((2, tiles, rows, LANES), F32)],
    )
    slabs = call(
        product_kernel,
        "product",
        pltpu.VMEM((slab_rows, LANES), BF16),
        halo,
        head,
        body,
        feature_taps,
        scratch=[pltpu.VMEM((2, tiles, 2 * HALO, LANES), F32)],
    )
    neighbours = [[NEAR * f + n for n in range(NEAR)] for f in range(far)]

    def exchange(x):
        slab = (NEAR, slab_rows // NEAR, LANES)
        y = lax.all_to_all(x.reshape(slab), "ctx", 0, 0, axis_index_groups=neighbours)
        return y.reshape(slab_rows, LANES)

    place = (lax.axis_index("ctx") % NEAR).reshape(1).astype(jnp.int32)
    table, step, jump = call(
        tables_kernel,
        "tables",
        [
            pltpu.VMEM((count, 7, LANES, LANES), BF16),
            pltpu.VMEM((pack, LANES), F32),
            pltpu.VMEM((pack, LANES), F32),
        ],
        decay_rates.T,
        residues.T,
        medium_taps.T,
        scalars=(place,),
    )
    outer_feat = call(
        outer_kernel,
        "outer",
        pltpu.VMEM((rows, channels), F32),
        halo,
        outer_input,
        feature_taps,
        scratch=[pltpu.VMEM((tiles, HALO + rows, LANES), F32)],
    )
    arrived = exchange(slabs)
    packet = pltpu.VMEM((3 * pack, LANES), BF16)
    states, end, packed = call(
        with_width(states_kernel),
        "states",
        [pltpu.VMEM((slab_rows, LANES), F32), pltpu.VMEM((pack, LANES), F32), packet],
        arrived,
        table,
        step,
    )
    local = call(
        with_width(local_kernel),
        "local",
        pltpu.VMEM((slab_rows, LANES), F32),
        arrived,
        table,
        states,
    )
    got = []
    for f in range(far - 1):
        if got:
            packed = call(with_width(chain_kernel), "chain", packet, got[-1], end, jump, packed)
        pairs = [(NEAR * f + n, NEAR * (f + 1) + n) for n in range(NEAR)]
        got.append(lax.ppermute(packed, "ctx", pairs))
    mixed = call(
        with_width(finish_kernel),
        "finish",
        pltpu.VMEM((slab_rows, LANES), BF16),
        local,
        *got,
        table,
        step,
    )
    hidden, sums = call(
        hidden_kernel,
        "hidden",
        [pltpu.VMEM((rows, channels), F32), pltpu.VMEM((8 * parts, LANES), F32)],
        exchange(mixed),
        outer_feat,
        residual,
    )
    all_sums = lax.all_to_all(sums.reshape(parts, 8, LANES), "tp", 0, 0)
    return call(
        norm_kernel,
        "norm",
        jax.ShapeDtypeStruct((rows, channels), BF16),
        hidden,
        all_sums.reshape(8 * parts, LANES),
        norm_gain.reshape(1, channels),
    )


def solution(mesh):
    return jax.shard_map(
        on_device,
        mesh=mesh,
        in_specs=(
            P("ctx", "tp"),
            P("ctx", "tp"),
            P("ctx", "tp"),
            P(None, None, "tp"),
            P(None, "tp"),
            P("tp", None),
            P("tp", None),
            P("ctx", "tp"),
            P("tp"),
        ),
        out_specs=P("ctx", "tp"),
        check_vma=False,
    )
```

time: 85.9 us -> 71 us (0.83)
  the two profiles are of different devices: /device:TPU:1 before, /device:TPU:384 now
where the time goes in v2:
time: 71 us; the launch traced here: 70.2 us
  waiting for transfers between devices  42.8 us (60%)
  starting transfers between devices  17.9 us (25%)
  Pallas kernels  5.99 us (8%)
  local copies, waits for them, and re-layouts  3.27 us (5%)
    ppermute x3, waiting for transfers between devices, on_device(): got.append(lax.ppermute(packed, 'ctx', pairs))  17.6 us
    all_to_all x2, waiting for transfers between devices, exchange(): lax.all_to_all(x.reshape(slab), 'ctx', 0, 0, axis_index_groups=neighbours)  16 us
    all_to_all x2, starting transfers between devices, exchange(): lax.all_to_all(x.reshape(slab), 'ctx', 0, 0, axis_index_groups=neighbours)  7.16 us
    pallas_call x11, Pallas kernels, call(): pl.pallas_call(kernel, in_specs=[smem] * len(scalars) + [vmem] * len(arra...  5.99 us
    all_to_all x1, waiting for transfers between devices, on_device(): all_sums = lax.all_to_all(sums.reshape(parts, 8, LANES), 'tp', 0, 0)  5.43 us
    all_to_all x1, starting transfers between devices, on_device(): all_sums = lax.all_to_all(sums.reshape(parts, 8, LANES), 'tp', 0, 0)  4.6 us
    ppermute x1, waiting for transfers between devices, on_device(): halo = lax.ppermute(sent, 'ctx', [(i, i + 1) for i in range(size - 1)])  3.79 us
    ppermute x1, starting transfers between devices, on_device(): halo = lax.ppermute(sent, 'ctx', [(i, i + 1) for i in range(size - 1)])  3.52 us
  transfers between devices with their start and end apart: 7, of which 5 were waited for; matrix products, arithmetic and copies ran while one was open for 0% of the time, Pallas kernels for 2%

profile of v2, /device:TPU:384, one launch (start us, length us, event | category | flops | bytes accessed | tf_op | source)
XLA Modules:
  0.0 70.2 jit_solution(6700323419341882272)
XLA Ops:
  0.0 0.7 %slice-done.2 = bf16[8,1024]{1,0:T(8,128)(2,1)S(1)} async-done(((bf16[64,1024]{1,0:T(8,128)(2,1)}), bf16[8,1024]{1,0:T(8,128)(2,1)S(1)}, s32[]{:S(2)}) %slice-start.2) | async-done | bytes 16408 | tf_op jit(solution)/shard_map/slice | solution.py:301
  0.8 3.5 %collective-permute-start = (bf16[24,1024]{1,0:T(8,128)(2,1)S(1)}, bf16[24,1024]{1,0:T(8,128)(2,1)S(1)}, u32[]{:S(2)}, u32[]{:S(2)}) collective-permute-start(bf16[24,1024]{1,0:T(8,128)(2,1)S(1)} %pad_maximum_fusion), channel_id=1, source_target_pairs={{0,8},{8,16},{16,24},{24,32},{32,40},{40,48},{48,56},{56,64},{64,7... | collective-permute-start | bytes 147464 | tf_op jit(solution)/shard_map/ppermute | solution.py:302
  4.3 0.9 %copy-done.1 = bf16[64,1024]{1,0:T(8,128)(2,1)S(1)} copy-done((bf16[64,1024]{1,0:T(8,128)(2,1)S(1)}, bf16[64,1024]{1,0:T(8,128)(2,1)}, u32[]{:S(2)}) %copy-start.1) | copy-done | bytes 131096
  5.2 0.9 %copy-done.2 = bf16[64,1024]{1,0:T(8,128)(2,1)S(1)} copy-done((bf16[64,1024]{1,0:T(8,128)(2,1)S(1)}, bf16[64,1024]{1,0:T(8,128)(2,1)}, u32[]{:S(2)}) %copy-start.2) | copy-done | bytes 131096
  6.1 0.3 body.1
  6.4 3.8 %collective-permute-done.halo_ref = bf16[24,1024]{1,0:T(8,128)(2,1)S(1)} collective-permute-done((bf16[24,1024]{1,0:T(8,128)(2,1)S(1)}, bf16[24,1024]{1,0:T(8,128)(2,1)S(1)}, u32[]{:S(2)}, u32[]{:S(2)}) %collective-permute-start) | collective-permute-done | bytes 49184 | tf_op jit(solution)/shard_map/ppermute | solution.py:302
  10.2 1.0 %product.1 = bf16[512,128]{1,0:T(8,128)(2,1)} custom-call(bf16[24,1024]{1,0:T(8,128)(2,1)S(1)} %collective-permute-done.halo_ref, f32[2,8,1024]{2,1,0:T(8,128)S(1)} %get-tuple-element.15.head_ref, f32[56,1024]{1,0:T(8,128)S(1)} %get-tuple-element.16.body_ref, bf16[3,7,1024]{2,1,0:T(8,128)(2,1)S(1)} %copy-done), custom_call_target="tpu_custom_call" | custom-call | tf_op jit(solution)/shard_map/product/pallas_call | solution.py:285
  11.2 3.5 %all-to-all-start = ((bf16[16,32,128]{2,1,0:T(8,128)(2,1)}), bf16[16,32,128]{2,1,0:T(8,128)(2,1)S(1)}, u32[]{:S(2)}, u32[]{:S(2)}) async-start(bf16[16,32,128]{2,1,0:T(8,128)(2,1)} %bitcast), calls=%async_computation | async-start | bytes 262144 | tf_op jit(solution)/shard_map/all_to_all | solution.py:326
  14.8 0.7 copy-done.5
  15.5 0.8 %tables.1 = (bf16[4,7,128,128]{3,2,1,0:T(8,128)(2,1)S(1)}, f32[32,128]{1,0:T(8,128)S(1)}, f32[32,128]{1,0:T(8,128)S(1)}) custom-call(s32[1]{0:T(128)} %bitcast.2.place, f32[16,64]{1,0:T(8,128)S(1)} %bitcast.15, f32[16,64]{1,0:T(8,128)S(1)} %bitcast.16, bf16[64,128]{1,0:T(8,128)(2,1)S(1)} %bitcast.14), custom_call_target="tpu_custom_call" | custom-call | tf_op jit(solution)/shard_map/tables/pallas_call | solution.py:285
  16.3 7.3 %all-to-all-done = bf16[16,32,128]{2,1,0:T(8,128)(2,1)S(1)} async-done(((bf16[16,32,128]{2,1,0:T(8,128)(2,1)}), bf16[16,32,128]{2,1,0:T(8,128)(2,1)S(1)}, u32[]{:S(2)}, u32[]{:S(2)}) %all-to-all-start) | async-done | bytes 131104 | tf_op jit(solution)/shard_map/all_to_all | solution.py:326
  23.6 0.2 states.1
  23.9 0.7 collective-permute-start.1
  24.7 0.7 collective-permute-start.2
  25.6 1.3 %collective-permute-start.3 = (bf16[96,128]{1,0:T(8,128)(2,1)S(1)}, bf16[96,128]{1,0:T(8,128)(2,1)S(1)}, u32[]{:S(2)}, u32[]{:S(2)}) collective-permute-start(bf16[96,128]{1,0:T(8,128)(2,1)S(1)} %chain.3), channel_id=1, source_target_pairs={{256,384},{264,392},{272,400},{280,408},{288,416},{296,424},{304,4... | collective-permute-start | bytes 73736 | tf_op jit(solution)/shard_map/ppermute | solution.py:375
  26.9 0.3 local.1.local_ref
  27.2 17.6 %collective-permute-done.3.third_ref = bf16[96,128]{1,0:T(8,128)(2,1)S(1)} collective-permute-done((bf16[96,128]{1,0:T(8,128)(2,1)S(1)}, bf16[96,128]{1,0:T(8,128)(2,1)S(1)}, u32[]{:S(2)}, u32[]{:S(2)}) %collective-permute-start.3) | collective-permute-done | bytes 24608 | tf_op jit(solution)/shard_map/ppermute | solution.py:375
  44.8 1.0 %finish.1 = bf16[512,128]{1,0:T(8,128)(2,1)} custom-call(f32[512,128]{1,0:T(8,128)S(1)} %local.1.local_ref, bf16[96,128]{1,0:T(8,128)(2,1)S(1)} %collective-permute-done.1.got_ref.first_ref, bf16[96,128]{1,0:T(8,128)(2,1)S(1)} %collective-permute-done.2.got_ref.second_ref, bf16[96,128]{1,0:T(8,128)(2,1)S(1)} %collective-permute-done.3.third_ref, ...), custom_call_target="tpu_custom_call" | custom-call | tf_op jit(solution)/shard_map/finish/pallas_call | solution.py:285
  45.8 3.6 %all-to-all-start.1 = ((bf16[16,32,128]{2,1,0:T(8,128)(2,1)}), bf16[16,32,128]{2,1,0:T(8,128)(2,1)S(1)}, u32[]{:S(2)}, u32[]{:S(2)}) async-start(bf16[16,32,128]{2,1,0:T(8,128)(2,1)} %bitcast.6), calls=%async_computation.1 | async-start | bytes 262144 | tf_op jit(solution)/shard_map/all_to_all | solution.py:326
  49.7 8.7 %all-to-all-done.1 = bf16[16,32,128]{2,1,0:T(8,128)(2,1)S(1)} async-done(((bf16[16,32,128]{2,1,0:T(8,128)(2,1)}), bf16[16,32,128]{2,1,0:T(8,128)(2,1)S(1)}, u32[]{:S(2)}, u32[]{:S(2)}) %all-to-all-start.1) | async-done | bytes 131104 | tf_op jit(solution)/shard_map/all_to_all | solution.py:326
  58.4 1.0 %hidden.1 = (f32[64,1024]{1,0:T(8,128)S(1)}, f32[64,128]{1,0:T(8,128)}) custom-call(bf16[512,128]{1,0:T(8,128)(2,1)S(1)} %bitcast.12, f32[64,1024]{1,0:T(8,128)S(1)} %outer.1.outer_ref, bf16[64,1024]{1,0:T(8,128)(2,1)S(1)} %copy-done.4), custom_call_target="tpu_custom_call" | custom-call | tf_op jit(solution)/shard_map/hidden/pallas_call | solution.py:285
  59.3 4.6 %all-to-all-start.2 = ((f32[8,8,128]{2,1,0:T(8,128)}), f32[8,8,128]{2,1,0:T(8,128)S(1)}, u32[]{:S(2)}, u32[]{:S(2)}) async-start(f32[8,8,128]{2,1,0:T(8,128)} %bitcast.8), calls=%async_computation.2 | async-start | bytes 65536 | tf_op jit(solution)/shard_map/all_to_all | solution.py:393
  64.0 5.4 %all-to-all-done.2 = f32[8,8,128]{2,1,0:T(8,128)S(1)} async-done(((f32[8,8,128]{2,1,0:T(8,128)}), f32[8,8,128]{2,1,0:T(8,128)S(1)}, u32[]{:S(2)}, u32[]{:S(2)}) %all-to-all-start.2) | async-done | bytes 32800 | tf_op jit(solution)/shard_map/all_to_all | solution.py:393
  69.4 0.8 %norm.1 = bf16[64,1024]{1,0:T(8,128)(2,1)} custom-call(f32[64,1024]{1,0:T(8,128)S(1)} %get-tuple-element.23.hidden_ref, f32[64,128]{1,0:T(8,128)S(1)} %bitcast.13, bf16[1,1024]{1,0:T(2,128)(2,1)S(1)} %reshape.31.gain_ref), custom_call_target="tpu_custom_call" | custom-call | tf_op jit(solution)/shard_map/norm/pallas_call | solution.py:285
  (27 shorter events, 0.6 us)
Async XLA Ops:
  0.0 0.7 %slice-start.2 = ((bf16[64,1024]{1,0:T(8,128)(2,1)}), bf16[8,1024]{1,0:T(8,128)(2,1)S(1)}, s32[]{:S(2)}) async-start(bf16[64,1024]{1,0:T(8,128)(2,1)} %outer_ref.1), calls=%async_computation.5 | async-start | bytes 32768 | tf_op jit(solution)/shard_map/slice | solution.py:301
  0.0 0.7 %slice-start = ((bf16[64,1024]{1,0:T(8,128)(2,1)}), bf16[8,1024]{1,0:T(8,128)(2,1)S(1)}, s32[]{:S(2)}) async-start(bf16[64,1024]{1,0:T(8,128)(2,1)} %value_ref.1), calls=%async_computation.3 | async-start | bytes 32768 | tf_op jit(solution)/shard_map/slice | solution.py:301
  0.0 0.7 %slice-start.1 = ((bf16[64,1024]{1,0:T(8,128)(2,1)}), bf16[8,1024]{1,0:T(8,128)(2,1)S(1)}, s32[]{:S(2)}) async-start(bf16[64,1024]{1,0:T(8,128)(2,1)} %inner_ref.1), calls=%async_computation.4 | async-start | bytes 32768 | tf_op jit(solution)/shard_map/slice | solution.py:301
  0.8 3.5 %copy-start = (bf16[3,7,1024]{2,1,0:T(8,128)(2,1)S(1)}, bf16[3,7,1024]{2,1,0:T(8,128)(2,1)}, u32[]{:S(2)}) copy-start(bf16[3,7,1024]{2,1,0:T(8,128)(2,1)} %tap_ref.5) | copy-start | bytes 129028
  0.8 9.4 %collective-permute-start = (bf16[24,1024]{1,0:T(8,128)(2,1)S(1)}, bf16[24,1024]{1,0:T(8,128)(2,1)S(1)}, u32[]{:S(2)}, u32[]{:S(2)}) collective-permute-start(bf16[24,1024]{1,0:T(8,128)(2,1)S(1)} %pad_maximum_fusion), channel_id=1, source_target_pairs={{0,8},{8,16},{16,24},{24,32},{32,40},{40,48},{48,56},{56,64},{64,7... | collective-permute-start | bytes 147464 | tf_op jit(solution)/shard_map/ppermute | solution.py:302
  4.3 0.9 %copy-start.1 = (bf16[64,1024]{1,0:T(8,128)(2,1)S(1)}, bf16[64,1024]{1,0:T(8,128)(2,1)}, u32[]{:S(2)}) copy-start(bf16[64,1024]{1,0:T(8,128)(2,1)} %value_ref.1) | copy-start | bytes 393220
  5.2 0.9 %copy-start.2 = (bf16[64,1024]{1,0:T(8,128)(2,1)S(1)}, bf16[64,1024]{1,0:T(8,128)(2,1)}, u32[]{:S(2)}) copy-start(bf16[64,1024]{1,0:T(8,128)(2,1)} %inner_ref.1) | copy-start | bytes 393220
  11.2 12.4 %all-to-all-start = ((bf16[16,32,128]{2,1,0:T(8,128)(2,1)}), bf16[16,32,128]{2,1,0:T(8,128)(2,1)S(1)}, u32[]{:S(2)}, u32[]{:S(2)}) async-start(bf16[16,32,128]{2,1,0:T(8,128)(2,1)} %bitcast), calls=%async_computation | async-start | bytes 262144 | tf_op jit(solution)/shard_map/all_to_all | solution.py:326
  14.8 0.7 %copy-start.5 = (bf16[128,64]{0,1:T(8,128)(2,1)S(1)}, bf16[128,64]{0,1:T(8,128)(2,1)}, u32[]{:S(2)}) copy-start(bf16[128,64]{0,1:T(8,128)(2,1)} %param.13) | copy-start | bytes 49156
  14.8 0.7 %copy-start.7 = (f32[64,16]{0,1:T(8,128)S(1)}, f32[64,16]{0,1:T(8,128)}, u32[]{:S(2)}) copy-start(f32[64,16]{0,1:T(8,128)} %param.15) | copy-start | bytes 12292
  14.8 0.7 %copy-start.6 = (f32[64,16]{0,1:T(8,128)S(1)}, f32[64,16]{0,1:T(8,128)}, u32[]{:S(2)}) copy-start(f32[64,16]{0,1:T(8,128)} %param.14) | copy-start | bytes 12292
  23.9 0.7 collective-permute-start.1
  24.7 0.7 collective-permute-start.2
  25.6 19.2 %collective-permute-start.3 = (bf16[96,128]{1,0:T(8,128)(2,1)S(1)}, bf16[96,128]{1,0:T(8,128)(2,1)S(1)}, u32[]{:S(2)}, u32[]{:S(2)}) collective-permute-start(bf16[96,128]{1,0:T(8,128)(2,1)S(1)} %chain.3), channel_id=1, source_target_pairs={{256,384},{264,392},{272,400},{280,408},{288,416},{296,424},{304,4... | collective-permute-start | bytes 73736 | tf_op jit(solution)/shard_map/ppermute | solution.py:375
  45.8 3.7 %copy-start.3 = (bf16[64,1024]{1,0:T(8,128)(2,1)S(1)}, bf16[64,1024]{1,0:T(8,128)(2,1)}, u32[]{:S(2)}) copy-start(bf16[64,1024]{1,0:T(8,128)(2,1)} %outer_ref.1) | copy-start | bytes 393220
  45.8 12.5 %all-to-all-start.1 = ((bf16[16,32,128]{2,1,0:T(8,128)(2,1)}), bf16[16,32,128]{2,1,0:T(8,128)(2,1)S(1)}, u32[]{:S(2)}, u32[]{:S(2)}) async-start(bf16[16,32,128]{2,1,0:T(8,128)(2,1)} %bitcast.6), calls=%async_computation.1 | async-start | bytes 262144 | tf_op jit(solution)/shard_map/all_to_all | solution.py:326
  49.5 8.9 %copy-start.4 = (bf16[64,1024]{1,0:T(8,128)(2,1)S(1)}, bf16[64,1024]{1,0:T(8,128)(2,1)}, u32[]{:S(2)}) copy-start(bf16[64,1024]{1,0:T(8,128)(2,1)} %residual_ref.1) | copy-start | bytes 393220
  59.3 4.6 %copy-start.8 = (bf16[1024]{0:T(1024)(128)(2,1)S(1)}, bf16[1024]{0:T(1024)(128)(2,1)}, u32[]{:S(2)}) copy-start(bf16[1024]{0:T(1024)(128)(2,1)} %param.17) | copy-start | bytes 6148
  59.3 10.1 %all-to-all-start.2 = ((f32[8,8,128]{2,1,0:T(8,128)}), f32[8,8,128]{2,1,0:T(8,128)S(1)}, u32[]{:S(2)}, u32[]{:S(2)}) async-start(f32[8,8,128]{2,1,0:T(8,128)} %bitcast.8), calls=%async_computation.2 | async-start | bytes 65536 | tf_op jit(solution)/shard_map/all_to_all | solution.py:393

commit v3 on v2

--- a/solution.py
+++ b/solution.py
@@ -181,10 +181,12 @@
     send_ref[rows:] = x_ref[(blocks - 2) * rows :]
 
 
-def chain_kernel(width, got_ref, end_ref, jump_ref, send_ref, next_ref):
+def chain_kernel(width, got_ref, end_ref, jump_ref, send_ref, next_ref, state_ref):
     rows = end_ref.shape[0]
     end = end_ref[...] + jump_ref[...] * join_three(got_ref[:rows], width)
-    next_ref[:rows] = split_three(end, width)
+    state = split_three(end, width)
+    state_ref[...] = state
+    next_ref[:rows] = state
     next_ref[rows:] = send_ref[rows:]
 
 
@@ -206,12 +208,14 @@
             out_ref[at : at + 8] = mixed[8 * block : 8 * block + 8]
 
 
-def finish_kernel(width, local_ref, first_ref, second_ref, third_ref, table_ref, step_ref, out_ref):
+def finish_kernel(
+    width, local_ref, got_01, got_23, got_12, got_13, table_ref, step_ref, jump_ref, out_ref
+):
     count = table_ref.shape[0]
     rows = 8 * count
     blocks = local_ref.shape[0] // rows
-    got = first_ref[...].astype(F32) + second_ref[...].astype(F32) + third_ref[...].astype(F32)
-    incoming = join_three(got[:rows], width)
+    got = got_01[...].astype(F32) + got_23[...].astype(F32) + got_12[...].astype(F32)
+    incoming = join_three(got[:rows], width) + jump_ref[...] * join_three(got_13[...], width)
     zeros = jnp.zeros((8, LANES), F32)
     parts = []
     for q in range(count):
@@ -295,6 +299,7 @@
     count = groups // NEAR
     width = 2 * modes
     far = size // NEAR
+    assert far == 4
     pack = 8 * count
     with_width = lambda kernel: functools.partial(kernel, width)
 
@@ -367,20 +372,35 @@
         table,
         states,
     )
-    got = []
-    for f in range(far - 1):
-        if got:
-            packed = call(with_width(chain_kernel), "chain", packet, got[-1], end, jump, packed)
-        pairs = [(NEAR * f + n, NEAR * (f + 1) + n) for n in range(NEAR)]
-        got.append(lax.ppermute(packed, "ctx", pairs))
+    def passed(x, start, end):
+        pairs = [(NEAR * start + n, NEAR * end + n) for n in range(NEAR)]
+        return lax.ppermute(x, "ctx", pairs)
+
+    got_01 = passed(packed, 0, 1)
+    got_23 = passed(packed, 2, 3)
+    repacked, state = call(
+        with_width(chain_kernel),
+        "chain",
+        [packet, pltpu.VMEM((pack, LANES), BF16)],
+        got_01,
+        end,
+        jump,
+        packed,
+    )
+    got_13 = passed(state, 1, 3)
+    got_12 = passed(repacked, 1, 2)
     mixed = call(
         with_width(finish_kernel),
         "finish",
         pltpu.VMEM((slab_rows, LANES), BF16),
         local,
-        *got,
+        got_01,
+        got_23,
+        got_12,
+        got_13,
         table,
         step,
+        jump,
     )
     hidden, sums = call(
         hidden_kernel,

time: 71 us -> 69 us (0.972)
  waiting for transfers between devices: 42.8 us -> 39.7 us
  starting transfers between devices: 17.9 us -> 19.2 us
    ppermute x3 -> x4, waiting for transfers between devices: 17.6 us -> 14.4 us  [passed(): return lax.ppermute(x, 'ctx', pairs)]
    ppermute x3 -> x4, starting transfers between devices: 2.62 us -> 3.91 us  [passed(): return lax.ppermute(x, 'ctx', pairs)]
    pallas_call x11 -> x10, Pallas kernels: 5.99 us -> 5.83 us  [call(): pl.pallas_call(kernel, in_specs=[smem] * len(scalars) + [vmem] * len(arra...]
  transfers between devices with their start and end apart: 7 -> 8, of which waited for: 5 -> 6; matrix products, arithmetic and copies ran while one was open for 0% -> 0% of each run, Pallas kernels for 2% -> 3%
where the time goes in v3:
time: 69 us; the launch traced here: 68.2 us
  waiting for transfers between devices  39.7 us (58%)
  starting transfers between devices  19.2 us (28%)
  Pallas kernels  5.83 us (8%)
  local copies, waits for them, and re-layouts  3.27 us (5%)
    all_to_all x2, waiting for transfers between devices, exchange(): lax.all_to_all(x.reshape(slab), 'ctx', 0, 0, axis_index_groups=neighbours)  16 us
    ppermute x4, waiting for transfers between devices, passed(): return lax.ppermute(x, 'ctx', pairs)  14.4 us
    all_to_all x2, starting transfers between devices, exchange(): lax.all_to_all(x.reshape(slab), 'ctx', 0, 0, axis_index_groups=neighbours)  7.16 us
    pallas_call x10, Pallas kernels, call(): pl.pallas_call(kernel, in_specs=[smem] * len(scalars) + [vmem] * len(arra...  5.83 us
    all_to_all x1, waiting for transfers between devices, on_device(): all_sums = lax.all_to_all(sums.reshape(parts, 8, LANES), 'tp', 0, 0)  5.43 us
    all_to_all x1, starting transfers between devices, on_device(): all_sums = lax.all_to_all(sums.reshape(parts, 8, LANES), 'tp', 0, 0)  4.6 us
    ppermute x4, starting transfers between devices, passed(): return lax.ppermute(x, 'ctx', pairs)  3.91 us
    ppermute x1, waiting for transfers between devices, on_device(): halo = lax.ppermute(sent, 'ctx', [(i, i + 1) for i in range(size - 1)])  3.79 us
  transfers between devices with their start and end apart: 8, of which 6 were waited for; matrix products, arithmetic and copies ran while one was open for 0% of the time, Pallas kernels for 3%

profile of v3, /device:TPU:384, one launch (start us, length us, event | category | flops | bytes accessed | tf_op | source)
XLA Modules:
  0.0 68.2 jit_solution(5733874571895085642)
XLA Ops:
  0.0 0.7 %slice-done.2 = bf16[8,1024]{1,0:T(8,128)(2,1)S(1)} async-done(((bf16[64,1024]{1,0:T(8,128)(2,1)}), bf16[8,1024]{1,0:T(8,128)(2,1)S(1)}, s32[]{:S(2)}) %slice-start.2) | async-done | bytes 16408 | tf_op jit(solution)/shard_map/slice | solution.py:306
  0.8 3.5 %collective-permute-start = (bf16[24,1024]{1,0:T(8,128)(2,1)S(1)}, bf16[24,1024]{1,0:T(8,128)(2,1)S(1)}, u32[]{:S(2)}, u32[]{:S(2)}) collective-permute-start(bf16[24,1024]{1,0:T(8,128)(2,1)S(1)} %pad_maximum_fusion), channel_id=1, source_target_pairs={{0,8},{8,16},{16,24},{24,32},{32,40},{40,48},{48,56},{56,64},{64,7... | collective-permute-start | bytes 147464 | tf_op jit(solution)/shard_map/ppermute | solution.py:307
  4.3 0.9 %copy-done.1 = bf16[64,1024]{1,0:T(8,128)(2,1)S(1)} copy-done((bf16[64,1024]{1,0:T(8,128)(2,1)S(1)}, bf16[64,1024]{1,0:T(8,128)(2,1)}, u32[]{:S(2)}) %copy-start.1) | copy-done | bytes 131096
  5.2 0.9 %copy-done.2 = bf16[64,1024]{1,0:T(8,128)(2,1)S(1)} copy-done((bf16[64,1024]{1,0:T(8,128)(2,1)S(1)}, bf16[64,1024]{1,0:T(8,128)(2,1)}, u32[]{:S(2)}) %copy-start.2) | copy-done | bytes 131096
  6.4 3.8 %collective-permute-done.halo_ref = bf16[24,1024]{1,0:T(8,128)(2,1)S(1)} collective-permute-done((bf16[24,1024]{1,0:T(8,128)(2,1)S(1)}, bf16[24,1024]{1,0:T(8,128)(2,1)S(1)}, u32[]{:S(2)}, u32[]{:S(2)}) %collective-permute-start) | collective-permute-done | bytes 49184 | tf_op jit(solution)/shard_map/ppermute | solution.py:307
  10.2 1.0 %product.1 = bf16[512,128]{1,0:T(8,128)(2,1)} custom-call(bf16[24,1024]{1,0:T(8,128)(2,1)S(1)} %collective-permute-done.halo_ref, f32[2,8,1024]{2,1,0:T(8,128)S(1)} %get-tuple-element.17.head_ref, f32[56,1024]{1,0:T(8,128)S(1)} %get-tuple-element.18.body_ref, bf16[3,7,1024]{2,1,0:T(8,128)(2,1)S(1)} %copy-done), custom_call_target="tpu_custom_call" | custom-call | tf_op jit(solution)/shard_map/product/pallas_call | solution.py:289
  11.2 3.5 %all-to-all-start = ((bf16[16,32,128]{2,1,0:T(8,128)(2,1)}), bf16[16,32,128]{2,1,0:T(8,128)(2,1)S(1)}, u32[]{:S(2)}, u32[]{:S(2)}) async-start(bf16[16,32,128]{2,1,0:T(8,128)(2,1)} %bitcast), calls=%async_computation | async-start | bytes 262144 | tf_op jit(solution)/shard_map/all_to_all | solution.py:331
  14.8 0.7 copy-done.5
  15.5 0.8 %tables.1 = (bf16[4,7,128,128]{3,2,1,0:T(8,128)(2,1)S(1)}, f32[32,128]{1,0:T(8,128)S(1)}, f32[32,128]{1,0:T(8,128)S(1)}) custom-call(s32[1]{0:T(128)} %bitcast.2.place, f32[16,64]{1,0:T(8,128)S(1)} %bitcast.15, f32[16,64]{1,0:T(8,128)S(1)} %bitcast.16, bf16[64,128]{1,0:T(8,128)(2,1)S(1)} %bitcast.14), custom_call_target="tpu_custom_call" | custom-call | tf_op jit(solution)/shard_map/tables/pallas_call | solution.py:289
  16.3 7.3 %all-to-all-done = bf16[16,32,128]{2,1,0:T(8,128)(2,1)S(1)} async-done(((bf16[16,32,128]{2,1,0:T(8,128)(2,1)}), bf16[16,32,128]{2,1,0:T(8,128)(2,1)S(1)}, u32[]{:S(2)}, u32[]{:S(2)}) %all-to-all-start) | async-done | bytes 131104 | tf_op jit(solution)/shard_map/all_to_all | solution.py:331
  23.9 0.7 collective-permute-start.1
  24.6 1.3 %collective-permute-start.2 = (bf16[96,128]{1,0:T(8,128)(2,1)S(1)}, bf16[96,128]{1,0:T(8,128)(2,1)S(1)}, u32[]{:S(2)}, u32[]{:S(2)}) collective-permute-start(bf16[96,128]{1,0:T(8,128)(2,1)S(1)} %get-tuple-element.22.send_ref), channel_id=1, source_target_pairs={{256,384},{264,392},{272,400},{280,408},{288,416},{296,424},{304,4... | collective-permute-start | bytes 73736 | tf_op jit(solution)/shard_map/ppermute | solution.py:377
  26.0 0.7 collective-permute-start.3
  26.7 1.3 %collective-permute-start.4 = (bf16[32,128]{1,0:T(8,128)(2,1)S(1)}, bf16[32,128]{1,0:T(8,128)(2,1)S(1)}, u32[]{:S(2)}, u32[]{:S(2)}) collective-permute-start(bf16[32,128]{1,0:T(8,128)(2,1)S(1)} %get-tuple-element.26), channel_id=1, source_target_pairs={{128,384},{136,392},{144,400},{152,408},{160,416},{168,424},{176,4... | collective-permute-start | bytes 24584 | tf_op jit(solution)/shard_map/ppermute | solution.py:377
  28.0 0.3 local.1.local_ref
  28.3 5.9 %collective-permute-done.2.got_23 = bf16[96,128]{1,0:T(8,128)(2,1)S(1)} collective-permute-done((bf16[96,128]{1,0:T(8,128)(2,1)S(1)}, bf16[96,128]{1,0:T(8,128)(2,1)S(1)}, u32[]{:S(2)}, u32[]{:S(2)}) %collective-permute-start.2) | collective-permute-done | bytes 24608 | tf_op jit(solution)/shard_map/ppermute | solution.py:377
  34.2 8.6 %collective-permute-done.4.got_13 = bf16[32,128]{1,0:T(8,128)(2,1)S(1)} collective-permute-done((bf16[32,128]{1,0:T(8,128)(2,1)S(1)}, bf16[32,128]{1,0:T(8,128)(2,1)S(1)}, u32[]{:S(2)}, u32[]{:S(2)}) %collective-permute-start.4) | collective-permute-done | bytes 8224 | tf_op jit(solution)/shard_map/ppermute | solution.py:377
  42.8 1.1 %finish.1 = bf16[512,128]{1,0:T(8,128)(2,1)} custom-call(f32[512,128]{1,0:T(8,128)S(1)} %local.1.local_ref, bf16[96,128]{1,0:T(8,128)(2,1)S(1)} %collective-permute-done.1.got_ref.got_01, bf16[96,128]{1,0:T(8,128)(2,1)S(1)} %collective-permute-done.2.got_23, bf16[96,128]{1,0:T(8,128)(2,1)S(1)} %collective-permute-done.3.got_12, ...), custom_call_target="tpu_custom_call" | custom-call | tf_op jit(solution)/shard_map/finish/pallas_call | solution.py:289
  43.8 3.6 %all-to-all-start.1 = ((bf16[16,32,128]{2,1,0:T(8,128)(2,1)}), bf16[16,32,128]{2,1,0:T(8,128)(2,1)S(1)}, u32[]{:S(2)}, u32[]{:S(2)}) async-start(bf16[16,32,128]{2,1,0:T(8,128)(2,1)} %bitcast.6), calls=%async_computation.1 | async-start | bytes 262144 | tf_op jit(solution)/shard_map/all_to_all | solution.py:331
  47.7 8.7 %all-to-all-done.1 = bf16[16,32,128]{2,1,0:T(8,128)(2,1)S(1)} async-done(((bf16[16,32,128]{2,1,0:T(8,128)(2,1)}), bf16[16,32,128]{2,1,0:T(8,128)(2,1)S(1)}, u32[]{:S(2)}, u32[]{:S(2)}) %all-to-all-start.1) | async-done | bytes 131104 | tf_op jit(solution)/shard_map/all_to_all | solution.py:331
  56.4 1.0 %hidden.1 = (f32[64,1024]{1,0:T(8,128)S(1)}, f32[64,128]{1,0:T(8,128)}) custom-call(bf16[512,128]{1,0:T(8,128)(2,1)S(1)} %bitcast.12, f32[64,1024]{1,0:T(8,128)S(1)} %outer.1.outer_ref, bf16[64,1024]{1,0:T(8,128)(2,1)S(1)} %copy-done.4), custom_call_target="tpu_custom_call" | custom-call | tf_op jit(solution)/shard_map/hidden/pallas_call | solution.py:289
  57.3 4.6 %all-to-all-start.2 = ((f32[8,8,128]{2,1,0:T(8,128)}), f32[8,8,128]{2,1,0:T(8,128)S(1)}, u32[]{:S(2)}, u32[]{:S(2)}) async-start(f32[8,8,128]{2,1,0:T(8,128)} %bitcast.8), calls=%async_computation.2 | async-start | bytes 65536 | tf_op jit(solution)/shard_map/all_to_all | solution.py:413
  62.0 5.4 %all-to-all-done.2 = f32[8,8,128]{2,1,0:T(8,128)S(1)} async-done(((f32[8,8,128]{2,1,0:T(8,128)}), f32[8,8,128]{2,1,0:T(8,128)S(1)}, u32[]{:S(2)}, u32[]{:S(2)}) %all-to-all-start.2) | async-done | bytes 32800 | tf_op jit(solution)/shard_map/all_to_all | solution.py:413
  67.4 0.8 %norm.1 = bf16[64,1024]{1,0:T(8,128)(2,1)} custom-call(f32[64,1024]{1,0:T(8,128)S(1)} %get-tuple-element.27.hidden_ref, f32[64,128]{1,0:T(8,128)S(1)} %bitcast.13, bf16[1,1024]{1,0:T(2,128)(2,1)S(1)} %reshape.31.gain_ref), custom_call_target="tpu_custom_call" | custom-call | tf_op jit(solution)/shard_map/norm/pallas_call | solution.py:289
  (28 shorter events, 0.9 us)
Async XLA Ops:
  0.0 0.7 %slice-start.2 = ((bf16[64,1024]{1,0:T(8,128)(2,1)}), bf16[8,1024]{1,0:T(8,128)(2,1)S(1)}, s32[]{:S(2)}) async-start(bf16[64,1024]{1,0:T(8,128)(2,1)} %outer_ref.1), calls=%async_computation.5 | async-start | bytes 32768 | tf_op jit(solution)/shard_map/slice | solution.py:306
  0.0 0.7 %slice-start = ((bf16[64,1024]{1,0:T(8,128)(2,1)}), bf16[8,1024]{1,0:T(8,128)(2,1)S(1)}, s32[]{:S(2)}) async-start(bf16[64,1024]{1,0:T(8,128)(2,1)} %value_ref.1), calls=%async_computation.3 | async-start | bytes 32768 | tf_op jit(solution)/shard_map/slice | solution.py:306
  0.0 0.7 %slice-start.1 = ((bf16[64,1024]{1,0:T(8,128)(2,1)}), bf16[8,1024]{1,0:T(8,128)(2,1)S(1)}, s32[]{:S(2)}) async-start(bf16[64,1024]{1,0:T(8,128)(2,1)} %inner_ref.1), calls=%async_computation.4 | async-start | bytes 32768 | tf_op jit(solution)/shard_map/slice | solution.py:306
  0.8 3.5 %copy-start = (bf16[3,7,1024]{2,1,0:T(8,128)(2,1)S(1)}, bf16[3,7,1024]{2,1,0:T(8,128)(2,1)}, u32[]{:S(2)}) copy-start(bf16[3,7,1024]{2,1,0:T(8,128)(2,1)} %tap_ref.5) | copy-start | bytes 129028
  0.8 9.4 %collective-permute-start = (bf16[24,1024]{1,0:T(8,128)(2,1)S(1)}, bf16[24,1024]{1,0:T(8,128)(2,1)S(1)}, u32[]{:S(2)}, u32[]{:S(2)}) collective-permute-start(bf16[24,1024]{1,0:T(8,128)(2,1)S(1)} %pad_maximum_fusion), channel_id=1, source_target_pairs={{0,8},{8,16},{16,24},{24,32},{32,40},{40,48},{48,56},{56,64},{64,7... | collective-permute-start | bytes 147464 | tf_op jit(solution)/shard_map/ppermute | solution.py:307
  4.3 0.9 %copy-start.1 = (bf16[64,1024]{1,0:T(8,128)(2,1)S(1)}, bf16[64,1024]{1,0:T(8,128)(2,1)}, u32[]{:S(2)}) copy-start(bf16[64,1024]{1,0:T(8,128)(2,1)} %value_ref.1) | copy-start | bytes 393220
  5.2 0.9 %copy-start.2 = (bf16[64,1024]{1,0:T(8,128)(2,1)S(1)}, bf16[64,1024]{1,0:T(8,128)(2,1)}, u32[]{:S(2)}) copy-start(bf16[64,1024]{1,0:T(8,128)(2,1)} %inner_ref.1) | copy-start | bytes 393220
  11.2 12.4 %all-to-all-start = ((bf16[16,32,128]{2,1,0:T(8,128)(2,1)}), bf16[16,32,128]{2,1,0:T(8,128)(2,1)S(1)}, u32[]{:S(2)}, u32[]{:S(2)}) async-start(bf16[16,32,128]{2,1,0:T(8,128)(2,1)} %bitcast), calls=%async_computation | async-start | bytes 262144 | tf_op jit(solution)/shard_map/all_to_all | solution.py:331
  14.8 0.7 %copy-start.5 = (bf16[128,64]{0,1:T(8,128)(2,1)S(1)}, bf16[128,64]{0,1:T(8,128)(2,1)}, u32[]{:S(2)}) copy-start(bf16[128,64]{0,1:T(8,128)(2,1)} %param.13) | copy-start | bytes 49156
  14.8 0.7 %copy-start.7 = (f32[64,16]{0,1:T(8,128)S(1)}, f32[64,16]{0,1:T(8,128)}, u32[]{:S(2)}) copy-start(f32[64,16]{0,1:T(8,128)} %param.15) | copy-start | bytes 12292
  14.8 0.7 %copy-start.6 = (f32[64,16]{0,1:T(8,128)S(1)}, f32[64,16]{0,1:T(8,128)}, u32[]{:S(2)}) copy-start(f32[64,16]{0,1:T(8,128)} %param.14) | copy-start | bytes 12292
  23.9 2.0 %collective-permute-start.1 = (bf16[96,128]{1,0:T(8,128)(2,1)S(1)}, bf16[96,128]{1,0:T(8,128)(2,1)S(1)}, u32[]{:S(2)}, u32[]{:S(2)}) collective-permute-start(bf16[96,128]{1,0:T(8,128)(2,1)S(1)} %get-tuple-element.22.send_ref), channel_id=1, source_target_pairs={{0,128},{8,136},{16,144},{24,152},{32,160},{40,168},{48,176},{56,1... | collective-permute-start | bytes 73736 | tf_op jit(solution)/shard_map/ppermute | solution.py:377
  24.6 9.6 %collective-permute-start.2 = (bf16[96,128]{1,0:T(8,128)(2,1)S(1)}, bf16[96,128]{1,0:T(8,128)(2,1)S(1)}, u32[]{:S(2)}, u32[]{:S(2)}) collective-permute-start(bf16[96,128]{1,0:T(8,128)(2,1)S(1)} %get-tuple-element.22.send_ref), channel_id=1, source_target_pairs={{256,384},{264,392},{272,400},{280,408},{288,416},{296,424},{304,4... | collective-permute-start | bytes 73736 | tf_op jit(solution)/shard_map/ppermute | solution.py:377
  26.0 16.7 %collective-permute-start.3 = (bf16[96,128]{1,0:T(8,128)(2,1)S(1)}, bf16[96,128]{1,0:T(8,128)(2,1)S(1)}, u32[]{:S(2)}, u32[]{:S(2)}) collective-permute-start(bf16[96,128]{1,0:T(8,128)(2,1)S(1)} %get-tuple-element.25), channel_id=1, source_target_pairs={{128,256},{136,264},{144,272},{152,280},{160,288},{168,296},{176,3... | collective-permute-start | bytes 73736 | tf_op jit(solution)/shard_map/ppermute | solution.py:377
  26.7 16.1 %collective-permute-start.4 = (bf16[32,128]{1,0:T(8,128)(2,1)S(1)}, bf16[32,128]{1,0:T(8,128)(2,1)S(1)}, u32[]{:S(2)}, u32[]{:S(2)}) collective-permute-start(bf16[32,128]{1,0:T(8,128)(2,1)S(1)} %get-tuple-element.26), channel_id=1, source_target_pairs={{128,384},{136,392},{144,400},{152,408},{160,416},{168,424},{176,4... | collective-permute-start | bytes 24584 | tf_op jit(solution)/shard_map/ppermute | solution.py:377
  43.8 3.7 %copy-start.3 = (bf16[64,1024]{1,0:T(8,128)(2,1)S(1)}, bf16[64,1024]{1,0:T(8,128)(2,1)}, u32[]{:S(2)}) copy-start(bf16[64,1024]{1,0:T(8,128)(2,1)} %outer_ref.1) | copy-start | bytes 393220
  43.8 12.5 %all-to-all-start.1 = ((bf16[16,32,128]{2,1,0:T(8,128)(2,1)}), bf16[16,32,128]{2,1,0:T(8,128)(2,1)S(1)}, u32[]{:S(2)}, u32[]{:S(2)}) async-start(bf16[16,32,128]{2,1,0:T(8,128)(2,1)} %bitcast.6), calls=%async_computation.1 | async-start | bytes 262144 | tf_op jit(solution)/shard_map/all_to_all | solution.py:331
  47.5 8.9 %copy-start.4 = (bf16[64,1024]{1,0:T(8,128)(2,1)S(1)}, bf16[64,1024]{1,0:T(8,128)(2,1)}, u32[]{:S(2)}) copy-start(bf16[64,1024]{1,0:T(8,128)(2,1)} %residual_ref.1) | copy-start | bytes 393220
  57.3 4.6 %copy-start.8 = (bf16[1024]{0:T(1024)(128)(2,1)S(1)}, bf16[1024]{0:T(1024)(128)(2,1)}, u32[]{:S(2)}) copy-start(bf16[1024]{0:T(1024)(128)(2,1)} %param.17) | copy-start | bytes 6148
  57.3 10.0 %all-to-all-start.2 = ((f32[8,8,128]{2,1,0:T(8,128)}), f32[8,8,128]{2,1,0:T(8,128)S(1)}, u32[]{:S(2)}, u32[]{:S(2)}) async-start(f32[8,8,128]{2,1,0:T(8,128)} %bitcast.8), calls=%async_computation.2 | async-start | bytes 65536 | tf_op jit(solution)/shard_map/all_to_all | solution.py:413

commit v4 on v3

--- a/solution.py
+++ b/solution.py
@@ -12,6 +12,8 @@
 BF16 = jnp.bfloat16
 LANES = 128
 HALO = 8
+FEAT = 7
+EDGE = 16
 NEAR = 16
 
 
@@ -21,6 +23,10 @@
 
 def in_vmem(*arrays):
     return [pltpu.with_memory_space_constraint(a, pltpu.VMEM) for a in arrays]
+
+
+def dot(a, b):
+    return jnp.dot(a, b, preferred_element_type=F32)
 
 
 def split(x):
@@ -49,7 +55,16 @@
     return jnp.where(copy == 1, low.astype(F32), high.astype(F32)).astype(BF16)
 
 
-def tables_kernel(place, decay_ref, residue_ref, medium_ref, table_ref, step_ref, jump_ref):
+def tables_kernel(
+    place, decay_ref, residue_ref, medium_ref, tap_ref, table_ref, step_ref, jump_ref, rest_ref, mine_ref
+):
+    channels = tap_ref.shape[2]
+    half = LANES // 2
+    at, to = iota((channels, LANES), 0), iota((channels, LANES), 1)
+    chosen = at == place[0] * half + to % half
+    for_inner = jnp.where(chosen & (to < half), 1.0, 0.0).astype(BF16)
+    for_value = jnp.where(chosen & (to >= half), 1.0, 0.0).astype(BF16)
+    mine_ref[...] = dot(tap_ref[1], for_inner) + dot(tap_ref[2], for_value)
     modes, groups = decay_ref.shape
     square = (LANES, LANES)
     block = LANES // 2
@@ -99,6 +114,7 @@
         rows = slice(8 * q, 8 * q + 8)
         step_ref[rows] = jnp.broadcast_to(jnp.exp(-rate_lanes * block), (8, LANES))
         jump_ref[rows] = jnp.broadcast_to(jnp.exp(-rate_lanes * (block * NEAR)), (8, LANES))
+        rest_ref[rows] = jnp.broadcast_to(jnp.exp(-rate_lanes * (block * (NEAR - 1))), (8, LANES))
 
 
 def featurized(tap_ref, which, lanes, padded, rows):
@@ -113,33 +129,19 @@
     return slice(tile * LANES, (tile + 1) * LANES)
 
 
-def body_kernel(inner_ref, value_ref, tap_ref, out_ref, head_ref, padded):
+def pack_kernel(inner_ref, value_ref, outer_ref, out_ref, tail_ref):
+    tail_ref[...] = outer_ref[...]
     rows, channels = inner_ref.shape
+    half = LANES // 2
+    low = iota((rows, LANES), 1) < half
     for tile in range(channels // LANES):
         lanes = tile_lanes(tile)
-        feats = []
-        for n, ref in enumerate((inner_ref, value_ref)):
-            wide = ref[:, lanes].astype(F32)
-            padded[n, tile] = wide
-            head_ref[n, :, lanes] = wide[:HALO]
-            feats.append(featurized(tap_ref, n + 1, lanes, padded.at[n, tile], rows - HALO))
-        out_ref[:, lanes] = feats[0] * feats[1]
-
-
-def product_kernel(halo_ref, head_ref, body_ref, tap_ref, out_ref, padded):
-    channels = body_ref.shape[1]
-    for tile in range(channels // LANES):
-        lanes = tile_lanes(tile)
-        feats = []
-        for n in range(2):
-            padded[n, tile, :HALO] = halo_ref[HALO * (n + 1) : HALO * (n + 2), lanes].astype(F32)
-            padded[n, tile, HALO:] = head_ref[n, :, lanes]
-            feats.append(featurized(tap_ref, n + 1, lanes, padded.at[n, tile], HALO))
-        product = jnp.concatenate([feats[0] * feats[1], body_ref[:, lanes]], 0)
-        product = product.astype(BF16).astype(F32)
-        both = jnp.concatenate([product, pltpu.roll(product, LANES - 8, 1)], 0).T
-        slabs = both.reshape(LANES // 16, 16, LANES)[:, :8].reshape(LANES // 2, LANES)
-        out_ref[tile * (LANES // 2) : (tile + 1) * (LANES // 2)] = slabs.astype(BF16)
+        inner = inner_ref[:, lanes].astype(F32)
+        value = value_ref[:, lanes].astype(F32)
+        first = jnp.where(low, inner, pltpu.roll(value, half, 1))
+        second = jnp.where(low, pltpu.roll(inner, half, 1), value)
+        out_ref[2 * tile * rows : (2 * tile + 1) * rows] = first.astype(BF16)
+        out_ref[(2 * tile + 1) * rows : (2 * tile + 2) * rows] = second.astype(BF16)
 
 
 def outer_kernel(halo_ref, outer_ref, tap_ref, out_ref, padded):
@@ -151,41 +153,90 @@
         out_ref[:, lanes] = featurized(tap_ref, 0, lanes, padded.at[tile], rows)
 
 
-def dot(a, b):
-    return jnp.dot(a, b, preferred_element_type=F32)
-
-
 def of_group(x, q, count):
     return x.reshape(x.shape[0] // (8 * count), count, 8, LANES)[:, q].reshape(-1, LANES)
 
 
-def states_kernel(width, x_ref, table_ref, step_ref, state_ref, end_ref, send_ref):
+def gated(tap_ref, padded, rows):
+    total = None
+    for k in range(FEAT):
+        term = tap_ref[k : k + 1] * padded[HALO - k : HALO - k + rows]
+        total = term if total is None else total + term
+    return (total * pltpu.roll(total, LANES // 2, 1)).astype(BF16).astype(F32)
+
+
+def slabs_of(product):
+    both = jnp.concatenate([product, pltpu.roll(product, LANES - 8, 1)], 0).T
+    return both.reshape(LANES // 16, 16, LANES)[:, :8].reshape(LANES // 2, LANES)
+
+
+def missing(tap_ref, tail, head):
+    block = LANES // 2
+    product = gated(tap_ref, jnp.concatenate([tail[-HALO:], head[:HALO]], 0), HALO)
+    kept = (iota(product.shape, 0) < FEAT - 1) & (iota(product.shape, 1) < block)
+    product = jnp.where(kept, product, 0.0)
+    return slabs_of(jnp.concatenate([product, jnp.zeros((block - HALO, LANES), F32)], 0))[: block // 2]
+
+
+def to_states(table_ref, slab):
     count = table_ref.shape[0]
-    blocks = x_ref.shape[0] // (8 * count)
-    wide = x_ref[...].astype(F32)
+    parts = []
+    for q in range(count):
+        x = slab[8 * q : 8 * q + 8].astype(BF16)
+        parts.append(dot(x, table_ref[q, 4]) + dot(x, table_ref[q, 5]))
+    return jnp.concatenate(parts, 0)
+
+
+def states_kernel(
+    width, place, raw_ref, tap_ref, table_ref, step_ref, x_ref, state_ref, end_ref, send_ref, padded
+):
+    count = table_ref.shape[0]
+    block = LANES // 2
+    blocks = raw_ref.shape[0] // block
+    padded[:HALO] = jnp.zeros((HALO, LANES), F32)
+    padded[HALO:] = raw_ref[...].astype(F32)
+    low = iota((block, LANES), 1) < block
+    early = (iota((block, LANES), 0) < FEAT - 1) & (place[1] > 0)
+    rows = 8 * count
+    slabs = []
+    for pair in range(blocks // 2):
+        products = []
+        for b in (2 * pair, 2 * pair + 1):
+            product = gated(tap_ref, padded.at[b * block : (b + 1) * block + HALO], block)
+            products.append(jnp.where(early, 0.0, product) if b == 0 else product)
+        slabs.append(slabs_of(jnp.where(low, products[0], products[1])))
+    wide = jnp.concatenate(slabs, 0)
+    x_ref[...] = wide.astype(BF16)
     ends = []
     for q in range(count):
         x = of_group(wide, q, count).astype(BF16)
         local = dot(x, table_ref[q, 4]) + dot(x, table_ref[q, 5])
         step = step_ref[8 * q : 8 * q + 8]
         carry = jnp.zeros((8, LANES), F32)
-        for block in range(blocks):
-            at = 8 * (count * block + q)
+        for b in range(blocks):
+            at = rows * b + 8 * q
             state_ref[at : at + 8] = carry
-            carry = carry * step + local[8 * block : 8 * block + 8]
+            carry = carry * step + local[8 * b : 8 * b + 8]
         ends.append(carry)
     end = jnp.concatenate(ends, 0)
     end_ref[...] = end
-    rows = 8 * count
     send_ref[:rows] = split_three(end, width)
-    send_ref[rows:] = x_ref[(blocks - 2) * rows :]
-
-
-def chain_kernel(width, got_ref, end_ref, jump_ref, send_ref, next_ref, state_ref):
+    send_ref[rows : 3 * rows] = wide[(blocks - 2) * rows :].astype(BF16)
+    send_ref[3 * rows : 3 * rows + EDGE] = raw_ref[blocks * block - EDGE :]
+    send_ref[3 * rows + EDGE :] = raw_ref[:EDGE]
+
+
+def chain_kernel(
+    width, got_ref, raw_ref, tap_ref, table_ref, end_ref, jump_ref, rest_ref, send_ref, next_ref, short_ref
+):
     rows = end_ref.shape[0]
-    end = end_ref[...] + jump_ref[...] * join_three(got_ref[:rows], width)
+    tail = got_ref[3 * rows : 3 * rows + EDGE].astype(F32)
+    slab = missing(tap_ref, tail, raw_ref[:EDGE].astype(F32))
+    end = end_ref[...] + rest_ref[...] * to_states(table_ref, slab)
+    end = end + jump_ref[...] * join_three(got_ref[:rows], width)
     state = split_three(end, width)
-    state_ref[...] = state
+    short_ref[:rows] = state
+    short_ref[rows:] = send_ref[3 * rows : 3 * rows + EDGE]
     next_ref[:rows] = state
     next_ref[rows:] = send_ref[rows:]
 
@@ -209,13 +260,33 @@
 
 
 def finish_kernel(
-    width, local_ref, got_01, got_23, got_12, got_13, table_ref, step_ref, jump_ref, out_ref
+    width,
+    place,
+    local_ref,
+    got_01,
+    got_23,
+    got_12,
+    got_13,
+    raw_ref,
+    tap_ref,
+    table_ref,
+    step_ref,
+    jump_ref,
+    rest_ref,
+    out_ref,
 ):
     count = table_ref.shape[0]
     rows = 8 * count
     blocks = local_ref.shape[0] // rows
     got = got_01[...].astype(F32) + got_23[...].astype(F32) + got_12[...].astype(F32)
-    incoming = join_three(got[:rows], width) + jump_ref[...] * join_three(got_13[...], width)
+    edge = slice(3 * rows, 3 * rows + EDGE)
+    far_tail = got_13[rows:].astype(F32)
+    far_slab = missing(tap_ref, far_tail, got_23[3 * rows + EDGE :].astype(F32))
+    own_slab = missing(tap_ref, got[edge], raw_ref[:EDGE].astype(F32))
+    own_slab = jnp.where(place[1] > 0, own_slab, 0.0)
+    incoming = join_three(got[:rows], width) + rest_ref[...] * to_states(table_ref, far_slab)
+    incoming = incoming + jump_ref[...] * join_three(got_13[:rows], width)
+    added = to_states(table_ref, own_slab)
     zeros = jnp.zeros((8, LANES), F32)
     parts = []
     for q in range(count):
@@ -226,12 +297,16 @@
         for block in range(blocks):
             states.append(state)
             state = state * step
+            if block == 0:
+                state = state + added[at]
         mixed = dot(two_parts(jnp.concatenate(states, 0), width), table_ref[q, 6])
-        last_but_one, last = got[rows:][at], got[2 * rows :][at]
-        before = jnp.concatenate([last, zeros], 0).astype(BF16)
-        earlier = jnp.concatenate([last_but_one, last], 0).astype(BF16)
-        start = dot(before, table_ref[q, 2]) + dot(earlier, table_ref[q, 3])
-        mixed = jnp.concatenate([mixed[:16] + start, mixed[16:]], 0)
+        last_but_one, last, first = got[rows:][at], got[2 * rows :][at], own_slab[at]
+        now = jnp.concatenate([first, zeros, zeros, zeros], 0).astype(BF16)
+        before = jnp.concatenate([last, first, zeros, zeros], 0).astype(BF16)
+        earlier = jnp.concatenate([last_but_one, last, first, zeros], 0).astype(BF16)
+        start = dot(now, table_ref[q, 0]) + dot(now, table_ref[q, 1])
+        start = start + dot(before, table_ref[q, 2]) + dot(earlier, table_ref[q, 3])
+        mixed = jnp.concatenate([mixed[:32] + start, mixed[32:]], 0)
         parts.append(mixed.reshape(blocks, 8, LANES))
     total = local_ref[...] + jnp.concatenate(parts, 1).reshape(local_ref.shape)
     out_ref[...] = total.astype(BF16)
@@ -303,46 +378,44 @@
     pack = 8 * count
     with_width = lambda kernel: functools.partial(kernel, width)
 
-    sent = jnp.concatenate([a[rows - HALO :] for a in (outer_input, inner_input, value_input)], 0)
-    halo = lax.ppermute(sent, "ctx", [(i, i + 1) for i in range(size - 1)])
-    body, head = call(
-        body_kernel,
-        "body",
-        [pltpu.VMEM((rows - HALO, channels), F32), pltpu.VMEM((2, HALO, channels), F32)],
-        inner_input,
-        value_input,
-        feature_taps,
-        scratch=[pltpu.VMEM((2, tiles, rows, LANES), F32)],
-    )
-    slabs = call(
-        product_kernel,
-        "product",
-        pltpu.VMEM((slab_rows, LANES), BF16),
-        halo,
-        head,
-        body,
-        feature_taps,
-        scratch=[pltpu.VMEM((2, tiles, 2 * HALO, LANES), F32)],
-    )
+    raw, outer_tail = pl.pallas_call(
+        pack_kernel,
+        grid=(1,),
+        in_specs=[
+            pl.BlockSpec((rows, channels), lambda i: (0, 0)),
+            pl.BlockSpec((rows, channels), lambda i: (0, 0)),
+            pl.BlockSpec((HALO, channels), lambda i: (rows // HALO - 1, 0)),
+        ],
+        out_shape=[pltpu.VMEM((NEAR * rows, LANES), BF16), pltpu.VMEM((HALO, channels), BF16)],
+        out_specs=[vmem, vmem],
+        name="pack",
+    )(inner_input, value_input, outer_input)
     neighbours = [[NEAR * f + n for n in range(NEAR)] for f in range(far)]
 
     def exchange(x):
-        slab = (NEAR, slab_rows // NEAR, LANES)
+        slab = (NEAR, x.shape[0] // NEAR, LANES)
         y = lax.all_to_all(x.reshape(slab), "ctx", 0, 0, axis_index_groups=neighbours)
-        return y.reshape(slab_rows, LANES)
-
-    place = (lax.axis_index("ctx") % NEAR).reshape(1).astype(jnp.int32)
-    table, step, jump = call(
+        return y.reshape(x.shape)
+
+    arrived = exchange(raw)
+    halo = lax.ppermute(outer_tail, "ctx", [(i, i + 1) for i in range(size - 1)])
+    arrived, halo = lax.optimization_barrier((arrived, halo))
+    index = lax.axis_index("ctx")
+    place = jnp.stack([index % NEAR, index // NEAR]).astype(jnp.int32)
+    table, step, jump, rest, taps = call(
         tables_kernel,
         "tables",
         [
             pltpu.VMEM((count, 7, LANES, LANES), BF16),
             pltpu.VMEM((pack, LANES), F32),
             pltpu.VMEM((pack, LANES), F32),
+            pltpu.VMEM((pack, LANES), F32),
+            pltpu.VMEM((FEAT, LANES), F32),
         ],
         decay_rates.T,
         residues.T,
         medium_taps.T,
+        feature_taps,
         scalars=(place,),
     )
     outer_feat = call(
@@ -354,24 +427,32 @@
         feature_taps,
         scratch=[pltpu.VMEM((tiles, HALO + rows, LANES), F32)],
     )
-    arrived = exchange(slabs)
-    packet = pltpu.VMEM((3 * pack, LANES), BF16)
-    states, end, packed = call(
+    packet = pltpu.VMEM((3 * pack + 2 * EDGE, LANES), BF16)
+    x, states, end, packed = call(
         with_width(states_kernel),
         "states",
-        [pltpu.VMEM((slab_rows, LANES), F32), pltpu.VMEM((pack, LANES), F32), packet],
+        [
+            pltpu.VMEM((slab_rows, LANES), BF16),
+            pltpu.VMEM((slab_rows, LANES), F32),
+            pltpu.VMEM((pack, LANES), F32),
+            packet,
+        ],
         arrived,
+        taps,
         table,
         step,
+        scalars=(place,),
+        scratch=[pltpu.VMEM((HALO + NEAR * rows, LANES), F32)],
     )
     local = call(
         with_width(local_kernel),
         "local",
         pltpu.VMEM((slab_rows, LANES), F32),
-        arrived,
+        x,
         table,
         states,
     )
+
     def passed(x, start, end):
         pairs = [(NEAR * start + n, NEAR * end + n) for n in range(NEAR)]
         return lax.ppermute(x, "ctx", pairs)
@@ -381,10 +462,14 @@
     repacked, state = call(
         with_width(chain_kernel),
         "chain",
-        [packet, pltpu.VMEM((pack, LANES), BF16)],
+        [packet, pltpu.VMEM((pack + EDGE, LANES), BF16)],
         got_01,
+        arrived,
+        taps,
+        table,
         end,
         jump,
+        rest,
         packed,
     )
     got_13 = passed(state, 1, 3)
@@ -398,9 +483,13 @@
         got_23,
         got_12,
         got_13,
+        arrived,
+        taps,
         table,
         step,
         jump,
+        rest,
+        scalars=(place,),
     )
     hidden, sums = call(
         hidden_kernel,

time: 69 us -> 66.5 us (0.964)
  waiting for transfers between devices: 39.7 us -> 33.1 us
  Pallas kernels: 5.83 us -> 9.44 us
  starting transfers between devices: 19.2 us -> 22.6 us
  local copies, waits for them, and re-layouts: 3.27 us -> 0.13 us
    all_to_all x2, waiting for transfers between devices: 16 us -> 9.54 us  [exchange(): lax.all_to_all(x.reshape(slab), 'ctx', 0, 0, axis_index_groups=neighbours)]
    all_to_all x2, starting transfers between devices: 7.16 us -> 10.1 us  [exchange(): lax.all_to_all(x.reshape(slab), 'ctx', 0, 0, axis_index_groups=neighbours)]
    unnamed x18 -> x14, local copies, waits for them, and re-layouts: 2.52 us -> 0.13 us
    pallas_call x0 -> x1, Pallas kernels: none -> 1.81 us  [on_device(): pl.pallas_call(pack_kernel, grid=(1,), in_specs=[pl.BlockSpec((rows, chan...]
    pallas_call x10 -> x8, Pallas kernels: 5.83 us -> 7.63 us  [call(): pl.pallas_call(kernel, in_specs=[smem] * len(scalars) + [vmem] * len(arra...]
    slice x6 -> x0, local copies, waits for them, and re-layouts: 0.75 us -> none  [on_device(): a[rows - HALO:]]
  transfers between devices with their start and end apart: 8 -> 8, of which waited for: 6 -> 6; matrix products, arithmetic and copies ran while one was open for 0% -> 1% of each run, Pallas kernels for 3% -> 4%
where the time goes in v4:
time: 66.5 us; the launch traced here: 66 us
  waiting for transfers between devices  33.1 us (50%)
  starting transfers between devices  22.6 us (34%)
  Pallas kernels  9.44 us (14%)
    ppermute x4, waiting for transfers between devices, passed(): return lax.ppermute(x, 'ctx', pairs)  14.5 us
    all_to_all x2, starting transfers between devices, exchange(): lax.all_to_all(x.reshape(slab), 'ctx', 0, 0, axis_index_groups=neighbours)  10.1 us
    all_to_all x2, waiting for transfers between devices, exchange(): lax.all_to_all(x.reshape(slab), 'ctx', 0, 0, axis_index_groups=neighbours)  9.54 us
    pallas_call x8, Pallas kernels, call(): pl.pallas_call(kernel, in_specs=[smem] * len(scalars) + [vmem] * len(arra...  7.63 us
    all_to_all x1, waiting for transfers between devices, on_device(): all_sums = lax.all_to_all(sums.reshape(parts, 8, LANES), 'tp', 0, 0)  5.43 us
    all_to_all x1, starting transfers between devices, on_device(): all_sums = lax.all_to_all(sums.reshape(parts, 8, LANES), 'tp', 0, 0)  4.61 us
    ppermute x1, starting transfers between devices, on_device(): lax.ppermute(outer_tail, 'ctx', [(i, i + 1) for i in range(size - 1)])  3.96 us
    ppermute x4, starting transfers between devices, passed(): return lax.ppermute(x, 'ctx', pairs)  3.91 us
  transfers between devices with their start and end apart: 8, of which 6 were waited for; matrix products, arithmetic and copies ran while one was open for 1% of the time, Pallas kernels for 4%

profile of v4, /device:TPU:384, one launch (start us, length us, event | category | flops | bytes accessed | tf_op | source)
XLA Modules:
  0.0 66.0 jit_solution(16997707149524535076)
XLA Ops:
  0.0 1.8 %pack.1 = (bf16[1024,128]{1,0:T(8,128)(2,1)}, bf16[8,1024]{1,0:T(8,128)(2,1)S(1)}) custom-call(bf16[64,1024]{1,0:T(8,128)(2,1)} %inner_ref.1, bf16[64,1024]{1,0:T(8,128)(2,1)} %value_ref.1, bf16[64,1024]{1,0:T(8,128)(2,1)} %outer_ref.3), custom_call_target="tpu_custom_call" | custom-call | tf_op jit(solution)/shard_map/pack/pallas_call | solution.py:381
  1.8 5.9 %all-to-all-start = ((bf16[16,64,128]{2,1,0:T(8,128)(2,1)}), bf16[16,64,128]{2,1,0:T(8,128)(2,1)S(1)}, u32[]{:S(2)}, u32[]{:S(2)}) async-start(bf16[16,64,128]{2,1,0:T(8,128)(2,1)} %bitcast.2), calls=%async_computation | async-start | bytes 524288 | tf_op jit(solution)/shard_map/all_to_all | solution.py:397
  7.7 4.0 %collective-permute-start = (bf16[8,1024]{1,0:T(8,128)(2,1)S(1)}, bf16[8,1024]{1,0:T(8,128)(2,1)S(1)}, u32[]{:S(2)}, u32[]{:S(2)}) collective-permute-start(bf16[8,1024]{1,0:T(8,128)(2,1)S(1)} %get-tuple-element.23), channel_id=1, source_target_pairs={{0,8},{8,16},{16,24},{24,32},{32,40},{40,48},{48,56},{56,64},{64,7... | collective-permute-start | bytes 49160 | tf_op jit(solution)/shard_map/ppermute | solution.py:401
  11.7 0.6 pad_add_fusion.place
  12.4 1.6 %tables.1 = (bf16[4,7,128,128]{3,2,1,0:T(8,128)(2,1)S(1)}, f32[32,128]{1,0:T(8,128)S(1)}, f32[32,128]{1,0:T(8,128)S(1)}, f32[32,128]{1,0:T(8,128)S(1)}, f32[7,128]{1,0:T(8,128)S(1)}) custom-call(s32[2]{0:T(128)} %pad_add_fusion.place, f32[16,64]{1,0:T(8,128)S(1)} %bitcast.17, f32[16,64]{1,0:T(8,128)S(1)} %bitcast.18, bf16[64,128]{1,0:T(8,128)(2,1)S(1)} %bitcast.16, ...), custom_call_target="tpu_custom_call" | custom-call | tf_op jit(solution)/shard_map/tables/pallas_call | solution.py:364
  14.0 3.6 %collective-permute-done.halo_ref = bf16[8,1024]{1,0:T(8,128)(2,1)S(1)} collective-permute-done((bf16[8,1024]{1,0:T(8,128)(2,1)S(1)}, bf16[8,1024]{1,0:T(8,128)(2,1)S(1)}, u32[]{:S(2)}, u32[]{:S(2)}) %collective-permute-start) | collective-permute-done | bytes 16416 | tf_op jit(solution)/shard_map/ppermute | solution.py:401
  17.6 0.8 %all-to-all-done = bf16[16,64,128]{2,1,0:T(8,128)(2,1)S(1)} async-done(((bf16[16,64,128]{2,1,0:T(8,128)(2,1)}), bf16[16,64,128]{2,1,0:T(8,128)(2,1)S(1)}, u32[]{:S(2)}, u32[]{:S(2)}) %all-to-all-start) | async-done | bytes 262176 | tf_op jit(solution)/shard_map/all_to_all | solution.py:397
  18.4 1.5 %states.1 = (bf16[512,128]{1,0:T(8,128)(2,1)S(1)}, f32[512,128]{1,0:T(8,128)S(1)}, f32[32,128]{1,0:T(8,128)S(1)}, bf16[128,128]{1,0:T(8,128)(2,1)S(1)}) custom-call(s32[2]{0:T(128)} %pad_add_fusion.place, bf16[1024,128]{1,0:T(8,128)(2,1)S(1)} %bitcast.11, f32[7,128]{1,0:T(8,128)S(1)} %get-tuple-element.25.tap_ref, ...), custom_call_target="tpu_custom_call" | custom-call | tf_op jit(solution)/shard_map/states/pallas_call | solution.py:364
  19.9 0.7 %collective-permute-start.1 = (bf16[128,128]{1,0:T(8,128)(2,1)S(1)}, bf16[128,128]{1,0:T(8,128)(2,1)S(1)}, u32[]{:S(2)}, u32[]{:S(2)}) collective-permute-start(bf16[128,128]{1,0:T(8,128)(2,1)S(1)} %get-tuple-element.30.send_ref), channel_id=1, source_target_pairs={{0,128},{8,136},{16,144},{24,152},{32,160},{40,168},{48,176},{56,1... | collective-permute-start | bytes 98312 | tf_op jit(solution)/shard_map/ppermute | solution.py:458
  20.6 1.3 %collective-permute-start.2 = (bf16[128,128]{1,0:T(8,128)(2,1)S(1)}, bf16[128,128]{1,0:T(8,128)(2,1)S(1)}, u32[]{:S(2)}, u32[]{:S(2)}) collective-permute-start(bf16[128,128]{1,0:T(8,128)(2,1)S(1)} %get-tuple-element.30.send_ref), channel_id=1, source_target_pairs={{256,384},{264,392},{272,400},{280,408},{288,416},{296,424},{304,4... | collective-permute-start | bytes 98312 | tf_op jit(solution)/shard_map/ppermute | solution.py:458
  21.9 0.4 chain.1
  22.3 0.7 %collective-permute-start.3 = (bf16[128,128]{1,0:T(8,128)(2,1)S(1)}, bf16[128,128]{1,0:T(8,128)(2,1)S(1)}, u32[]{:S(2)}, u32[]{:S(2)}) collective-permute-start(bf16[128,128]{1,0:T(8,128)(2,1)S(1)} %get-tuple-element.34), channel_id=1, source_target_pairs={{128,256},{136,264},{144,272},{152,280},{160,288},{168,296},{176,3... | collective-permute-start | bytes 98312 | tf_op jit(solution)/shard_map/ppermute | solution.py:458
  22.9 1.3 %collective-permute-start.4 = (bf16[48,128]{1,0:T(8,128)(2,1)S(1)}, bf16[48,128]{1,0:T(8,128)(2,1)S(1)}, u32[]{:S(2)}, u32[]{:S(2)}) collective-permute-start(bf16[48,128]{1,0:T(8,128)(2,1)S(1)} %get-tuple-element.35), channel_id=1, source_target_pairs={{128,384},{136,392},{144,400},{152,408},{160,416},{168,424},{176,4... | collective-permute-start | bytes 36872 | tf_op jit(solution)/shard_map/ppermute | solution.py:458
  24.2 0.3 local.1.local_ref
  24.6 5.7 %collective-permute-done.2.got_23 = bf16[128,128]{1,0:T(8,128)(2,1)S(1)} collective-permute-done((bf16[128,128]{1,0:T(8,128)(2,1)S(1)}, bf16[128,128]{1,0:T(8,128)(2,1)S(1)}, u32[]{:S(2)}, u32[]{:S(2)}) %collective-permute-start.2) | collective-permute-done | bytes 32800 | tf_op jit(solution)/shard_map/ppermute | solution.py:458
  30.3 8.8 %collective-permute-done.4.got_13 = bf16[48,128]{1,0:T(8,128)(2,1)S(1)} collective-permute-done((bf16[48,128]{1,0:T(8,128)(2,1)S(1)}, bf16[48,128]{1,0:T(8,128)(2,1)S(1)}, u32[]{:S(2)}, u32[]{:S(2)}) %collective-permute-start.4) | collective-permute-done | bytes 12320 | tf_op jit(solution)/shard_map/ppermute | solution.py:458
  39.0 2.0 %finish.1 = bf16[512,128]{1,0:T(8,128)(2,1)} custom-call(s32[2]{0:T(128)} %pad_add_fusion.place, f32[512,128]{1,0:T(8,128)S(1)} %local.1.local_ref, bf16[128,128]{1,0:T(8,128)(2,1)S(1)} %collective-permute-done.1.got_ref.got_01, bf16[128,128]{1,0:T(8,128)(2,1)S(1)} %collective-permute-done.2.got_23, bf16[128,128]{1,0:T(8,128)(2,1)S(1)} %collective-permute-done.3.got_12, ...), custom_call_target="tpu_custom_call" | custom-call | tf_op jit(solution)/shard_map/finish/pallas_call | solution.py:364
  41.0 4.2 %all-to-all-start.1 = ((bf16[16,32,128]{2,1,0:T(8,128)(2,1)}), bf16[16,32,128]{2,1,0:T(8,128)(2,1)S(1)}, u32[]{:S(2)}, u32[]{:S(2)}) async-start(bf16[16,32,128]{2,1,0:T(8,128)(2,1)} %bitcast.7), calls=%async_computation.1 | async-start | bytes 262144 | tf_op jit(solution)/shard_map/all_to_all | solution.py:397
  45.3 0.2 outer.1.outer_ref
  45.4 8.7 %all-to-all-done.1 = bf16[16,32,128]{2,1,0:T(8,128)(2,1)S(1)} async-done(((bf16[16,32,128]{2,1,0:T(8,128)(2,1)}), bf16[16,32,128]{2,1,0:T(8,128)(2,1)S(1)}, u32[]{:S(2)}, u32[]{:S(2)}) %all-to-all-start.1) | async-done | bytes 131104 | tf_op jit(solution)/shard_map/all_to_all | solution.py:397
  54.2 1.0 %hidden.1 = (f32[64,1024]{1,0:T(8,128)S(1)}, f32[64,128]{1,0:T(8,128)}) custom-call(bf16[512,128]{1,0:T(8,128)(2,1)S(1)} %bitcast.14, f32[64,1024]{1,0:T(8,128)S(1)} %outer.1.outer_ref, bf16[64,1024]{1,0:T(8,128)(2,1)S(1)} %copy-done.2), custom_call_target="tpu_custom_call" | custom-call | tf_op jit(solution)/shard_map/hidden/pallas_call | solution.py:364
  55.1 4.6 %all-to-all-start.2 = ((f32[8,8,128]{2,1,0:T(8,128)}), f32[8,8,128]{2,1,0:T(8,128)S(1)}, u32[]{:S(2)}, u32[]{:S(2)}) async-start(f32[8,8,128]{2,1,0:T(8,128)} %bitcast.9), calls=%async_computation.2 | async-start | bytes 65536 | tf_op jit(solution)/shard_map/all_to_all | solution.py:502
  59.8 5.4 %all-to-all-done.2 = f32[8,8,128]{2,1,0:T(8,128)S(1)} async-done(((f32[8,8,128]{2,1,0:T(8,128)}), f32[8,8,128]{2,1,0:T(8,128)S(1)}, u32[]{:S(2)}, u32[]{:S(2)}) %all-to-all-start.2) | async-done | bytes 32800 | tf_op jit(solution)/shard_map/all_to_all | solution.py:502
  65.2 0.8 %norm.1 = bf16[64,1024]{1,0:T(8,128)(2,1)} custom-call(f32[64,1024]{1,0:T(8,128)S(1)} %get-tuple-element.37.hidden_ref, f32[64,128]{1,0:T(8,128)S(1)} %bitcast.15, bf16[1,1024]{1,0:T(2,128)(2,1)S(1)} %reshape.27.gain_ref), custom_call_target="tpu_custom_call" | custom-call | tf_op jit(solution)/shard_map/norm/pallas_call | solution.py:364
  (17 shorter events, 0.1 us)
Async XLA Ops:
  1.8 10.5 %copy-start.3 = (bf16[128,64]{0,1:T(8,128)(2,1)S(1)}, bf16[128,64]{0,1:T(8,128)(2,1)}, u32[]{:S(2)}) copy-start(bf16[128,64]{0,1:T(8,128)(2,1)} %param.13) | copy-start | bytes 49156
  1.8 10.5 %copy-start.5 = (f32[64,16]{0,1:T(8,128)S(1)}, f32[64,16]{0,1:T(8,128)}, u32[]{:S(2)}) copy-start(f32[64,16]{0,1:T(8,128)} %param.15) | copy-start | bytes 12292
  1.8 16.6 %all-to-all-start = ((bf16[16,64,128]{2,1,0:T(8,128)(2,1)}), bf16[16,64,128]{2,1,0:T(8,128)(2,1)S(1)}, u32[]{:S(2)}, u32[]{:S(2)}) async-start(bf16[16,64,128]{2,1,0:T(8,128)(2,1)} %bitcast.2), calls=%async_computation | async-start | bytes 524288 | tf_op jit(solution)/shard_map/all_to_all | solution.py:397
  7.7 4.6 %copy-start.1 = (bf16[3,7,1024]{2,1,0:T(8,128)(2,1)S(1)}, bf16[3,7,1024]{2,1,0:T(8,128)(2,1)}, u32[]{:S(2)}) copy-start(bf16[3,7,1024]{2,1,0:T(8,128)(2,1)} %tap_ref.3) | copy-start | bytes 129028
  7.7 9.9 %collective-permute-start = (bf16[8,1024]{1,0:T(8,128)(2,1)S(1)}, bf16[8,1024]{1,0:T(8,128)(2,1)S(1)}, u32[]{:S(2)}, u32[]{:S(2)}) collective-permute-start(bf16[8,1024]{1,0:T(8,128)(2,1)S(1)} %get-tuple-element.23), channel_id=1, source_target_pairs={{0,8},{8,16},{16,24},{24,32},{32,40},{40,48},{48,56},{56,64},{64,7... | collective-permute-start | bytes 49160 | tf_op jit(solution)/shard_map/ppermute | solution.py:401
  11.7 0.7 %copy-start.4 = (f32[64,16]{0,1:T(8,128)S(1)}, f32[64,16]{0,1:T(8,128)}, u32[]{:S(2)}) copy-start(f32[64,16]{0,1:T(8,128)} %param.14) | copy-start | bytes 12292
  19.9 2.0 %collective-permute-start.1 = (bf16[128,128]{1,0:T(8,128)(2,1)S(1)}, bf16[128,128]{1,0:T(8,128)(2,1)S(1)}, u32[]{:S(2)}, u32[]{:S(2)}) collective-permute-start(bf16[128,128]{1,0:T(8,128)(2,1)S(1)} %get-tuple-element.30.send_ref), channel_id=1, source_target_pairs={{0,128},{8,136},{16,144},{24,152},{32,160},{40,168},{48,176},{56,1... | collective-permute-start | bytes 98312 | tf_op jit(solution)/shard_map/ppermute | solution.py:458
  20.6 9.7 %collective-permute-start.2 = (bf16[128,128]{1,0:T(8,128)(2,1)S(1)}, bf16[128,128]{1,0:T(8,128)(2,1)S(1)}, u32[]{:S(2)}, u32[]{:S(2)}) collective-permute-start(bf16[128,128]{1,0:T(8,128)(2,1)S(1)} %get-tuple-element.30.send_ref), channel_id=1, source_target_pairs={{256,384},{264,392},{272,400},{280,408},{288,416},{296,424},{304,4... | collective-permute-start | bytes 98312 | tf_op jit(solution)/shard_map/ppermute | solution.py:458
  22.3 16.8 %collective-permute-start.3 = (bf16[128,128]{1,0:T(8,128)(2,1)S(1)}, bf16[128,128]{1,0:T(8,128)(2,1)S(1)}, u32[]{:S(2)}, u32[]{:S(2)}) collective-permute-start(bf16[128,128]{1,0:T(8,128)(2,1)S(1)} %get-tuple-element.34), channel_id=1, source_target_pairs={{128,256},{136,264},{144,272},{152,280},{160,288},{168,296},{176,3... | collective-permute-start | bytes 98312 | tf_op jit(solution)/shard_map/ppermute | solution.py:458
  22.9 16.1 %collective-permute-start.4 = (bf16[48,128]{1,0:T(8,128)(2,1)S(1)}, bf16[48,128]{1,0:T(8,128)(2,1)S(1)}, u32[]{:S(2)}, u32[]{:S(2)}) collective-permute-start(bf16[48,128]{1,0:T(8,128)(2,1)S(1)} %get-tuple-element.35), channel_id=1, source_target_pairs={{128,384},{136,392},{144,400},{152,408},{160,416},{168,424},{176,4... | collective-permute-start | bytes 36872 | tf_op jit(solution)/shard_map/ppermute | solution.py:458
  41.0 4.2 %copy-start = (bf16[64,1024]{1,0:T(8,128)(2,1)S(1)}, bf16[64,1024]{1,0:T(8,128)(2,1)}, u32[]{:S(2)}) copy-start(bf16[64,1024]{1,0:T(8,128)(2,1)} %outer_ref.3) | copy-start | bytes 393220
  41.0 13.1 %all-to-all-start.1 = ((bf16[16,32,128]{2,1,0:T(8,128)(2,1)}), bf16[16,32,128]{2,1,0:T(8,128)(2,1)S(1)}, u32[]{:S(2)}, u32[]{:S(2)}) async-start(bf16[16,32,128]{2,1,0:T(8,128)(2,1)} %bitcast.7), calls=%async_computation.1 | async-start | bytes 262144 | tf_op jit(solution)/shard_map/all_to_all | solution.py:397
  45.2 8.9 %copy-start.2 = (bf16[64,1024]{1,0:T(8,128)(2,1)S(1)}, bf16[64,1024]{1,0:T(8,128)(2,1)}, u32[]{:S(2)}) copy-start(bf16[64,1024]{1,0:T(8,128)(2,1)} %residual_ref.1) | copy-start | bytes 393220
  55.1 4.6 %copy-start.6 = (bf16[1024]{0:T(1024)(128)(2,1)S(1)}, bf16[1024]{0:T(1024)(128)(2,1)}, u32[]{:S(2)}) copy-start(bf16[1024]{0:T(1024)(128)(2,1)} %param.17) | copy-start | bytes 6148
  55.1 10.1 %all-to-all-start.2 = ((f32[8,8,128]{2,1,0:T(8,128)}), f32[8,8,128]{2,1,0:T(8,128)S(1)}, u32[]{:S(2)}, u32[]{:S(2)}) async-start(f32[8,8,128]{2,1,0:T(8,128)} %bitcast.9), calls=%async_computation.2 | async-start | bytes 65536 | tf_op jit(solution)/shard_map/all_to_all | solution.py:502

commit v5 on v4

--- a/solution.py
+++ b/solution.py
@@ -6,6 +6,7 @@
 from jax.experimental import pallas as pl
 from jax.experimental.pallas import tpu as pltpu
 from jax.sharding import PartitionSpec as P
+
 
 D = 8192
 F32 = jnp.float32
@@ -35,7 +36,7 @@
 
 
 def split_three(x, width):
-    high, rest = split(x)
+    high, _ = split(x)
     middle, _ = split(x - high.astype(F32))
     low = x - high.astype(F32) - middle.astype(F32)
     copy = iota(x.shape, 1) // width
@@ -61,7 +62,8 @@
     channels = tap_ref.shape[2]
     half = LANES // 2
     at, to = iota((channels, LANES), 0), iota((channels, LANES), 1)
-    chosen = at == place[0] * half + to % half
+    position = lax.rem(place[0], NEAR)
+    chosen = at == position * half + to % half
     for_inner = jnp.where(chosen & (to < half), 1.0, 0.0).astype(BF16)
     for_value = jnp.where(chosen & (to >= half), 1.0, 0.0).astype(BF16)
     mine_ref[...] = dot(tap_ref[1], for_inner) + dot(tap_ref[2], for_value)
@@ -88,7 +90,7 @@
         return pltpu.roll(wide, 0, 1, stride=1, stride_axis=0)
 
     for q in range(count):
-        group = place[0] * count + q
+        group = position * count + q
         mine = iota((modes, groups), 1) == group
         rate = jnp.sum(jnp.where(mine, decay_ref[...], 0.0), 1, keepdims=True)
         weight = jnp.sum(jnp.where(mine, residue_ref[...], 0.0), 1, keepdims=True)
@@ -187,8 +189,8 @@
     return jnp.concatenate(parts, 0)
 
 
-def states_kernel(
-    width, place, raw_ref, tap_ref, table_ref, step_ref, x_ref, state_ref, end_ref, send_ref, padded
+def find_states(
+    width, later, raw_ref, tap_ref, table_ref, step_ref, x_ref, state_ref, end_ref, send_ref, padded
 ):
     count = table_ref.shape[0]
     block = LANES // 2
@@ -196,14 +198,14 @@
     padded[:HALO] = jnp.zeros((HALO, LANES), F32)
     padded[HALO:] = raw_ref[...].astype(F32)
     low = iota((block, LANES), 1) < block
-    early = (iota((block, LANES), 0) < FEAT - 1) & (place[1] > 0)
+    early = (iota((block, LANES), 0) < FEAT - 1)
     rows = 8 * count
     slabs = []
     for pair in range(blocks // 2):
         products = []
         for b in (2 * pair, 2 * pair + 1):
             product = gated(tap_ref, padded.at[b * block : (b + 1) * block + HALO], block)
-            products.append(jnp.where(early, 0.0, product) if b == 0 else product)
+            products.append(jnp.where(early, 0.0, product) if later and b == 0 else product)
         slabs.append(slabs_of(jnp.where(low, products[0], products[1])))
     wide = jnp.concatenate(slabs, 0)
     x_ref[...] = wide.astype(BF16)
@@ -226,19 +228,49 @@
     send_ref[3 * rows + EDGE :] = raw_ref[:EDGE]
 
 
+def super_block(place):
+    return lax.div(place[0], NEAR)
+
+
+def first_states_kernel(width, place, *refs):
+    @pl.when(super_block(place) == 0)
+    def _():
+        find_states(width, False, *refs)
+
+
+def later_states_kernel(width, place, raw_ref, tap_ref, table_ref, step_ref, x_in, state_in, *refs):
+    @pl.when(super_block(place) > 0)
+    def _():
+        find_states(width, True, raw_ref, tap_ref, table_ref, step_ref, *refs)
+
+
 def chain_kernel(
-    width, got_ref, raw_ref, tap_ref, table_ref, end_ref, jump_ref, rest_ref, send_ref, next_ref, short_ref
+    width,
+    place,
+    got_ref,
+    raw_ref,
+    tap_ref,
+    table_ref,
+    end_ref,
+    jump_ref,
+    rest_ref,
+    send_ref,
+    short_ref,
+    next_ref,
 ):
     rows = end_ref.shape[0]
-    tail = got_ref[3 * rows : 3 * rows + EDGE].astype(F32)
-    slab = missing(tap_ref, tail, raw_ref[:EDGE].astype(F32))
-    end = end_ref[...] + rest_ref[...] * to_states(table_ref, slab)
-    end = end + jump_ref[...] * join_three(got_ref[:rows], width)
-    state = split_three(end, width)
-    short_ref[:rows] = state
-    short_ref[rows:] = send_ref[3 * rows : 3 * rows + EDGE]
-    next_ref[:rows] = state
-    next_ref[rows:] = send_ref[rows:]
+
+    @pl.when(super_block(place) == 1)
+    def _():
+        tail = got_ref[3 * rows : 3 * rows + EDGE].astype(F32)
+        slab = missing(tap_ref, tail, raw_ref[:EDGE].astype(F32))
+        end = end_ref[...] + rest_ref[...] * to_states(table_ref, slab)
+        end = end + jump_ref[...] * join_three(got_ref[:rows], width)
+        state = split_three(end, width)
+        short_ref[:rows] = state
+        short_ref[rows:] = send_ref[3 * rows : 3 * rows + EDGE]
+        next_ref[:rows] = state
+        next_ref[rows:] = send_ref[rows:]
 
 
 def local_kernel(width, x_ref, table_ref, state_ref, out_ref):
@@ -274,42 +306,56 @@
     jump_ref,
     rest_ref,
     out_ref,
+    incoming_ref,
 ):
-    count = table_ref.shape[0]
-    rows = 8 * count
-    blocks = local_ref.shape[0] // rows
-    got = got_01[...].astype(F32) + got_23[...].astype(F32) + got_12[...].astype(F32)
-    edge = slice(3 * rows, 3 * rows + EDGE)
-    far_tail = got_13[rows:].astype(F32)
-    far_slab = missing(tap_ref, far_tail, got_23[3 * rows + EDGE :].astype(F32))
-    own_slab = missing(tap_ref, got[edge], raw_ref[:EDGE].astype(F32))
-    own_slab = jnp.where(place[1] > 0, own_slab, 0.0)
-    incoming = join_three(got[:rows], width) + rest_ref[...] * to_states(table_ref, far_slab)
-    incoming = incoming + jump_ref[...] * join_three(got_13[:rows], width)
-    added = to_states(table_ref, own_slab)
-    zeros = jnp.zeros((8, LANES), F32)
-    parts = []
-    for q in range(count):
-        at = slice(8 * q, 8 * q + 8)
-        step = step_ref[at]
-        state = incoming[at]
-        states = []
-        for block in range(blocks):
-            states.append(state)
-            state = state * step
-            if block == 0:
-                state = state + added[at]
-        mixed = dot(two_parts(jnp.concatenate(states, 0), width), table_ref[q, 6])
-        last_but_one, last, first = got[rows:][at], got[2 * rows :][at], own_slab[at]
-        now = jnp.concatenate([first, zeros, zeros, zeros], 0).astype(BF16)
-        before = jnp.concatenate([last, first, zeros, zeros], 0).astype(BF16)
-        earlier = jnp.concatenate([last_but_one, last, first, zeros], 0).astype(BF16)
-        start = dot(now, table_ref[q, 0]) + dot(now, table_ref[q, 1])
-        start = start + dot(before, table_ref[q, 2]) + dot(earlier, table_ref[q, 3])
-        mixed = jnp.concatenate([mixed[:32] + start, mixed[32:]], 0)
-        parts.append(mixed.reshape(blocks, 8, LANES))
-    total = local_ref[...] + jnp.concatenate(parts, 1).reshape(local_ref.shape)
-    out_ref[...] = total.astype(BF16)
+    here = super_block(place)
+
+    @pl.when(here == 0)
+    def _():
+        out_ref[...] = local_ref[...].astype(BF16)
+
+    @pl.when(here > 0)
+    def _():
+        count = table_ref.shape[0]
+        rows = 8 * count
+        blocks = local_ref.shape[0] // rows
+        got = got_01[...].astype(F32) + got_23[...].astype(F32) + got_12[...].astype(F32)
+        edge = slice(3 * rows, 3 * rows + EDGE)
+        own_slab = missing(tap_ref, got[edge], raw_ref[:EDGE].astype(F32))
+        incoming_ref[...] = join_three(got[:rows], width)
+
+        @pl.when(here == 3)
+        def _():
+            far_tail = got_13[rows:].astype(F32)
+            far_slab = missing(tap_ref, far_tail, got_23[3 * rows + EDGE :].astype(F32))
+            more = rest_ref[...] * to_states(table_ref, far_slab)
+            incoming_ref[...] += more + jump_ref[...] * join_three(got_13[:rows], width)
+
+        incoming = incoming_ref[...]
+        added = to_states(table_ref, own_slab)
+        zeros = jnp.zeros((8, LANES), F32)
+        parts = []
+        for q in range(count):
+            at = slice(8 * q, 8 * q + 8)
+            step = step_ref[at]
+            state = incoming[at]
+            states = []
+            for block in range(blocks):
+                states.append(state)
+                state = state * step
+                if block == 0:
+                    state = state + added[at]
+            mixed = dot(two_parts(jnp.concatenate(states, 0), width), table_ref[q, 6])
+            last_but_one, last, first = got[rows:][at], got[2 * rows :][at], own_slab[at]
+            now = jnp.concatenate([first, zeros, zeros, zeros], 0).astype(BF16)
+            before = jnp.concatenate([last, first, zeros, zeros], 0).astype(BF16)
+            earlier = jnp.concatenate([last_but_one, last, first, zeros], 0).astype(BF16)
+            start = dot(now, table_ref[q, 0]) + dot(now, table_ref[q, 1])
+            start = start + dot(before, table_ref[q, 2]) + dot(earlier, table_ref[q, 3])
+            mixed = jnp.concatenate([mixed[:32] + start, mixed[32:]], 0)
+            parts.append(mixed.reshape(blocks, 8, LANES))
+        total = local_ref[...] + jnp.concatenate(parts, 1).reshape(local_ref.shape)
+        out_ref[...] = total.astype(BF16)
 
 
 def hidden_kernel(mixed_ref, outer_ref, residual_ref, hidden_ref, sum_ref):
@@ -360,14 +406,14 @@
     vmem = pl.BlockSpec(memory_space=pltpu.VMEM)
     smem = pl.BlockSpec(memory_space=pltpu.SMEM)
 
-    def call(kernel, name, out, *arrays, scalars=(), scratch=()):
+    def call(kernel, out, *arrays, scalars=(), scratch=(), aliases={}):
         return pl.pallas_call(
             kernel,
             in_specs=[smem] * len(scalars) + [vmem] * len(arrays),
             out_specs=jax.tree.map(lambda _: vmem, out),
             out_shape=out,
             scratch_shapes=scratch,
-            name=name,
+            input_output_aliases=aliases,
         )(*scalars, *in_vmem(*arrays))
 
     slab_rows = rows * channels // LANES
@@ -400,11 +446,9 @@
     arrived = exchange(raw)
     halo = lax.ppermute(outer_tail, "ctx", [(i, i + 1) for i in range(size - 1)])
     arrived, halo = lax.optimization_barrier((arrived, halo))
-    index = lax.axis_index("ctx")
-    place = jnp.stack([index % NEAR, index // NEAR]).astype(jnp.int32)
+    place = lax.axis_index("ctx").reshape(1).astype(jnp.int32)
     table, step, jump, rest, taps = call(
         tables_kernel,
-        "tables",
         [
             pltpu.VMEM((count, 7, LANES, LANES), BF16),
             pltpu.VMEM((pack, LANES), F32),
@@ -420,7 +464,6 @@
     )
     outer_feat = call(
         outer_kernel,
-        "outer",
         pltpu.VMEM((rows, channels), F32),
         halo,
         outer_input,
@@ -428,41 +471,38 @@
         scratch=[pltpu.VMEM((tiles, HALO + rows, LANES), F32)],
     )
     packet = pltpu.VMEM((3 * pack + 2 * EDGE, LANES), BF16)
+    found = [
+        pltpu.VMEM((slab_rows, LANES), BF16),
+        pltpu.VMEM((slab_rows, LANES), F32),
+        pltpu.VMEM((pack, LANES), F32),
+        packet,
+    ]
+    padded = [pltpu.VMEM((HALO + NEAR * rows, LANES), F32)]
+    known = (arrived, taps, table, step)
+    x, states, _, first_packed = call(
+        with_width(first_states_kernel), found, *known, scalars=(place,), scratch=padded
+    )
     x, states, end, packed = call(
-        with_width(states_kernel),
-        "states",
-        [
-            pltpu.VMEM((slab_rows, LANES), BF16),
-            pltpu.VMEM((slab_rows, LANES), F32),
-            pltpu.VMEM((pack, LANES), F32),
-            packet,
-        ],
-        arrived,
-        taps,
-        table,
-        step,
+        with_width(later_states_kernel),
+        found,
+        *known,
+        x,
+        states,
         scalars=(place,),
-        scratch=[pltpu.VMEM((HALO + NEAR * rows, LANES), F32)],
-    )
-    local = call(
-        with_width(local_kernel),
-        "local",
-        pltpu.VMEM((slab_rows, LANES), F32),
-        x,
-        table,
-        states,
-    )
+        scratch=padded,
+        aliases={5: 0, 6: 1},
+    )
+    local = call(with_width(local_kernel), pltpu.VMEM((slab_rows, LANES), F32), x, table, states)
 
     def passed(x, start, end):
         pairs = [(NEAR * start + n, NEAR * end + n) for n in range(NEAR)]
         return lax.ppermute(x, "ctx", pairs)
 
-    got_01 = passed(packed, 0, 1)
+    got_01 = passed(first_packed, 0, 1)
     got_23 = passed(packed, 2, 3)
-    repacked, state = call(
+    state, repacked = call(
         with_width(chain_kernel),
-        "chain",
-        [packet, pltpu.VMEM((pack + EDGE, LANES), BF16)],
+        [pltpu.VMEM((pack + EDGE, LANES), BF16), packet],
         got_01,
         arrived,
         taps,
@@ -471,12 +511,12 @@
         jump,
         rest,
         packed,
+        scalars=(place,),
     )
     got_13 = passed(state, 1, 3)
     got_12 = passed(repacked, 1, 2)
     mixed = call(
         with_width(finish_kernel),
-        "finish",
         pltpu.VMEM((slab_rows, LANES), BF16),
         local,
         got_01,
@@ -490,10 +530,10 @@
         jump,
         rest,
         scalars=(place,),
+        scratch=[pltpu.VMEM((pack, LANES), F32)],
     )
     hidden, sums = call(
         hidden_kernel,
-        "hidden",
         [pltpu.VMEM((rows, channels), F32), pltpu.VMEM((8 * parts, LANES), F32)],
         exchange(mixed),
         outer_feat,
@@ -502,7 +542,6 @@
     all_sums = lax.all_to_all(sums.reshape(parts, 8, LANES), "tp", 0, 0)
     return call(
         norm_kernel,
-        "norm",
         jax.ShapeDtypeStruct((rows, channels), BF16),
         hidden,
         all_sums.reshape(8 * parts, LANES),

time: 66.5 us -> 65.7 us (0.988)
  Pallas kernels: 9.44 us -> 8.04 us
  waiting for transfers between devices: 33.1 us -> 34.5 us
    pallas_call x8 -> x9, Pallas kernels: 7.63 us -> 6.23 us  [call(): pl.pallas_call(kernel, in_specs=[smem] * len(scalars) + [vmem] * len(arra...]
    ppermute x1, waiting for transfers between devices: 3.63 us -> 4.96 us  [on_device(): lax.ppermute(outer_tail, 'ctx', [(i, i + 1) for i in range(size - 1)])]
  transfers between devices with their start and end apart: 8 -> 8, of which waited for: 6 -> 6; matrix products, arithmetic and copies ran while one was open for 1% -> 0% of each run, Pallas kernels for 4% -> 3%
where the time goes in v5:
time: 65.7 us; the launch traced here: 65.2 us
  waiting for transfers between devices  34.5 us (53%)
  starting transfers between devices  22.4 us (34%)
  Pallas kernels  8.04 us (12%)
    ppermute x4, waiting for transfers between devices, passed(): return lax.ppermute(x, 'ctx', pairs)  14.5 us
    all_to_all x2, starting transfers between devices, exchange(): lax.all_to_all(x.reshape(slab), 'ctx', 0, 0, axis_index_groups=neighbours)  10.1 us
    all_to_all x2, waiting for transfers between devices, exchange(): lax.all_to_all(x.reshape(slab), 'ctx', 0, 0, axis_index_groups=neighbours)  9.67 us
    pallas_call x9, Pallas kernels, call(): pl.pallas_call(kernel, in_specs=[smem] * len(scalars) + [vmem] * len(arra...  6.23 us
    all_to_all x1, waiting for transfers between devices, on_device(): all_sums = lax.all_to_all(sums.reshape(parts, 8, LANES), 'tp', 0, 0)  5.43 us
    ppermute x1, waiting for transfers between devices, on_device(): lax.ppermute(outer_tail, 'ctx', [(i, i + 1) for i in range(size - 1)])  4.96 us
    all_to_all x1, starting transfers between devices, on_device(): all_sums = lax.all_to_all(sums.reshape(parts, 8, LANES), 'tp', 0, 0)  4.6 us
    ppermute x4, starting transfers between devices, passed(): return lax.ppermute(x, 'ctx', pairs)  3.9 us
  transfers between devices with their start and end apart: 8, of which 6 were waited for; matrix products, arithmetic and copies ran while one was open for 0% of the time, Pallas kernels for 3%

profile of v5, /device:TPU:384, one launch (start us, length us, event | category | flops | bytes accessed | tf_op | source)
XLA Modules:
  0.0 65.2 jit_solution(5352112397783199449)
XLA Ops:
  0.0 1.8 %pack.1 = (bf16[1024,128]{1,0:T(8,128)(2,1)}, bf16[8,1024]{1,0:T(8,128)(2,1)S(1)}) custom-call(bf16[64,1024]{1,0:T(8,128)(2,1)} %inner_ref.1, bf16[64,1024]{1,0:T(8,128)(2,1)} %value_ref.1, bf16[64,1024]{1,0:T(8,128)(2,1)} %outer_ref.3), custom_call_target="tpu_custom_call" | custom-call | tf_op jit(solution)/shard_map/pack/pallas_call | solution.py:427
  1.8 5.9 %all-to-all-start = ((bf16[16,64,128]{2,1,0:T(8,128)(2,1)}), bf16[16,64,128]{2,1,0:T(8,128)(2,1)S(1)}, u32[]{:S(2)}, u32[]{:S(2)}) async-start(bf16[16,64,128]{2,1,0:T(8,128)(2,1)} %bitcast.1), calls=%async_computation | async-start | bytes 524288 | tf_op jit(solution)/shard_map/all_to_all | solution.py:443
  7.7 0.0 copy-start.3
  7.7 3.8 %collective-permute-start = (bf16[8,1024]{1,0:T(8,128)(2,1)S(1)}, bf16[8,1024]{1,0:T(8,128)(2,1)S(1)}, u32[]{:S(2)}, u32[]{:S(2)}) collective-permute-start(bf16[8,1024]{1,0:T(8,128)(2,1)S(1)} %get-tuple-element.26), channel_id=1, source_target_pairs={{0,8},{8,16},{16,24},{24,32},{32,40},{40,48},{48,56},{56,64},{64,7... | collective-permute-start | bytes 49160 | tf_op jit(solution)/shard_map/ppermute | solution.py:447
  11.6 0.9 %shard_map.91 = (bf16[4,7,128,128]{3,2,1,0:T(8,128)(2,1)S(1)}, f32[32,128]{1,0:T(8,128)S(1)}, f32[32,128]{1,0:T(8,128)S(1)}, f32[32,128]{1,0:T(8,128)S(1)}, f32[7,128]{1,0:T(8,128)S(1)}) custom-call(s32[1]{0:T(128)} %bitcast.place, f32[16,64]{1,0:T(8,128)S(1)} %bitcast.17, f32[16,64]{1,0:T(8,128)S(1)} %bitcast.18, bf16[64,128]{1,0:T(8,128)(2,1)S(1)} %bitcast.16, ...), custom_call_target="tpu_custom_call" | custom-call | tf_op jit(solution)/shard_map/pallas_call | solution.py:410
  12.5 5.0 %collective-permute-done.halo_ref = bf16[8,1024]{1,0:T(8,128)(2,1)S(1)} collective-permute-done((bf16[8,1024]{1,0:T(8,128)(2,1)S(1)}, bf16[8,1024]{1,0:T(8,128)(2,1)S(1)}, u32[]{:S(2)}, u32[]{:S(2)}) %collective-permute-start) | collective-permute-done | bytes 16416 | tf_op jit(solution)/shard_map/ppermute | solution.py:447
  17.5 0.9 %all-to-all-done = bf16[16,64,128]{2,1,0:T(8,128)(2,1)S(1)} async-done(((bf16[16,64,128]{2,1,0:T(8,128)(2,1)}), bf16[16,64,128]{2,1,0:T(8,128)(2,1)S(1)}, u32[]{:S(2)}, u32[]{:S(2)}) %all-to-all-start) | async-done | bytes 262176 | tf_op jit(solution)/shard_map/all_to_all | solution.py:443
  18.4 0.6 shard_map.92
  19.0 0.7 collective-permute-start.1
  19.7 0.8 %shard_map.93 = (bf16[512,128]{1,0:T(8,128)(2,1)S(1)}, f32[512,128]{1,0:T(8,128)S(1)}, f32[32,128]{1,0:T(8,128)S(1)}, bf16[128,128]{1,0:T(8,128)(2,1)S(1)}) custom-call(s32[1]{0:T(128)} %bitcast.place, bf16[1024,128]{1,0:T(8,128)(2,1)S(1)} %bitcast.11, f32[7,128]{1,0:T(8,128)S(1)} %get-tuple-element.28.refs_1_.tap_ref, ...), custom_call_target="tpu_custom_call", output_to_operand_aliasing={{0}: (5, {}), {1}: (6, {})} | custom-call | tf_op jit(solution)/shard_map/pallas_call | solution.py:410
  20.5 1.3 %collective-permute-start.2 = (bf16[128,128]{1,0:T(8,128)(2,1)S(1)}, bf16[128,128]{1,0:T(8,128)(2,1)S(1)}, u32[]{:S(2)}, u32[]{:S(2)}) collective-permute-start(bf16[128,128]{1,0:T(8,128)(2,1)S(1)} %get-tuple-element.36.send_ref), channel_id=1, source_target_pairs={{256,384},{264,392},{272,400},{280,408},{288,416},{296,424},{304,4... | collective-permute-start | bytes 98312 | tf_op jit(solution)/shard_map/ppermute | solution.py:499
  21.8 0.7 %collective-permute-start.3 = (bf16[128,128]{1,0:T(8,128)(2,1)S(1)}, bf16[128,128]{1,0:T(8,128)(2,1)S(1)}, u32[]{:S(2)}, u32[]{:S(2)}) collective-permute-start(bf16[128,128]{1,0:T(8,128)(2,1)S(1)} %get-tuple-element.40), channel_id=1, source_target_pairs={{128,256},{136,264},{144,272},{152,280},{160,288},{168,296},{176,3... | collective-permute-start | bytes 98312 | tf_op jit(solution)/shard_map/ppermute | solution.py:499
  22.5 1.3 %collective-permute-start.4 = (bf16[48,128]{1,0:T(8,128)(2,1)S(1)}, bf16[48,128]{1,0:T(8,128)(2,1)S(1)}, u32[]{:S(2)}, u32[]{:S(2)}) collective-permute-start(bf16[48,128]{1,0:T(8,128)(2,1)S(1)} %get-tuple-element.41), channel_id=1, source_target_pairs={{128,384},{136,392},{144,400},{152,408},{160,416},{168,424},{176,4... | collective-permute-start | bytes 36872 | tf_op jit(solution)/shard_map/ppermute | solution.py:499
  23.8 0.3 shard_map.94.local_ref
  24.1 6.1 %collective-permute-done.2.got_23 = bf16[128,128]{1,0:T(8,128)(2,1)S(1)} collective-permute-done((bf16[128,128]{1,0:T(8,128)(2,1)S(1)}, bf16[128,128]{1,0:T(8,128)(2,1)S(1)}, u32[]{:S(2)}, u32[]{:S(2)}) %collective-permute-start.2) | collective-permute-done | bytes 32800 | tf_op jit(solution)/shard_map/ppermute | solution.py:499
  30.2 8.4 %collective-permute-done.4.got_13 = bf16[48,128]{1,0:T(8,128)(2,1)S(1)} collective-permute-done((bf16[48,128]{1,0:T(8,128)(2,1)S(1)}, bf16[48,128]{1,0:T(8,128)(2,1)S(1)}, u32[]{:S(2)}, u32[]{:S(2)}) %collective-permute-start.4) | collective-permute-done | bytes 12320 | tf_op jit(solution)/shard_map/ppermute | solution.py:499
  38.6 1.7 %shard_map.96 = bf16[512,128]{1,0:T(8,128)(2,1)} custom-call(s32[1]{0:T(128)} %bitcast.place, f32[512,128]{1,0:T(8,128)S(1)} %shard_map.94.local_ref, bf16[128,128]{1,0:T(8,128)(2,1)S(1)} %collective-permute-done.1.got_ref.got_01, bf16[128,128]{1,0:T(8,128)(2,1)S(1)} %collective-permute-done.2.got_23, bf16[128,128]{1,0:T(8,128)(2,1)S(1)} %collective-permute-done.3.got_12, ...), custom_call_target="tpu_custom_call" | custom-call | tf_op jit(solution)/shard_map/pallas_call | solution.py:410
  40.3 4.2 %all-to-all-start.1 = ((bf16[16,32,128]{2,1,0:T(8,128)(2,1)}), bf16[16,32,128]{2,1,0:T(8,128)(2,1)S(1)}, u32[]{:S(2)}, u32[]{:S(2)}) async-start(bf16[16,32,128]{2,1,0:T(8,128)(2,1)} %bitcast.6), calls=%async_computation.1 | async-start | bytes 262144 | tf_op jit(solution)/shard_map/all_to_all | solution.py:443
  44.5 0.2 shard_map.97.outer_ref
  44.7 8.7 %all-to-all-done.1 = bf16[16,32,128]{2,1,0:T(8,128)(2,1)S(1)} async-done(((bf16[16,32,128]{2,1,0:T(8,128)(2,1)}), bf16[16,32,128]{2,1,0:T(8,128)(2,1)S(1)}, u32[]{:S(2)}, u32[]{:S(2)}) %all-to-all-start.1) | async-done | bytes 131104 | tf_op jit(solution)/shard_map/all_to_all | solution.py:443
  53.4 1.0 %shard_map.98 = (f32[64,1024]{1,0:T(8,128)S(1)}, f32[64,128]{1,0:T(8,128)}) custom-call(bf16[512,128]{1,0:T(8,128)(2,1)S(1)} %bitcast.14, f32[64,1024]{1,0:T(8,128)S(1)} %shard_map.97.outer_ref, bf16[64,1024]{1,0:T(8,128)(2,1)S(1)} %copy-done.2), custom_call_target="tpu_custom_call" | custom-call | tf_op jit(solution)/shard_map/pallas_call | solution.py:410
  54.4 4.6 %all-to-all-start.2 = ((f32[8,8,128]{2,1,0:T(8,128)}), f32[8,8,128]{2,1,0:T(8,128)S(1)}, u32[]{:S(2)}, u32[]{:S(2)}) async-start(f32[8,8,128]{2,1,0:T(8,128)} %bitcast.8), calls=%async_computation.2 | async-start | bytes 65536 | tf_op jit(solution)/shard_map/all_to_all | solution.py:542
  59.0 5.4 %all-to-all-done.2 = f32[8,8,128]{2,1,0:T(8,128)S(1)} async-done(((f32[8,8,128]{2,1,0:T(8,128)}), f32[8,8,128]{2,1,0:T(8,128)S(1)}, u32[]{:S(2)}, u32[]{:S(2)}) %all-to-all-start.2) | async-done | bytes 32800 | tf_op jit(solution)/shard_map/all_to_all | solution.py:542
  64.4 0.8 %shard_map.99 = bf16[64,1024]{1,0:T(8,128)(2,1)} custom-call(f32[64,1024]{1,0:T(8,128)S(1)} %get-tuple-element.43.hidden_ref, f32[64,128]{1,0:T(8,128)S(1)} %bitcast.15, bf16[1,1024]{1,0:T(2,128)(2,1)S(1)} %reshape.31.gain_ref), custom_call_target="tpu_custom_call" | custom-call | tf_op jit(solution)/shard_map/pallas_call | solution.py:410
  (17 shorter events, 0.1 us)
Async XLA Ops:
  1.8 9.8 %copy-start.1 = (bf16[3,7,1024]{2,1,0:T(8,128)(2,1)S(1)}, bf16[3,7,1024]{2,1,0:T(8,128)(2,1)}, u32[]{:S(2)}) copy-start(bf16[3,7,1024]{2,1,0:T(8,128)(2,1)} %tap_ref.3) | copy-start | bytes 129028
  1.8 9.8 %copy-start.4 = (f32[64,16]{0,1:T(8,128)S(1)}, f32[64,16]{0,1:T(8,128)}, u32[]{:S(2)}) copy-start(f32[64,16]{0,1:T(8,128)} %param.14) | copy-start | bytes 12292
  1.8 9.8 %copy-start.5 = (f32[64,16]{0,1:T(8,128)S(1)}, f32[64,16]{0,1:T(8,128)}, u32[]{:S(2)}) copy-start(f32[64,16]{0,1:T(8,128)} %param.15) | copy-start | bytes 12292
  1.8 16.6 %all-to-all-start = ((bf16[16,64,128]{2,1,0:T(8,128)(2,1)}), bf16[16,64,128]{2,1,0:T(8,128)(2,1)S(1)}, u32[]{:S(2)}, u32[]{:S(2)}) async-start(bf16[16,64,128]{2,1,0:T(8,128)(2,1)} %bitcast.1), calls=%async_computation | async-start | bytes 524288 | tf_op jit(solution)/shard_map/all_to_all | solution.py:443
  7.7 3.9 %copy-start.3 = (bf16[128,64]{0,1:T(8,128)(2,1)S(1)}, bf16[128,64]{0,1:T(8,128)(2,1)}, u32[]{:S(2)}) copy-start(bf16[128,64]{0,1:T(8,128)(2,1)} %param.13) | copy-start | bytes 49156
  7.7 9.7 %collective-permute-start = (bf16[8,1024]{1,0:T(8,128)(2,1)S(1)}, bf16[8,1024]{1,0:T(8,128)(2,1)S(1)}, u32[]{:S(2)}, u32[]{:S(2)}) collective-permute-start(bf16[8,1024]{1,0:T(8,128)(2,1)S(1)} %get-tuple-element.26), channel_id=1, source_target_pairs={{0,8},{8,16},{16,24},{24,32},{32,40},{40,48},{48,56},{56,64},{64,7... | collective-permute-start | bytes 49160 | tf_op jit(solution)/shard_map/ppermute | solution.py:447
  19.0 2.8 %collective-permute-start.1 = (bf16[128,128]{1,0:T(8,128)(2,1)S(1)}, bf16[128,128]{1,0:T(8,128)(2,1)S(1)}, u32[]{:S(2)}, u32[]{:S(2)}) collective-permute-start(bf16[128,128]{1,0:T(8,128)(2,1)S(1)} %get-tuple-element.35), channel_id=1, source_target_pairs={{0,128},{8,136},{16,144},{24,152},{32,160},{40,168},{48,176},{56,1... | collective-permute-start | bytes 98312 | tf_op jit(solution)/shard_map/ppermute | solution.py:499
  20.5 9.7 %collective-permute-start.2 = (bf16[128,128]{1,0:T(8,128)(2,1)S(1)}, bf16[128,128]{1,0:T(8,128)(2,1)S(1)}, u32[]{:S(2)}, u32[]{:S(2)}) collective-permute-start(bf16[128,128]{1,0:T(8,128)(2,1)S(1)} %get-tuple-element.36.send_ref), channel_id=1, source_target_pairs={{256,384},{264,392},{272,400},{280,408},{288,416},{296,424},{304,4... | collective-permute-start | bytes 98312 | tf_op jit(solution)/shard_map/ppermute | solution.py:499
  21.8 16.8 %collective-permute-start.3 = (bf16[128,128]{1,0:T(8,128)(2,1)S(1)}, bf16[128,128]{1,0:T(8,128)(2,1)S(1)}, u32[]{:S(2)}, u32[]{:S(2)}) collective-permute-start(bf16[128,128]{1,0:T(8,128)(2,1)S(1)} %get-tuple-element.40), channel_id=1, source_target_pairs={{128,256},{136,264},{144,272},{152,280},{160,288},{168,296},{176,3... | collective-permute-start | bytes 98312 | tf_op jit(solution)/shard_map/ppermute | solution.py:499
  22.5 16.1 %collective-permute-start.4 = (bf16[48,128]{1,0:T(8,128)(2,1)S(1)}, bf16[48,128]{1,0:T(8,128)(2,1)S(1)}, u32[]{:S(2)}, u32[]{:S(2)}) collective-permute-start(bf16[48,128]{1,0:T(8,128)(2,1)S(1)} %get-tuple-element.41), channel_id=1, source_target_pairs={{128,384},{136,392},{144,400},{152,408},{160,416},{168,424},{176,4... | collective-permute-start | bytes 36872 | tf_op jit(solution)/shard_map/ppermute | solution.py:499
  40.3 4.2 %copy-start = (bf16[64,1024]{1,0:T(8,128)(2,1)S(1)}, bf16[64,1024]{1,0:T(8,128)(2,1)}, u32[]{:S(2)}) copy-start(bf16[64,1024]{1,0:T(8,128)(2,1)} %outer_ref.3) | copy-start | bytes 393220
  40.3 13.1 %all-to-all-start.1 = ((bf16[16,32,128]{2,1,0:T(8,128)(2,1)}), bf16[16,32,128]{2,1,0:T(8,128)(2,1)S(1)}, u32[]{:S(2)}, u32[]{:S(2)}) async-start(bf16[16,32,128]{2,1,0:T(8,128)(2,1)} %bitcast.6), calls=%async_computation.1 | async-start | bytes 262144 | tf_op jit(solution)/shard_map/all_to_all | solution.py:443
  44.5 8.9 %copy-start.2 = (bf16[64,1024]{1,0:T(8,128)(2,1)S(1)}, bf16[64,1024]{1,0:T(8,128)(2,1)}, u32[]{:S(2)}) copy-start(bf16[64,1024]{1,0:T(8,128)(2,1)} %residual_ref.1) | copy-start | bytes 393220
  54.4 4.6 %copy-start.6 = (bf16[1024]{0:T(1024)(128)(2,1)S(1)}, bf16[1024]{0:T(1024)(128)(2,1)}, u32[]{:S(2)}) copy-start(bf16[1024]{0:T(1024)(128)(2,1)} %param.17) | copy-start | bytes 6148
  54.4 10.1 %all-to-all-start.2 = ((f32[8,8,128]{2,1,0:T(8,128)}), f32[8,8,128]{2,1,0:T(8,128)S(1)}, u32[]{:S(2)}, u32[]{:S(2)}) async-start(f32[8,8,128]{2,1,0:T(8,128)} %bitcast.8), calls=%async_computation.2 | async-start | bytes 65536 | tf_op jit(solution)/shard_map/all_to_all | solution.py:542

commit v6 on v5

--- a/solution.py
+++ b/solution.py
@@ -57,8 +57,20 @@
 
 
 def tables_kernel(
-    place, decay_ref, residue_ref, medium_ref, tap_ref, table_ref, step_ref, jump_ref, rest_ref, mine_ref
+    place,
+    decay_ref,
+    residue_ref,
+    medium_ref,
+    tap_ref,
+    gain_in,
+    table_ref,
+    step_ref,
+    jump_ref,
+    rest_ref,
+    mine_ref,
+    gain_ref,
 ):
+    gain_ref[...] = gain_in[...].astype(F32)
     channels = tap_ref.shape[2]
     half = LANES // 2
     at, to = iota((channels, LANES), 0), iota((channels, LANES), 1)
@@ -232,10 +244,13 @@
     return lax.div(place[0], NEAR)
 
 
-def first_states_kernel(width, place, *refs):
+def first_states_kernel(
+    width, place, raw_ref, tap_ref, table_ref, step_ref, x_ref, state_ref, send_ref, padded, end
+):
     @pl.when(super_block(place) == 0)
     def _():
-        find_states(width, False, *refs)
+        known = (raw_ref, tap_ref, table_ref, step_ref)
+        find_states(width, False, *known, x_ref, state_ref, end, send_ref, padded)
 
 
 def later_states_kernel(width, place, raw_ref, tap_ref, table_ref, step_ref, x_in, state_in, *refs):
@@ -384,7 +399,7 @@
     tall = jnp.broadcast_to(scale[:1], (LANES, LANES)).T[:rows]
     for tile in range(channels // LANES):
         lanes = slice(tile * LANES, (tile + 1) * LANES)
-        out_ref[:, lanes] = (hidden_ref[:, lanes] * gain_ref[:, lanes].astype(F32) * tall).astype(BF16)
+        out_ref[:, lanes] = (hidden_ref[:, lanes] * gain_ref[:, lanes] * tall).astype(BF16)
 
 
 def on_device(
@@ -447,7 +462,7 @@
     halo = lax.ppermute(outer_tail, "ctx", [(i, i + 1) for i in range(size - 1)])
     arrived, halo = lax.optimization_barrier((arrived, halo))
     place = lax.axis_index("ctx").reshape(1).astype(jnp.int32)
-    table, step, jump, rest, taps = call(
+    table, step, jump, rest, taps, gain = call(
         tables_kernel,
         [
             pltpu.VMEM((count, 7, LANES, LANES), BF16),
@@ -455,11 +470,13 @@
             pltpu.VMEM((pack, LANES), F32),
             pltpu.VMEM((pack, LANES), F32),
             pltpu.VMEM((FEAT, LANES), F32),
+            pltpu.VMEM((1, channels), F32),
         ],
         decay_rates.T,
         residues.T,
         medium_taps.T,
         feature_taps,
+        norm_gain.reshape(1, channels),
         scalars=(place,),
     )
     outer_feat = call(
@@ -479,8 +496,12 @@
     ]
     padded = [pltpu.VMEM((HALO + NEAR * rows, LANES), F32)]
     known = (arrived, taps, table, step)
-    x, states, _, first_packed = call(
-        with_width(first_states_kernel), found, *known, scalars=(place,), scratch=padded
+    x, states, first_packed = call(
+        with_width(first_states_kernel),
+        [found[0], found[1], packet],
+        *known,
+        scalars=(place,),
+        scratch=padded + [pltpu.VMEM((pack, LANES), F32)],
     )
     x, states, end, packed = call(
         with_width(later_states_kernel),
@@ -493,6 +514,8 @@
         aliases={5: 0, 6: 1},
     )
     local = call(with_width(local_kernel), pltpu.VMEM((slab_rows, LANES), F32), x, table, states)
+
+    local, outer_feat = lax.optimization_barrier((local, outer_feat))
 
     def passed(x, start, end):
         pairs = [(NEAR * start + n, NEAR * end + n) for n in range(NEAR)]
@@ -545,7 +568,7 @@
         jax.ShapeDtypeStruct((rows, channels), BF16),
         hidden,
         all_sums.reshape(8 * parts, LANES),
-        norm_gain.reshape(1, channels),
+        gain,
     )
 
 

time: 65.7 us -> 63.2 us (0.962)
  blocking collectives: 0 us -> 22.5 us
  waiting for transfers between devices: 34.5 us -> 20.2 us
  starting transfers between devices: 22.4 us -> 13.8 us
  Pallas kernels: 8.04 us -> 6.15 us
    all_to_all x0 -> x2, blocking collectives: none -> 22.5 us  [the longest x1 12.8 us: exchange(): lax.all_to_all(x.reshape(slab), 'ctx', 0, 0, axis_index_groups=neighbours)]
    all_to_all x2 -> x1, waiting for transfers between devices: 9.67 us -> 0.92 us  [exchange(): lax.all_to_all(x.reshape(slab), 'ctx', 0, 0, axis_index_groups=neighbours)]
    all_to_all x1 -> x0, waiting for transfers between devices: 5.43 us -> none  [on_device(): all_sums = lax.all_to_all(sums.reshape(parts, 8, LANES), 'tp', 0, 0)]
    all_to_all x1 -> x0, starting transfers between devices: 4.6 us -> none  [on_device(): all_sums = lax.all_to_all(sums.reshape(parts, 8, LANES), 'tp', 0, 0)]
    all_to_all x2 -> x1, starting transfers between devices: 10.1 us -> 5.91 us  [exchange(): lax.all_to_all(x.reshape(slab), 'ctx', 0, 0, axis_index_groups=neighbours)]
    pallas_call x9, Pallas kernels: 6.23 us -> 4.35 us  [call(): pl.pallas_call(kernel, in_specs=[smem] * len(scalars) + [vmem] * len(arra...]
  transfers between devices with their start and end apart: 8 -> 6, of which waited for: 6 -> 4; matrix products, arithmetic and copies ran while one was open for 0% -> 0% of each run, Pallas kernels for 3% -> 4%
where the time goes in v6:
time: 63.2 us; the launch traced here: 62.8 us
  blocking collectives  22.5 us (36%)
  waiting for transfers between devices  20.2 us (32%)
  starting transfers between devices  13.8 us (22%)
  Pallas kernels  6.15 us (10%)
    ppermute x4, waiting for transfers between devices, passed(): return lax.ppermute(x, 'ctx', pairs)  14.3 us
    all_to_all x1, blocking collectives, exchange(): lax.all_to_all(x.reshape(slab), 'ctx', 0, 0, axis_index_groups=neighbours)  12.8 us
    all_to_all x1, blocking collectives, on_device(): all_sums = lax.all_to_all(sums.reshape(parts, 8, LANES), 'tp', 0, 0)  9.71 us
    all_to_all x1, starting transfers between devices, exchange(): lax.all_to_all(x.reshape(slab), 'ctx', 0, 0, axis_index_groups=neighbours)  5.91 us
    ppermute x1, waiting for transfers between devices, on_device(): lax.ppermute(outer_tail, 'ctx', [(i, i + 1) for i in range(size - 1)])  4.93 us
    pallas_call x9, Pallas kernels, call(): pl.pallas_call(kernel, in_specs=[smem] * len(scalars) + [vmem] * len(arra...  4.35 us
    ppermute x4, starting transfers between devices, passed(): return lax.ppermute(x, 'ctx', pairs)  4.03 us
    ppermute x1, starting transfers between devices, on_device(): lax.ppermute(outer_tail, 'ctx', [(i, i + 1) for i in range(size - 1)])  3.83 us
  transfers between devices with their start and end apart: 6, of which 4 were waited for; matrix products, arithmetic and copies ran while one was open for 0% of the time, Pallas kernels for 4%

profile of v6, /device:TPU:384, one launch (start us, length us, event | category | flops | bytes accessed | tf_op | source)
XLA Modules:
  0.0 62.8 jit_solution(7059247983757085193)
XLA Ops:
  0.0 1.8 %pack.1 = (bf16[1024,128]{1,0:T(8,128)(2,1)}, bf16[8,1024]{1,0:T(8,128)(2,1)S(1)}) custom-call(bf16[64,1024]{1,0:T(8,128)(2,1)} %inner_ref.1, bf16[64,1024]{1,0:T(8,128)(2,1)} %value_ref.1, bf16[64,1024]{1,0:T(8,128)(2,1)} %outer_ref.3), custom_call_target="tpu_custom_call" | custom-call | tf_op jit(solution)/shard_map/pack/pallas_call | solution.py:442
  1.8 5.9 %all-to-all-start = ((bf16[16,64,128]{2,1,0:T(8,128)(2,1)}), bf16[16,64,128]{2,1,0:T(8,128)(2,1)S(1)}, u32[]{:S(2)}, u32[]{:S(2)}) async-start(bf16[16,64,128]{2,1,0:T(8,128)(2,1)} %bitcast.1), calls=%async_computation | async-start | bytes 524288 | tf_op jit(solution)/shard_map/all_to_all | solution.py:458
  7.7 0.0 copy-start.3
  7.7 3.8 %collective-permute-start = (bf16[8,1024]{1,0:T(8,128)(2,1)S(1)}, bf16[8,1024]{1,0:T(8,128)(2,1)S(1)}, u32[]{:S(2)}, u32[]{:S(2)}) collective-permute-start(bf16[8,1024]{1,0:T(8,128)(2,1)S(1)} %get-tuple-element.29), channel_id=1, source_target_pairs={{0,8},{8,16},{16,24},{24,32},{32,40},{40,48},{48,56},{56,64},{64,7... | collective-permute-start | bytes 49160 | tf_op jit(solution)/shard_map/ppermute | solution.py:462
  11.7 0.9 %shard_map.91 = (bf16[4,7,128,128]{3,2,1,0:T(8,128)(2,1)S(1)}, f32[32,128]{1,0:T(8,128)S(1)}, f32[32,128]{1,0:T(8,128)S(1)}, f32[32,128]{1,0:T(8,128)S(1)}, f32[7,128]{1,0:T(8,128)S(1)}, /*index=5*/f32[1,1024]{1,0:T(1,128)S(1)}) custom-call(s32[1]{0:T(128)} %bitcast.place, f32[16,64]{1,0:T(8,128)S(1)} %bitcast.19, f32[16,64]{1,0:T(8,128)S(1)} %bitcast.20, ...), custom_call_target="tpu_custom_call" | custom-call | tf_op jit(solution)/shard_map/pallas_call | solution.py:425
  12.6 4.9 %collective-permute-done.halo_ref = bf16[8,1024]{1,0:T(8,128)(2,1)S(1)} collective-permute-done((bf16[8,1024]{1,0:T(8,128)(2,1)S(1)}, bf16[8,1024]{1,0:T(8,128)(2,1)S(1)}, u32[]{:S(2)}, u32[]{:S(2)}) %collective-permute-start) | collective-permute-done | bytes 16416 | tf_op jit(solution)/shard_map/ppermute | solution.py:462
  17.5 0.9 %all-to-all-done = bf16[16,64,128]{2,1,0:T(8,128)(2,1)S(1)} async-done(((bf16[16,64,128]{2,1,0:T(8,128)(2,1)}), bf16[16,64,128]{2,1,0:T(8,128)(2,1)S(1)}, u32[]{:S(2)}, u32[]{:S(2)}) %all-to-all-start) | async-done | bytes 262176 | tf_op jit(solution)/shard_map/all_to_all | solution.py:458
  18.4 0.7 %collective-permute-start.1 = (bf16[128,128]{1,0:T(8,128)(2,1)S(1)}, bf16[128,128]{1,0:T(8,128)(2,1)S(1)}, u32[]{:S(2)}, u32[]{:S(2)}) collective-permute-start(bf16[128,128]{1,0:T(8,128)(2,1)S(1)} %get-tuple-element.40), channel_id=1, source_target_pairs={{0,128},{8,136},{16,144},{24,152},{32,160},{40,168},{48,176},{56,1... | collective-permute-start | bytes 98312 | tf_op jit(solution)/shard_map/ppermute | solution.py:522
  19.1 0.8 %shard_map.93 = (bf16[512,128]{1,0:T(8,128)(2,1)S(1)}, f32[512,128]{1,0:T(8,128)S(1)}, f32[32,128]{1,0:T(8,128)S(1)}, bf16[128,128]{1,0:T(8,128)(2,1)S(1)}) custom-call(s32[1]{0:T(128)} %bitcast.place, bf16[1024,128]{1,0:T(8,128)(2,1)S(1)} %bitcast.11, f32[7,128]{1,0:T(8,128)S(1)} %get-tuple-element.31.tap_ref, ...), custom_call_target="tpu_custom_call", output_to_operand_aliasing={{0}: (5, {}), {1}: (6, {})} | custom-call | tf_op jit(solution)/shard_map/pallas_call | solution.py:425
  19.9 1.3 %collective-permute-start.2 = (bf16[128,128]{1,0:T(8,128)(2,1)S(1)}, bf16[128,128]{1,0:T(8,128)(2,1)S(1)}, u32[]{:S(2)}, u32[]{:S(2)}) collective-permute-start(bf16[128,128]{1,0:T(8,128)(2,1)S(1)} %get-tuple-element.41.send_ref), channel_id=1, source_target_pairs={{256,384},{264,392},{272,400},{280,408},{288,416},{296,424},{304,4... | collective-permute-start | bytes 98312 | tf_op jit(solution)/shard_map/ppermute | solution.py:522
  21.2 0.0 collective-permute-done.1.got_ref.got_01
  21.2 0.0 copy-start
  21.3 0.8 %collective-permute-start.3 = (bf16[128,128]{1,0:T(8,128)(2,1)S(1)}, bf16[128,128]{1,0:T(8,128)(2,1)S(1)}, u32[]{:S(2)}, u32[]{:S(2)}) collective-permute-start(bf16[128,128]{1,0:T(8,128)(2,1)S(1)} %get-tuple-element.45), channel_id=1, source_target_pairs={{128,256},{136,264},{144,272},{152,280},{160,288},{168,296},{176,3... | collective-permute-start | bytes 98312 | tf_op jit(solution)/shard_map/ppermute | solution.py:522
  22.1 1.3 %collective-permute-start.4 = (bf16[48,128]{1,0:T(8,128)(2,1)S(1)}, bf16[48,128]{1,0:T(8,128)(2,1)S(1)}, u32[]{:S(2)}, u32[]{:S(2)}) collective-permute-start(bf16[48,128]{1,0:T(8,128)(2,1)S(1)} %get-tuple-element.46), channel_id=1, source_target_pairs={{128,384},{136,392},{144,400},{152,408},{160,416},{168,424},{176,4... | collective-permute-start | bytes 36872 | tf_op jit(solution)/shard_map/ppermute | solution.py:522
  23.4 0.2 shard_map.95.outer_ref
  23.5 0.3 shard_map.94.local_ref
  23.9 5.8 %collective-permute-done.2.got_23 = bf16[128,128]{1,0:T(8,128)(2,1)S(1)} collective-permute-done((bf16[128,128]{1,0:T(8,128)(2,1)S(1)}, bf16[128,128]{1,0:T(8,128)(2,1)S(1)}, u32[]{:S(2)}, u32[]{:S(2)}) %collective-permute-start.2) | collective-permute-done | bytes 32800 | tf_op jit(solution)/shard_map/ppermute | solution.py:522
  29.6 8.5 %collective-permute-done.4.got_13 = bf16[48,128]{1,0:T(8,128)(2,1)S(1)} collective-permute-done((bf16[48,128]{1,0:T(8,128)(2,1)S(1)}, bf16[48,128]{1,0:T(8,128)(2,1)S(1)}, u32[]{:S(2)}, u32[]{:S(2)}) %collective-permute-start.4) | collective-permute-done | bytes 12320 | tf_op jit(solution)/shard_map/ppermute | solution.py:522
  38.2 0.0 collective-permute-done.3.got_12
  38.2 1.0 %shard_map.97 = bf16[512,128]{1,0:T(8,128)(2,1)S(1)} custom-call(s32[1]{0:T(128)} %bitcast.place, f32[512,128]{1,0:T(8,128)S(1)} %shard_map.94.local_ref, bf16[128,128]{1,0:T(8,128)(2,1)S(1)} %collective-permute-done.1.got_ref.got_01, bf16[128,128]{1,0:T(8,128)(2,1)S(1)} %collective-permute-done.2.got_23, ...), custom_call_target="tpu_custom_call" | custom-call | tf_op jit(solution)/shard_map/pallas_call | solution.py:425
  39.2 12.8 %all_to_all.15 = bf16[16,32,128]{2,1,0:T(8,128)(2,1)S(1)} all-to-all(bf16[16,32,128]{2,1,0:T(8,128)(2,1)S(1)} %bitcast.14), channel_id=1, replica_groups={{0,8,16,24,32,40,48,56,64,72,80,88,96,104,112,120},{128,136,144,152,160..., dimensions={0} | all-to-all | bytes 262144 | tf_op jit(solution)/shard_map/all_to_all | solution.py:458
  52.0 0.3 shard_map.98
  52.3 9.7 %all_to_all.16 = f32[8,8,128]{2,1,0:T(8,128)S(1)} all-to-all(f32[8,8,128]{2,1,0:T(8,128)S(1)} %bitcast.17), channel_id=1, replica_groups=mesh['ctx'=64,'tp'=8] {'tp'}, dimensions={0} | all-to-all | bytes 65536 | tf_op jit(solution)/shard_map/all_to_all | solution.py:565
  62.0 0.8 %shard_map.99 = bf16[64,1024]{1,0:T(8,128)(2,1)} custom-call(f32[64,1024]{1,0:T(8,128)S(1)} %get-tuple-element.48.hidden_ref, f32[64,128]{1,0:T(8,128)S(1)} %bitcast.16, f32[1,1024]{1,0:T(1,128)S(1)} %get-tuple-element.50.gain_ref), custom_call_target="tpu_custom_call" | custom-call | tf_op jit(solution)/shard_map/pallas_call | solution.py:425
  (15 shorter events, 0.0 us)
Async XLA Ops:
  1.8 9.8 %copy-start.6 = (bf16[1024]{0:T(1024)(128)(2,1)S(1)}, bf16[1024]{0:T(1024)(128)(2,1)}, u32[]{:S(2)}) copy-start(bf16[1024]{0:T(1024)(128)(2,1)} %param.17) | copy-start | bytes 6148
  1.8 9.8 %copy-start.1 = (bf16[3,7,1024]{2,1,0:T(8,128)(2,1)S(1)}, bf16[3,7,1024]{2,1,0:T(8,128)(2,1)}, u32[]{:S(2)}) copy-start(bf16[3,7,1024]{2,1,0:T(8,128)(2,1)} %tap_ref.3) | copy-start | bytes 129028
  1.8 9.8 %copy-start.4 = (f32[64,16]{0,1:T(8,128)S(1)}, f32[64,16]{0,1:T(8,128)}, u32[]{:S(2)}) copy-start(f32[64,16]{0,1:T(8,128)} %param.14) | copy-start | bytes 12292
  1.8 9.8 %copy-start.5 = (f32[64,16]{0,1:T(8,128)S(1)}, f32[64,16]{0,1:T(8,128)}, u32[]{:S(2)}) copy-start(f32[64,16]{0,1:T(8,128)} %param.15) | copy-start | bytes 12292
  1.8 16.6 %all-to-all-start = ((bf16[16,64,128]{2,1,0:T(8,128)(2,1)}), bf16[16,64,128]{2,1,0:T(8,128)(2,1)S(1)}, u32[]{:S(2)}, u32[]{:S(2)}) async-start(bf16[16,64,128]{2,1,0:T(8,128)(2,1)} %bitcast.1), calls=%async_computation | async-start | bytes 524288 | tf_op jit(solution)/shard_map/all_to_all | solution.py:458
  7.7 3.9 %copy-start.3 = (bf16[128,64]{0,1:T(8,128)(2,1)S(1)}, bf16[128,64]{0,1:T(8,128)(2,1)}, u32[]{:S(2)}) copy-start(bf16[128,64]{0,1:T(8,128)(2,1)} %param.13) | copy-start | bytes 49156
  7.7 9.7 %collective-permute-start = (bf16[8,1024]{1,0:T(8,128)(2,1)S(1)}, bf16[8,1024]{1,0:T(8,128)(2,1)S(1)}, u32[]{:S(2)}, u32[]{:S(2)}) collective-permute-start(bf16[8,1024]{1,0:T(8,128)(2,1)S(1)} %get-tuple-element.29), channel_id=1, source_target_pairs={{0,8},{8,16},{16,24},{24,32},{32,40},{40,48},{48,56},{56,64},{64,7... | collective-permute-start | bytes 49160 | tf_op jit(solution)/shard_map/ppermute | solution.py:462
  18.4 2.8 %collective-permute-start.1 = (bf16[128,128]{1,0:T(8,128)(2,1)S(1)}, bf16[128,128]{1,0:T(8,128)(2,1)S(1)}, u32[]{:S(2)}, u32[]{:S(2)}) collective-permute-start(bf16[128,128]{1,0:T(8,128)(2,1)S(1)} %get-tuple-element.40), channel_id=1, source_target_pairs={{0,128},{8,136},{16,144},{24,152},{32,160},{40,168},{48,176},{56,1... | collective-permute-start | bytes 98312 | tf_op jit(solution)/shard_map/ppermute | solution.py:522
  19.9 9.7 %collective-permute-start.2 = (bf16[128,128]{1,0:T(8,128)(2,1)S(1)}, bf16[128,128]{1,0:T(8,128)(2,1)S(1)}, u32[]{:S(2)}, u32[]{:S(2)}) collective-permute-start(bf16[128,128]{1,0:T(8,128)(2,1)S(1)} %get-tuple-element.41.send_ref), channel_id=1, source_target_pairs={{256,384},{264,392},{272,400},{280,408},{288,416},{296,424},{304,4... | collective-permute-start | bytes 98312 | tf_op jit(solution)/shard_map/ppermute | solution.py:522
  21.2 2.1 %copy-start = (bf16[64,1024]{1,0:T(8,128)(2,1)S(1)}, bf16[64,1024]{1,0:T(8,128)(2,1)}, u32[]{:S(2)}) copy-start(bf16[64,1024]{1,0:T(8,128)(2,1)} %outer_ref.3) | copy-start | bytes 393220
  21.3 16.9 %collective-permute-start.3 = (bf16[128,128]{1,0:T(8,128)(2,1)S(1)}, bf16[128,128]{1,0:T(8,128)(2,1)S(1)}, u32[]{:S(2)}, u32[]{:S(2)}) collective-permute-start(bf16[128,128]{1,0:T(8,128)(2,1)S(1)} %get-tuple-element.45), channel_id=1, source_target_pairs={{128,256},{136,264},{144,272},{152,280},{160,288},{168,296},{176,3... | collective-permute-start | bytes 98312 | tf_op jit(solution)/shard_map/ppermute | solution.py:522
  22.1 16.1 %collective-permute-start.4 = (bf16[48,128]{1,0:T(8,128)(2,1)S(1)}, bf16[48,128]{1,0:T(8,128)(2,1)S(1)}, u32[]{:S(2)}, u32[]{:S(2)}) collective-permute-start(bf16[48,128]{1,0:T(8,128)(2,1)S(1)} %get-tuple-element.46), channel_id=1, source_target_pairs={{128,384},{136,392},{144,400},{152,408},{160,416},{168,424},{176,4... | collective-permute-start | bytes 36872 | tf_op jit(solution)/shard_map/ppermute | solution.py:522
  39.2 12.8 %copy-start.2 = (bf16[64,1024]{1,0:T(8,128)(2,1)S(1)}, bf16[64,1024]{1,0:T(8,128)(2,1)}, u32[]{:S(2)}) copy-start(bf16[64,1024]{1,0:T(8,128)(2,1)} %residual_ref.1) | copy-start | bytes 393220

commit v7 on v6

--- a/solution.py
+++ b/solution.py
@@ -201,8 +201,24 @@
     return jnp.concatenate(parts, 0)
 
 
+def find_local(width, wide, table_ref, states, out_ref):
+    count = table_ref.shape[0]
+    zeros = jnp.zeros((8, LANES), F32)
+    for q in range(count):
+        x = of_group(wide, q, count)
+        before = jnp.concatenate([zeros, x[:-8]], 0).astype(BF16)
+        earlier = jnp.concatenate([zeros, zeros, x[:-16]], 0).astype(BF16)
+        x = x.astype(BF16)
+        mixed = dot(x, table_ref[q, 0]) + dot(x, table_ref[q, 1])
+        mixed = mixed + dot(before, table_ref[q, 2]) + dot(earlier, table_ref[q, 3])
+        mixed = mixed + dot(two_parts(of_group(states, q, count), width), table_ref[q, 6])
+        for block in range(x.shape[0] // 8):
+            at = 8 * (count * block + q)
+            out_ref[at : at + 8] = mixed[8 * block : 8 * block + 8]
+
+
 def find_states(
-    width, later, raw_ref, tap_ref, table_ref, step_ref, x_ref, state_ref, end_ref, send_ref, padded
+    width, later, raw_ref, tap_ref, table_ref, step_ref, local_ref, end_ref, send_ref, padded, state_ref
 ):
     count = table_ref.shape[0]
     block = LANES // 2
@@ -220,7 +236,6 @@
             products.append(jnp.where(early, 0.0, product) if later and b == 0 else product)
         slabs.append(slabs_of(jnp.where(low, products[0], products[1])))
     wide = jnp.concatenate(slabs, 0)
-    x_ref[...] = wide.astype(BF16)
     ends = []
     for q in range(count):
         x = of_group(wide, q, count).astype(BF16)
@@ -238,22 +253,23 @@
     send_ref[rows : 3 * rows] = wide[(blocks - 2) * rows :].astype(BF16)
     send_ref[3 * rows : 3 * rows + EDGE] = raw_ref[blocks * block - EDGE :]
     send_ref[3 * rows + EDGE :] = raw_ref[:EDGE]
+    find_local(width, wide, table_ref, state_ref[...], local_ref)
 
 
 def super_block(place):
     return lax.div(place[0], NEAR)
 
 
-def first_states_kernel(
-    width, place, raw_ref, tap_ref, table_ref, step_ref, x_ref, state_ref, send_ref, padded, end
-):
+def first_states_kernel(width, place, *refs):
+    raw_ref, tap_ref, table_ref, step_ref, local_ref, send_ref, padded, state_ref, end_ref = refs
+
     @pl.when(super_block(place) == 0)
     def _():
         known = (raw_ref, tap_ref, table_ref, step_ref)
-        find_states(width, False, *known, x_ref, state_ref, end, send_ref, padded)
-
-
-def later_states_kernel(width, place, raw_ref, tap_ref, table_ref, step_ref, x_in, state_in, *refs):
+        find_states(width, False, *known, local_ref, end_ref, send_ref, padded, state_ref)
+
+
+def later_states_kernel(width, place, raw_ref, tap_ref, table_ref, step_ref, local_in, *refs):
     @pl.when(super_block(place) > 0)
     def _():
         find_states(width, True, raw_ref, tap_ref, table_ref, step_ref, *refs)
@@ -288,48 +304,20 @@
         next_ref[rows:] = send_ref[rows:]
 
 
-def local_kernel(width, x_ref, table_ref, state_ref, out_ref):
-    count = table_ref.shape[0]
-    wide = x_ref[...].astype(F32)
-    states = state_ref[...]
-    zeros = jnp.zeros((8, LANES), F32)
-    for q in range(count):
-        x = of_group(wide, q, count)
-        before = jnp.concatenate([zeros, x[:-8]], 0).astype(BF16)
-        earlier = jnp.concatenate([zeros, zeros, x[:-16]], 0).astype(BF16)
-        x = x.astype(BF16)
-        mixed = dot(x, table_ref[q, 0]) + dot(x, table_ref[q, 1])
-        mixed = mixed + dot(before, table_ref[q, 2]) + dot(earlier, table_ref[q, 3])
-        mixed = mixed + dot(two_parts(of_group(states, q, count), width), table_ref[q, 6])
-        for block in range(x.shape[0] // 8):
-            at = 8 * (count * block + q)
-            out_ref[at : at + 8] = mixed[8 * block : 8 * block + 8]
-
-
-def finish_kernel(
-    width,
-    place,
-    local_ref,
-    got_01,
-    got_23,
-    got_12,
-    got_13,
-    raw_ref,
-    tap_ref,
-    table_ref,
-    step_ref,
-    jump_ref,
-    rest_ref,
-    out_ref,
-    incoming_ref,
+def spread(width, state, step, table, blocks, added=None):
+    states = []
+    for block in range(blocks):
+        states.append(state)
+        state = state * step
+        if block == 0 and added is not None:
+            state = state + added
+    return dot(two_parts(jnp.concatenate(states, 0), width), table)
+
+
+def join_kernel(
+    width, place, local_ref, got_01, got_23, got_12, raw_ref, tap_ref, table_ref, step_ref, out_ref
 ):
-    here = super_block(place)
-
-    @pl.when(here == 0)
-    def _():
-        out_ref[...] = local_ref[...].astype(BF16)
-
-    @pl.when(here > 0)
+    @pl.when(super_block(place) > 0)
     def _():
         count = table_ref.shape[0]
         rows = 8 * count
@@ -337,30 +325,13 @@
         got = got_01[...].astype(F32) + got_23[...].astype(F32) + got_12[...].astype(F32)
         edge = slice(3 * rows, 3 * rows + EDGE)
         own_slab = missing(tap_ref, got[edge], raw_ref[:EDGE].astype(F32))
-        incoming_ref[...] = join_three(got[:rows], width)
-
-        @pl.when(here == 3)
-        def _():
-            far_tail = got_13[rows:].astype(F32)
-            far_slab = missing(tap_ref, far_tail, got_23[3 * rows + EDGE :].astype(F32))
-            more = rest_ref[...] * to_states(table_ref, far_slab)
-            incoming_ref[...] += more + jump_ref[...] * join_three(got_13[:rows], width)
-
-        incoming = incoming_ref[...]
+        incoming = join_three(got[:rows], width)
         added = to_states(table_ref, own_slab)
         zeros = jnp.zeros((8, LANES), F32)
         parts = []
         for q in range(count):
             at = slice(8 * q, 8 * q + 8)
-            step = step_ref[at]
-            state = incoming[at]
-            states = []
-            for block in range(blocks):
-                states.append(state)
-                state = state * step
-                if block == 0:
-                    state = state + added[at]
-            mixed = dot(two_parts(jnp.concatenate(states, 0), width), table_ref[q, 6])
+            mixed = spread(width, incoming[at], step_ref[at], table_ref[q, 6], blocks, added[at])
             last_but_one, last, first = got[rows:][at], got[2 * rows :][at], own_slab[at]
             now = jnp.concatenate([first, zeros, zeros, zeros], 0).astype(BF16)
             before = jnp.concatenate([last, first, zeros, zeros], 0).astype(BF16)
@@ -369,7 +340,43 @@
             start = start + dot(before, table_ref[q, 2]) + dot(earlier, table_ref[q, 3])
             mixed = jnp.concatenate([mixed[:32] + start, mixed[32:]], 0)
             parts.append(mixed.reshape(blocks, 8, LANES))
-        total = local_ref[...] + jnp.concatenate(parts, 1).reshape(local_ref.shape)
+        out_ref[...] = local_ref[...] + jnp.concatenate(parts, 1).reshape(local_ref.shape)
+
+
+def finish_kernel(
+    width,
+    place,
+    near_ref,
+    got_23,
+    got_13,
+    tap_ref,
+    table_ref,
+    step_ref,
+    jump_ref,
+    rest_ref,
+    out_ref,
+):
+    here = super_block(place)
+
+    @pl.when(here != 3)
+    def _():
+        out_ref[...] = near_ref[...].astype(BF16)
+
+    @pl.when(here == 3)
+    def _():
+        count = table_ref.shape[0]
+        rows = 8 * count
+        blocks = near_ref.shape[0] // rows
+        far_tail = got_13[rows:].astype(F32)
+        far_slab = missing(tap_ref, far_tail, got_23[3 * rows + EDGE :].astype(F32))
+        incoming = rest_ref[...] * to_states(table_ref, far_slab)
+        incoming = incoming + jump_ref[...] * join_three(got_13[:rows], width)
+        parts = []
+        for q in range(count):
+            at = slice(8 * q, 8 * q + 8)
+            mixed = spread(width, incoming[at], step_ref[at], table_ref[q, 6], blocks)
+            parts.append(mixed.reshape(blocks, 8, LANES))
+        total = near_ref[...] + jnp.concatenate(parts, 1).reshape(near_ref.shape)
         out_ref[...] = total.astype(BF16)
 
 
@@ -439,16 +446,24 @@
     pack = 8 * count
     with_width = lambda kernel: functools.partial(kernel, width)
 
+    steps = 4
+    part = pl.BlockSpec((rows, channels // steps), lambda i: (0, i))
     raw, outer_tail = pl.pallas_call(
         pack_kernel,
-        grid=(1,),
+        grid=(steps,),
         in_specs=[
-            pl.BlockSpec((rows, channels), lambda i: (0, 0)),
-            pl.BlockSpec((rows, channels), lambda i: (0, 0)),
-            pl.BlockSpec((HALO, channels), lambda i: (rows // HALO - 1, 0)),
+            part,
+            part,
+            pl.BlockSpec((HALO, channels // steps), lambda i: (rows // HALO - 1, i)),
         ],
-        out_shape=[pltpu.VMEM((NEAR * rows, LANES), BF16), pltpu.VMEM((HALO, channels), BF16)],
-        out_specs=[vmem, vmem],
+        out_specs=[
+            pl.BlockSpec((NEAR * rows // steps, LANES), lambda i: (i, 0)),
+            pl.BlockSpec((HALO, channels // steps), lambda i: (0, i)),
+        ],
+        out_shape=[
+            jax.ShapeDtypeStruct((NEAR * rows, LANES), BF16),
+            jax.ShapeDtypeStruct((HALO, channels), BF16),
+        ],
         name="pack",
     )(inner_input, value_input, outer_input)
     neighbours = [[NEAR * f + n for n in range(NEAR)] for f in range(far)]
@@ -488,32 +503,26 @@
         scratch=[pltpu.VMEM((tiles, HALO + rows, LANES), F32)],
     )
     packet = pltpu.VMEM((3 * pack + 2 * EDGE, LANES), BF16)
-    found = [
-        pltpu.VMEM((slab_rows, LANES), BF16),
-        pltpu.VMEM((slab_rows, LANES), F32),
-        pltpu.VMEM((pack, LANES), F32),
-        packet,
-    ]
-    padded = [pltpu.VMEM((HALO + NEAR * rows, LANES), F32)]
+    whole = pltpu.VMEM((slab_rows, LANES), F32)
+    ends = pltpu.VMEM((pack, LANES), F32)
+    scratch = [pltpu.VMEM((HALO + NEAR * rows, LANES), F32), whole]
     known = (arrived, taps, table, step)
-    x, states, first_packed = call(
+    local, first_packed = call(
         with_width(first_states_kernel),
-        [found[0], found[1], packet],
+        [whole, packet],
         *known,
         scalars=(place,),
-        scratch=padded + [pltpu.VMEM((pack, LANES), F32)],
-    )
-    x, states, end, packed = call(
+        scratch=scratch + [ends],
+    )
+    local, end, packed = call(
         with_width(later_states_kernel),
-        found,
+        [whole, ends, packet],
         *known,
-        x,
-        states,
+        local,
         scalars=(place,),
-        scratch=padded,
-        aliases={5: 0, 6: 1},
-    )
-    local = call(with_width(local_kernel), pltpu.VMEM((slab_rows, LANES), F32), x, table, states)
+        scratch=scratch,
+        aliases={5: 0},
+    )
 
     local, outer_feat = lax.optimization_barrier((local, outer_feat))
 
@@ -538,22 +547,32 @@
     )
     got_13 = passed(state, 1, 3)
     got_12 = passed(repacked, 1, 2)
-    mixed = call(
-        with_width(finish_kernel),
-        pltpu.VMEM((slab_rows, LANES), BF16),
+    near = call(
+        with_width(join_kernel),
+        whole,
         local,
         got_01,
         got_23,
         got_12,
+        arrived,
+        taps,
+        table,
+        step,
+        scalars=(place,),
+        aliases={1: 0},
+    )
+    mixed = call(
+        with_width(finish_kernel),
+        pltpu.VMEM((slab_rows, LANES), BF16),
+        near,
+        got_23,
         got_13,
-        arrived,
         taps,
         table,
         step,
         jump,
         rest,
         scalars=(place,),
-        scratch=[pltpu.VMEM((pack, LANES), F32)],
     )
     hidden, sums = call(
         hidden_kernel,

time: 63.2 us -> 64.4 us (1.019)
  Pallas kernels: 6.15 us -> 7.26 us
    pallas_call x1, Pallas kernels: 1.8 us -> 2.99 us  [on_device(): pl.pallas_call(pack_kernel, grid=(steps,), in_specs=[part, part, pl.Block...]
where the time goes in v7:
time: 64.4 us; the launch traced here: 63.8 us
  blocking collectives  22.6 us (35%)
  waiting for transfers between devices  19.9 us (31%)
  starting transfers between devices  13.8 us (21%)
  Pallas kernels  7.26 us (11%)
    ppermute x4, waiting for transfers between devices, passed(): return lax.ppermute(x, 'ctx', pairs)  14 us
    all_to_all x1, blocking collectives, exchange(): lax.all_to_all(x.reshape(slab), 'ctx', 0, 0, axis_index_groups=neighbours)  12.9 us
    all_to_all x1, blocking collectives, on_device(): all_sums = lax.all_to_all(sums.reshape(parts, 8, LANES), 'tp', 0, 0)  9.72 us
    all_to_all x1, starting transfers between devices, exchange(): lax.all_to_all(x.reshape(slab), 'ctx', 0, 0, axis_index_groups=neighbours)  5.91 us
    ppermute x1, waiting for transfers between devices, on_device(): lax.ppermute(outer_tail, 'ctx', [(i, i + 1) for i in range(size - 1)])  4.93 us
    pallas_call x9, Pallas kernels, call(): pl.pallas_call(kernel, in_specs=[smem] * len(scalars) + [vmem] * len(arra...  4.27 us
    ppermute x4, starting transfers between devices, passed(): return lax.ppermute(x, 'ctx', pairs)  4.03 us
    ppermute x1, starting transfers between devices, on_device(): lax.ppermute(outer_tail, 'ctx', [(i, i + 1) for i in range(size - 1)])  3.83 us
  transfers between devices with their start and end apart: 6, of which 4 were waited for; matrix products, arithmetic and copies ran while one was open for 0% of the time, Pallas kernels for 4%

profile of v7, /device:TPU:384, one launch (start us, length us, event | category | flops | bytes accessed | tf_op | source)
XLA Modules:
  0.0 63.8 jit_solution(6817525014978537401)
XLA Ops:
  0.0 3.0 %pack.1 = (bf16[1024,128]{1,0:T(8,128)(2,1)}, bf16[8,1024]{1,0:T(8,128)(2,1)}) custom-call(bf16[64,1024]{1,0:T(8,128)(2,1)} %inner_ref.1, bf16[64,1024]{1,0:T(8,128)(2,1)} %value_ref.1, bf16[64,1024]{1,0:T(8,128)(2,1)} %outer_ref.3), custom_call_target="tpu_custom_call" | custom-call | tf_op jit(solution)/shard_map/pack/pallas_call | solution.py:451
  3.0 0.0 copy-start.1
  3.0 0.0 copy-start.5
  3.0 5.9 %all-to-all-start = ((bf16[16,64,128]{2,1,0:T(8,128)(2,1)}), bf16[16,64,128]{2,1,0:T(8,128)(2,1)S(1)}, u32[]{:S(2)}, u32[]{:S(2)}) async-start(bf16[16,64,128]{2,1,0:T(8,128)(2,1)} %bitcast.21), calls=%async_computation | async-start | bytes 524288 | tf_op jit(solution)/shard_map/all_to_all | solution.py:473
  9.0 0.0 copy-start.3
  9.0 3.8 %collective-permute-start = (bf16[8,1024]{1,0:T(8,128)(2,1)S(1)}, bf16[8,1024]{1,0:T(8,128)(2,1)S(1)}, u32[]{:S(2)}, u32[]{:S(2)}) collective-permute-start(bf16[8,1024]{1,0:T(8,128)(2,1)S(1)} %copy-done.7), channel_id=1, source_target_pairs={{0,8},{8,16},{16,24},{24,32},{32,40},{40,48},{48,56},{56,64},{64,7... | collective-permute-start | bytes 49160 | tf_op jit(solution)/shard_map/ppermute | solution.py:477
  12.9 0.9 %shard_map.91 = (bf16[4,7,128,128]{3,2,1,0:T(8,128)(2,1)S(1)}, f32[32,128]{1,0:T(8,128)S(1)}, f32[32,128]{1,0:T(8,128)S(1)}, f32[32,128]{1,0:T(8,128)S(1)}, f32[7,128]{1,0:T(8,128)S(1)}, /*index=5*/f32[1,1024]{1,0:T(1,128)S(1)}) custom-call(s32[1]{0:T(128)} %bitcast.place, f32[16,64]{1,0:T(8,128)S(1)} %bitcast.19, f32[16,64]{1,0:T(8,128)S(1)} %bitcast.20, ...), custom_call_target="tpu_custom_call" | custom-call | tf_op jit(solution)/shard_map/pallas_call | solution.py:432
  13.8 4.9 %collective-permute-done.halo_ref = bf16[8,1024]{1,0:T(8,128)(2,1)S(1)} collective-permute-done((bf16[8,1024]{1,0:T(8,128)(2,1)S(1)}, bf16[8,1024]{1,0:T(8,128)(2,1)S(1)}, u32[]{:S(2)}, u32[]{:S(2)}) %collective-permute-start) | collective-permute-done | bytes 16416 | tf_op jit(solution)/shard_map/ppermute | solution.py:477
  18.7 0.9 %all-to-all-done = bf16[16,64,128]{2,1,0:T(8,128)(2,1)S(1)} async-done(((bf16[16,64,128]{2,1,0:T(8,128)(2,1)}), bf16[16,64,128]{2,1,0:T(8,128)(2,1)S(1)}, u32[]{:S(2)}, u32[]{:S(2)}) %all-to-all-start) | async-done | bytes 262176 | tf_op jit(solution)/shard_map/all_to_all | solution.py:473
  19.6 0.7 %collective-permute-start.1 = (bf16[128,128]{1,0:T(8,128)(2,1)S(1)}, bf16[128,128]{1,0:T(8,128)(2,1)S(1)}, u32[]{:S(2)}, u32[]{:S(2)}) collective-permute-start(bf16[128,128]{1,0:T(8,128)(2,1)S(1)} %get-tuple-element.36), channel_id=1, source_target_pairs={{0,128},{8,136},{16,144},{24,152},{32,160},{40,168},{48,176},{56,1... | collective-permute-start | bytes 98312 | tf_op jit(solution)/shard_map/ppermute | solution.py:531
  20.3 0.9 %shard_map.93 = (f32[512,128]{1,0:T(8,128)S(1)}, f32[32,128]{1,0:T(8,128)S(1)}, bf16[128,128]{1,0:T(8,128)(2,1)S(1)}) custom-call(s32[1]{0:T(128)} %bitcast.place, bf16[1024,128]{1,0:T(8,128)(2,1)S(1)} %bitcast.11, f32[7,128]{1,0:T(8,128)S(1)} %get-tuple-element.29.refs_1_.tap_ref, ...), custom_call_target="tpu_custom_call", output_to_operand_aliasing={{0}: (5, {})} | custom-call | tf_op jit(solution)/shard_map/pallas_call | solution.py:432
  21.2 1.3 %collective-permute-start.2 = (bf16[128,128]{1,0:T(8,128)(2,1)S(1)}, bf16[128,128]{1,0:T(8,128)(2,1)S(1)}, u32[]{:S(2)}, u32[]{:S(2)}) collective-permute-start(bf16[128,128]{1,0:T(8,128)(2,1)S(1)} %get-tuple-element.37.send_ref), channel_id=1, source_target_pairs={{256,384},{264,392},{272,400},{280,408},{288,416},{296,424},{304,4... | collective-permute-start | bytes 98312 | tf_op jit(solution)/shard_map/ppermute | solution.py:531
  22.6 0.8 %collective-permute-start.3 = (bf16[128,128]{1,0:T(8,128)(2,1)S(1)}, bf16[128,128]{1,0:T(8,128)(2,1)S(1)}, u32[]{:S(2)}, u32[]{:S(2)}) collective-permute-start(bf16[128,128]{1,0:T(8,128)(2,1)S(1)} %get-tuple-element.41), channel_id=1, source_target_pairs={{128,256},{136,264},{144,272},{152,280},{160,288},{168,296},{176,3... | collective-permute-start | bytes 98312 | tf_op jit(solution)/shard_map/ppermute | solution.py:531
  23.4 1.3 %collective-permute-start.4 = (bf16[48,128]{1,0:T(8,128)(2,1)S(1)}, bf16[48,128]{1,0:T(8,128)(2,1)S(1)}, u32[]{:S(2)}, u32[]{:S(2)}) collective-permute-start(bf16[48,128]{1,0:T(8,128)(2,1)S(1)} %get-tuple-element.42), channel_id=1, source_target_pairs={{128,384},{136,392},{144,400},{152,408},{160,416},{168,424},{176,4... | collective-permute-start | bytes 36872 | tf_op jit(solution)/shard_map/ppermute | solution.py:531
  24.7 0.2 shard_map.94.outer_ref
  24.9 6.1 %collective-permute-done.2.got_23 = bf16[128,128]{1,0:T(8,128)(2,1)S(1)} collective-permute-done((bf16[128,128]{1,0:T(8,128)(2,1)S(1)}, bf16[128,128]{1,0:T(8,128)(2,1)S(1)}, u32[]{:S(2)}, u32[]{:S(2)}) %collective-permute-start.2) | collective-permute-done | bytes 32800 | tf_op jit(solution)/shard_map/ppermute | solution.py:531
  31.0 0.6 shard_map.96.near_ref
  31.6 7.9 %collective-permute-done.4.got_13 = bf16[48,128]{1,0:T(8,128)(2,1)S(1)} collective-permute-done((bf16[48,128]{1,0:T(8,128)(2,1)S(1)}, bf16[48,128]{1,0:T(8,128)(2,1)S(1)}, u32[]{:S(2)}, u32[]{:S(2)}) %collective-permute-start.4) | collective-permute-done | bytes 12320 | tf_op jit(solution)/shard_map/ppermute | solution.py:531
  39.5 0.5 shard_map.97
  40.0 0.0 copy-start.2
  40.0 12.9 %all_to_all.15 = bf16[16,32,128]{2,1,0:T(8,128)(2,1)S(1)} all-to-all(bf16[16,32,128]{2,1,0:T(8,128)(2,1)S(1)} %bitcast.14), channel_id=1, replica_groups={{0,8,16,24,32,40,48,56,64,72,80,88,96,104,112,120},{128,136,144,152,160..., dimensions={0} | all-to-all | bytes 262144 | tf_op jit(solution)/shard_map/all_to_all | solution.py:473
  53.0 0.3 shard_map.98
  53.3 9.7 %all_to_all.16 = f32[8,8,128]{2,1,0:T(8,128)S(1)} all-to-all(f32[8,8,128]{2,1,0:T(8,128)S(1)} %bitcast.17), channel_id=1, replica_groups=mesh['ctx'=64,'tp'=8] {'tp'}, dimensions={0} | all-to-all | bytes 65536 | tf_op jit(solution)/shard_map/all_to_all | solution.py:584
  63.0 0.8 %shard_map.99 = bf16[64,1024]{1,0:T(8,128)(2,1)} custom-call(f32[64,1024]{1,0:T(8,128)S(1)} %get-tuple-element.44.hidden_ref, f32[64,128]{1,0:T(8,128)S(1)} %bitcast.16, f32[1,1024]{1,0:T(1,128)S(1)} %get-tuple-element.46.gain_ref), custom_call_target="tpu_custom_call" | custom-call | tf_op jit(solution)/shard_map/pallas_call | solution.py:432
  (17 shorter events, 0.1 us)
Async XLA Ops:
  3.0 6.0 %copy-start.7 = (bf16[8,1024]{1,0:T(8,128)(2,1)S(1)}, bf16[8,1024]{1,0:T(8,128)(2,1)}, u32[]{:S(2)}) copy-start(bf16[8,1024]{1,0:T(8,128)(2,1)} %get-tuple-element.27) | copy-start | bytes 49156
  3.0 9.8 %copy-start.6 = (bf16[1024]{0:T(1024)(128)(2,1)S(1)}, bf16[1024]{0:T(1024)(128)(2,1)}, u32[]{:S(2)}) copy-start(bf16[1024]{0:T(1024)(128)(2,1)} %param.17) | copy-start | bytes 6148
  3.0 9.8 %copy-start.1 = (bf16[3,7,1024]{2,1,0:T(8,128)(2,1)S(1)}, bf16[3,7,1024]{2,1,0:T(8,128)(2,1)}, u32[]{:S(2)}) copy-start(bf16[3,7,1024]{2,1,0:T(8,128)(2,1)} %tap_ref.3) | copy-start | bytes 129028
  3.0 9.8 %copy-start.4 = (f32[64,16]{0,1:T(8,128)S(1)}, f32[64,16]{0,1:T(8,128)}, u32[]{:S(2)}) copy-start(f32[64,16]{0,1:T(8,128)} %param.14) | copy-start | bytes 12292
  3.0 9.8 %copy-start.5 = (f32[64,16]{0,1:T(8,128)S(1)}, f32[64,16]{0,1:T(8,128)}, u32[]{:S(2)}) copy-start(f32[64,16]{0,1:T(8,128)} %param.15) | copy-start | bytes 12292
  3.0 16.6 %all-to-all-start = ((bf16[16,64,128]{2,1,0:T(8,128)(2,1)}), bf16[16,64,128]{2,1,0:T(8,128)(2,1)S(1)}, u32[]{:S(2)}, u32[]{:S(2)}) async-start(bf16[16,64,128]{2,1,0:T(8,128)(2,1)} %bitcast.21), calls=%async_computation | async-start | bytes 524288 | tf_op jit(solution)/shard_map/all_to_all | solution.py:473
  9.0 3.9 %copy-start.3 = (bf16[128,64]{0,1:T(8,128)(2,1)S(1)}, bf16[128,64]{0,1:T(8,128)(2,1)}, u32[]{:S(2)}) copy-start(bf16[128,64]{0,1:T(8,128)(2,1)} %param.13) | copy-start | bytes 49156
  9.0 9.7 %collective-permute-start = (bf16[8,1024]{1,0:T(8,128)(2,1)S(1)}, bf16[8,1024]{1,0:T(8,128)(2,1)S(1)}, u32[]{:S(2)}, u32[]{:S(2)}) collective-permute-start(bf16[8,1024]{1,0:T(8,128)(2,1)S(1)} %copy-done.7), channel_id=1, source_target_pairs={{0,8},{8,16},{16,24},{24,32},{32,40},{40,48},{48,56},{56,64},{64,7... | collective-permute-start | bytes 49160 | tf_op jit(solution)/shard_map/ppermute | solution.py:477
  19.6 2.9 %collective-permute-start.1 = (bf16[128,128]{1,0:T(8,128)(2,1)S(1)}, bf16[128,128]{1,0:T(8,128)(2,1)S(1)}, u32[]{:S(2)}, u32[]{:S(2)}) collective-permute-start(bf16[128,128]{1,0:T(8,128)(2,1)S(1)} %get-tuple-element.36), channel_id=1, source_target_pairs={{0,128},{8,136},{16,144},{24,152},{32,160},{40,168},{48,176},{56,1... | collective-permute-start | bytes 98312 | tf_op jit(solution)/shard_map/ppermute | solution.py:531
  21.2 9.7 %collective-permute-start.2 = (bf16[128,128]{1,0:T(8,128)(2,1)S(1)}, bf16[128,128]{1,0:T(8,128)(2,1)S(1)}, u32[]{:S(2)}, u32[]{:S(2)}) collective-permute-start(bf16[128,128]{1,0:T(8,128)(2,1)S(1)} %get-tuple-element.37.send_ref), channel_id=1, source_target_pairs={{256,384},{264,392},{272,400},{280,408},{288,416},{296,424},{304,4... | collective-permute-start | bytes 98312 | tf_op jit(solution)/shard_map/ppermute | solution.py:531
  22.6 2.1 %copy-start = (bf16[64,1024]{1,0:T(8,128)(2,1)S(1)}, bf16[64,1024]{1,0:T(8,128)(2,1)}, u32[]{:S(2)}) copy-start(bf16[64,1024]{1,0:T(8,128)(2,1)} %outer_ref.3) | copy-start | bytes 393220
  22.6 8.4 %collective-permute-start.3 = (bf16[128,128]{1,0:T(8,128)(2,1)S(1)}, bf16[128,128]{1,0:T(8,128)(2,1)S(1)}, u32[]{:S(2)}, u32[]{:S(2)}) collective-permute-start(bf16[128,128]{1,0:T(8,128)(2,1)S(1)} %get-tuple-element.41), channel_id=1, source_target_pairs={{128,256},{136,264},{144,272},{152,280},{160,288},{168,296},{176,3... | collective-permute-start | bytes 98312 | tf_op jit(solution)/shard_map/ppermute | solution.py:531
  23.4 16.1 %collective-permute-start.4 = (bf16[48,128]{1,0:T(8,128)(2,1)S(1)}, bf16[48,128]{1,0:T(8,128)(2,1)S(1)}, u32[]{:S(2)}, u32[]{:S(2)}) collective-permute-start(bf16[48,128]{1,0:T(8,128)(2,1)S(1)} %get-tuple-element.42), channel_id=1, source_target_pairs={{128,384},{136,392},{144,400},{152,408},{160,416},{168,424},{176,4... | collective-permute-start | bytes 36872 | tf_op jit(solution)/shard_map/ppermute | solution.py:531
  40.0 12.9 %copy-start.2 = (bf16[64,1024]{1,0:T(8,128)(2,1)S(1)}, bf16[64,1024]{1,0:T(8,128)(2,1)}, u32[]{:S(2)}) copy-start(bf16[64,1024]{1,0:T(8,128)(2,1)} %residual_ref.1) | copy-start | bytes 393220

commit v8 on v7

--- a/solution.py
+++ b/solution.py
@@ -14,7 +14,7 @@
 LANES = 128
 HALO = 8
 FEAT = 7
-EDGE = 16
+EDGE = 8
 NEAR = 16
 
 
@@ -35,19 +35,24 @@
     return high, (x - high.astype(F32)).astype(BF16)
 
 
-def split_three(x, width):
-    high, _ = split(x)
-    middle, _ = split(x - high.astype(F32))
-    low = x - high.astype(F32) - middle.astype(F32)
+def pack_state(x, width):
+    high, low = split(x)
     copy = iota(x.shape, 1) // width
-    part = jnp.where(copy == 0, high.astype(F32), jnp.where(copy == 1, middle.astype(F32), low))
-    return jnp.where(copy < 3, part, 0.0).astype(BF16)
-
-
-def join_three(parts, width):
-    x = parts.astype(F32)
-    x = x + pltpu.roll(x, width, 1)
-    return x + pltpu.roll(x, 2 * width, 1)
+    part = jnp.where(copy % 2 == 0, high.astype(F32), low.astype(F32))
+    half = x.shape[0] // 2
+    return jnp.where(copy[:half] < 2, part[:half], part[half:]).astype(BF16)
+
+
+def unpack_state(packed, width):
+    x = packed.astype(F32)
+    both = x + pltpu.roll(x, width, 1)
+    copy = iota(x.shape, 1) // width
+    parts = []
+    for place in (1, 3):
+        y = jnp.where(copy == place, both, 0.0)
+        y = y + pltpu.roll(y, width, 1)
+        parts.append(y + pltpu.roll(y, 2 * width, 1))
+    return jnp.concatenate(parts, 0)
 
 
 def two_parts(x, width):
@@ -118,7 +123,7 @@
         table_ref[q, 3] = jnp.where(same, medium_wide[:, LANES:], 0.0).astype(BF16)
         rate_lanes, rate_rows, weight_rows = along_lanes(rate), along_rows(rate), along_rows(weight)
         to_end = jnp.exp(-rate_lanes * (block - 1 - row % block).astype(F32))
-        kept = ((lane // modes) % 2 == row // block) & (lane < 3 * width)
+        kept = (lane // modes) % 2 == row // block
         table_ref[q, 4], table_ref[q, 5] = split(jnp.where(kept, to_end, 0.0))
         from_start = weight_rows * jnp.exp(-rate_rows * (lane % block + 1).astype(F32))
         kept = ((row // modes) % 2 == lane // block) & (row < 3 * width)
@@ -249,10 +254,13 @@
         ends.append(carry)
     end = jnp.concatenate(ends, 0)
     end_ref[...] = end
-    send_ref[:rows] = split_three(end, width)
-    send_ref[rows : 3 * rows] = wide[(blocks - 2) * rows :].astype(BF16)
-    send_ref[3 * rows : 3 * rows + EDGE] = raw_ref[blocks * block - EDGE :]
-    send_ref[3 * rows + EDGE :] = raw_ref[:EDGE]
+    at = rows // 2
+    send_ref[:at] = pack_state(end, width)
+    send_ref[at : at + 2 * rows] = wide[(blocks - 2) * rows :].astype(BF16)
+    at = at + 2 * rows
+    send_ref[at : at + EDGE] = raw_ref[blocks * block - EDGE :]
+    if later:
+        send_ref[at + EDGE :] = raw_ref[:EDGE]
     find_local(width, wide, table_ref, state_ref[...], local_ref)
 
 
@@ -293,15 +301,16 @@
 
     @pl.when(super_block(place) == 1)
     def _():
-        tail = got_ref[3 * rows : 3 * rows + EDGE].astype(F32)
+        at = rows // 2 + 2 * rows
+        tail = got_ref[at:].astype(F32)
         slab = missing(tap_ref, tail, raw_ref[:EDGE].astype(F32))
         end = end_ref[...] + rest_ref[...] * to_states(table_ref, slab)
-        end = end + jump_ref[...] * join_three(got_ref[:rows], width)
-        state = split_three(end, width)
-        short_ref[:rows] = state
-        short_ref[rows:] = send_ref[3 * rows : 3 * rows + EDGE]
-        next_ref[:rows] = state
-        next_ref[rows:] = send_ref[rows:]
+        end = end + jump_ref[...] * unpack_state(got_ref[: rows // 2], width)
+        state = pack_state(end, width)
+        short_ref[: rows // 2] = state
+        short_ref[rows // 2 :] = send_ref[at : at + EDGE]
+        next_ref[: rows // 2] = state
+        next_ref[rows // 2 :] = send_ref[rows // 2 : at + EDGE]
 
 
 def spread(width, state, step, table, blocks, added=None):
@@ -314,41 +323,47 @@
     return dot(two_parts(jnp.concatenate(states, 0), width), table)
 
 
+def joined(width, got, local_ref, raw_ref, tap_ref, table_ref, step_ref):
+    count = table_ref.shape[0]
+    rows = 8 * count
+    blocks = local_ref.shape[0] // rows
+    one, two, end = rows // 2, rows // 2 + rows, rows // 2 + 2 * rows
+    own_slab = missing(tap_ref, got[end : end + EDGE], raw_ref[:EDGE].astype(F32))
+    incoming = unpack_state(got[:one], width)
+    added = to_states(table_ref, own_slab)
+    zeros = jnp.zeros((8, LANES), F32)
+    parts = []
+    for q in range(count):
+        at = slice(8 * q, 8 * q + 8)
+        mixed = spread(width, incoming[at], step_ref[at], table_ref[q, 6], blocks, added[at])
+        last_but_one, last, first = got[one:two][at], got[two:end][at], own_slab[at]
+        now = jnp.concatenate([first, zeros, zeros, zeros], 0).astype(BF16)
+        before = jnp.concatenate([last, first, zeros, zeros], 0).astype(BF16)
+        earlier = jnp.concatenate([last_but_one, last, first, zeros], 0).astype(BF16)
+        start = dot(now, table_ref[q, 0]) + dot(now, table_ref[q, 1])
+        start = start + dot(before, table_ref[q, 2]) + dot(earlier, table_ref[q, 3])
+        mixed = jnp.concatenate([mixed[:32] + start, mixed[32:]], 0)
+        parts.append(mixed.reshape(blocks, 8, LANES))
+    return local_ref[...] + jnp.concatenate(parts, 1).reshape(local_ref.shape)
+
+
 def join_kernel(
-    width, place, local_ref, got_01, got_23, got_12, raw_ref, tap_ref, table_ref, step_ref, out_ref
+    width, place, local_ref, got_01, got_23, raw_ref, tap_ref, table_ref, step_ref, out_ref
 ):
-    @pl.when(super_block(place) > 0)
+    @pl.when(lax.rem(super_block(place), 2) == 1)
     def _():
-        count = table_ref.shape[0]
-        rows = 8 * count
-        blocks = local_ref.shape[0] // rows
-        got = got_01[...].astype(F32) + got_23[...].astype(F32) + got_12[...].astype(F32)
-        edge = slice(3 * rows, 3 * rows + EDGE)
-        own_slab = missing(tap_ref, got[edge], raw_ref[:EDGE].astype(F32))
-        incoming = join_three(got[:rows], width)
-        added = to_states(table_ref, own_slab)
-        zeros = jnp.zeros((8, LANES), F32)
-        parts = []
-        for q in range(count):
-            at = slice(8 * q, 8 * q + 8)
-            mixed = spread(width, incoming[at], step_ref[at], table_ref[q, 6], blocks, added[at])
-            last_but_one, last, first = got[rows:][at], got[2 * rows :][at], own_slab[at]
-            now = jnp.concatenate([first, zeros, zeros, zeros], 0).astype(BF16)
-            before = jnp.concatenate([last, first, zeros, zeros], 0).astype(BF16)
-            earlier = jnp.concatenate([last_but_one, last, first, zeros], 0).astype(BF16)
-            start = dot(now, table_ref[q, 0]) + dot(now, table_ref[q, 1])
-            start = start + dot(before, table_ref[q, 2]) + dot(earlier, table_ref[q, 3])
-            mixed = jnp.concatenate([mixed[:32] + start, mixed[32:]], 0)
-            parts.append(mixed.reshape(blocks, 8, LANES))
-        out_ref[...] = local_ref[...] + jnp.concatenate(parts, 1).reshape(local_ref.shape)
+        got = got_01[...].astype(F32) + got_23[: got_01.shape[0]].astype(F32)
+        out_ref[...] = joined(width, got, local_ref, raw_ref, tap_ref, table_ref, step_ref)
 
 
 def finish_kernel(
     width,
     place,
     near_ref,
+    got_12,
     got_23,
     got_13,
+    raw_ref,
     tap_ref,
     table_ref,
     step_ref,
@@ -358,19 +373,25 @@
 ):
     here = super_block(place)
 
-    @pl.when(here != 3)
+    @pl.when(here < 2)
     def _():
         out_ref[...] = near_ref[...].astype(BF16)
+
+    @pl.when(here == 2)
+    def _():
+        got = got_12[...].astype(F32)
+        total = joined(width, got, near_ref, raw_ref, tap_ref, table_ref, step_ref)
+        out_ref[...] = total.astype(BF16)
 
     @pl.when(here == 3)
     def _():
         count = table_ref.shape[0]
         rows = 8 * count
         blocks = near_ref.shape[0] // rows
-        far_tail = got_13[rows:].astype(F32)
-        far_slab = missing(tap_ref, far_tail, got_23[3 * rows + EDGE :].astype(F32))
-        incoming = rest_ref[...] * to_states(table_ref, far_slab)
-        incoming = incoming + jump_ref[...] * join_three(got_13[:rows], width)
+        far_tail = got_13[rows // 2 :].astype(F32)
+        head = got_23[got_23.shape[0] - EDGE :].astype(F32)
+        incoming = rest_ref[...] * to_states(table_ref, missing(tap_ref, far_tail, head))
+        incoming = incoming + jump_ref[...] * unpack_state(got_13[: rows // 2], width)
         parts = []
         for q in range(count):
             at = slice(8 * q, 8 * q + 8)
@@ -446,24 +467,17 @@
     pack = 8 * count
     with_width = lambda kernel: functools.partial(kernel, width)
 
-    steps = 4
-    part = pl.BlockSpec((rows, channels // steps), lambda i: (0, i))
+    part = pl.BlockSpec((rows, channels), lambda i: (0, 0))
     raw, outer_tail = pl.pallas_call(
         pack_kernel,
-        grid=(steps,),
+        grid=(1,),
         in_specs=[
             part,
             part,
-            pl.BlockSpec((HALO, channels // steps), lambda i: (rows // HALO - 1, i)),
+            pl.BlockSpec((HALO, channels), lambda i: (rows // HALO - 1, 0)),
         ],
-        out_specs=[
-            pl.BlockSpec((NEAR * rows // steps, LANES), lambda i: (i, 0)),
-            pl.BlockSpec((HALO, channels // steps), lambda i: (0, i)),
-        ],
-        out_shape=[
-            jax.ShapeDtypeStruct((NEAR * rows, LANES), BF16),
-            jax.ShapeDtypeStruct((HALO, channels), BF16),
-        ],
+        out_specs=[vmem, vmem],
+        out_shape=[pltpu.VMEM((NEAR * rows, LANES), BF16), pltpu.VMEM((HALO, channels), BF16)],
         name="pack",
     )(inner_input, value_input, outer_input)
     neighbours = [[NEAR * f + n for n in range(NEAR)] for f in range(far)]
@@ -502,7 +516,8 @@
         feature_taps,
         scratch=[pltpu.VMEM((tiles, HALO + rows, LANES), F32)],
     )
-    packet = pltpu.VMEM((3 * pack + 2 * EDGE, LANES), BF16)
+    packet = pltpu.VMEM((pack // 2 + 2 * pack + EDGE, LANES), BF16)
+    with_head = pltpu.VMEM((pack // 2 + 2 * pack + 2 * EDGE, LANES), BF16)
     whole = pltpu.VMEM((slab_rows, LANES), F32)
     ends = pltpu.VMEM((pack, LANES), F32)
     scratch = [pltpu.VMEM((HALO + NEAR * rows, LANES), F32), whole]
@@ -516,7 +531,7 @@
     )
     local, end, packed = call(
         with_width(later_states_kernel),
-        [whole, ends, packet],
+        [whole, ends, with_head],
         *known,
         local,
         scalars=(place,),
@@ -534,7 +549,7 @@
     got_23 = passed(packed, 2, 3)
     state, repacked = call(
         with_width(chain_kernel),
-        [pltpu.VMEM((pack + EDGE, LANES), BF16), packet],
+        [pltpu.VMEM((pack // 2 + EDGE, LANES), BF16), packet],
         got_01,
         arrived,
         taps,
@@ -553,7 +568,6 @@
         local,
         got_01,
         got_23,
-        got_12,
         arrived,
         taps,
         table,
@@ -565,8 +579,10 @@
         with_width(finish_kernel),
         pltpu.VMEM((slab_rows, LANES), BF16),
         near,
+        got_12,
         got_23,
         got_13,
+        arrived,
         taps,
         table,
         step,

time: 64.4 us -> 62.9 us (0.977)
  Pallas kernels: 7.26 us -> 6.05 us
    pallas_call x1, Pallas kernels: 2.99 us -> 1.8 us  [on_device(): pl.pallas_call(pack_kernel, grid=(1,), in_specs=[part, part, pl.BlockSpec...]
where the time goes in v8:
time: 62.9 us; the launch traced here: 62.5 us
  blocking collectives  22.6 us (36%)
  waiting for transfers between devices  19.8 us (31%)
  starting transfers between devices  13.8 us (22%)
  Pallas kernels  6.05 us (10%)
    ppermute x4, waiting for transfers between devices, passed(): return lax.ppermute(x, 'ctx', pairs)  14 us
    all_to_all x1, blocking collectives, exchange(): lax.all_to_all(x.reshape(slab), 'ctx', 0, 0, axis_index_groups=neighbours)  12.9 us
    all_to_all x1, blocking collectives, on_device(): all_sums = lax.all_to_all(sums.reshape(parts, 8, LANES), 'tp', 0, 0)  9.72 us
    all_to_all x1, starting transfers between devices, exchange(): lax.all_to_all(x.reshape(slab), 'ctx', 0, 0, axis_index_groups=neighbours)  5.91 us
    ppermute x1, waiting for transfers between devices, on_device(): lax.ppermute(outer_tail, 'ctx', [(i, i + 1) for i in range(size - 1)])  4.94 us
    pallas_call x9, Pallas kernels, call(): pl.pallas_call(kernel, in_specs=[smem] * len(scalars) + [vmem] * len(arra...  4.25 us
    ppermute x4, starting transfers between devices, passed(): return lax.ppermute(x, 'ctx', pairs)  4.03 us
    ppermute x1, starting transfers between devices, on_device(): lax.ppermute(outer_tail, 'ctx', [(i, i + 1) for i in range(size - 1)])  3.83 us
  transfers between devices with their start and end apart: 6, of which 4 were waited for; matrix products, arithmetic and copies ran while one was open for 0% of the time, Pallas kernels for 4%

profile of v8, /device:TPU:384, one launch (start us, length us, event | category | flops | bytes accessed | tf_op | source)
XLA Modules:
  0.0 62.5 jit_solution(4713956040455317857)
XLA Ops:
  0.0 1.8 %pack.1 = (bf16[1024,128]{1,0:T(8,128)(2,1)}, bf16[8,1024]{1,0:T(8,128)(2,1)S(1)}) custom-call(bf16[64,1024]{1,0:T(8,128)(2,1)} %inner_ref.1, bf16[64,1024]{1,0:T(8,128)(2,1)} %value_ref.1, bf16[64,1024]{1,0:T(8,128)(2,1)} %outer_ref.3), custom_call_target="tpu_custom_call" | custom-call | tf_op jit(solution)/shard_map/pack/pallas_call | solution.py:471
  1.8 5.9 %all-to-all-start = ((bf16[16,64,128]{2,1,0:T(8,128)(2,1)}), bf16[16,64,128]{2,1,0:T(8,128)(2,1)S(1)}, u32[]{:S(2)}, u32[]{:S(2)}) async-start(bf16[16,64,128]{2,1,0:T(8,128)(2,1)} %bitcast.1), calls=%async_computation | async-start | bytes 524288 | tf_op jit(solution)/shard_map/all_to_all | solution.py:487
  7.7 0.0 copy-start.3
  7.7 3.8 %collective-permute-start = (bf16[8,1024]{1,0:T(8,128)(2,1)S(1)}, bf16[8,1024]{1,0:T(8,128)(2,1)S(1)}, u32[]{:S(2)}, u32[]{:S(2)}) collective-permute-start(bf16[8,1024]{1,0:T(8,128)(2,1)S(1)} %get-tuple-element.27), channel_id=1, source_target_pairs={{0,8},{8,16},{16,24},{24,32},{32,40},{40,48},{48,56},{56,64},{64,7... | collective-permute-start | bytes 49160 | tf_op jit(solution)/shard_map/ppermute | solution.py:491
  11.7 0.9 %shard_map.91 = (bf16[4,7,128,128]{3,2,1,0:T(8,128)(2,1)S(1)}, f32[32,128]{1,0:T(8,128)S(1)}, f32[32,128]{1,0:T(8,128)S(1)}, f32[32,128]{1,0:T(8,128)S(1)}, f32[7,128]{1,0:T(8,128)S(1)}, /*index=5*/f32[1,1024]{1,0:T(1,128)S(1)}) custom-call(s32[1]{0:T(128)} %bitcast.place, f32[16,64]{1,0:T(8,128)S(1)} %bitcast.20, f32[16,64]{1,0:T(8,128)S(1)} %bitcast.21, ...), custom_call_target="tpu_custom_call" | custom-call | tf_op jit(solution)/shard_map/pallas_call | solution.py:453
  12.6 4.9 %collective-permute-done.halo_ref = bf16[8,1024]{1,0:T(8,128)(2,1)S(1)} collective-permute-done((bf16[8,1024]{1,0:T(8,128)(2,1)S(1)}, bf16[8,1024]{1,0:T(8,128)(2,1)S(1)}, u32[]{:S(2)}, u32[]{:S(2)}) %collective-permute-start) | collective-permute-done | bytes 16416 | tf_op jit(solution)/shard_map/ppermute | solution.py:491
  17.5 0.9 %all-to-all-done = bf16[16,64,128]{2,1,0:T(8,128)(2,1)S(1)} async-done(((bf16[16,64,128]{2,1,0:T(8,128)(2,1)}), bf16[16,64,128]{2,1,0:T(8,128)(2,1)S(1)}, u32[]{:S(2)}, u32[]{:S(2)}) %all-to-all-start) | async-done | bytes 262176 | tf_op jit(solution)/shard_map/all_to_all | solution.py:487
  18.4 0.7 %collective-permute-start.1 = (bf16[88,128]{1,0:T(8,128)(2,1)S(1)}, bf16[88,128]{1,0:T(8,128)(2,1)S(1)}, u32[]{:S(2)}, u32[]{:S(2)}) collective-permute-start(bf16[88,128]{1,0:T(8,128)(2,1)S(1)} %get-tuple-element.36), channel_id=1, source_target_pairs={{0,128},{8,136},{16,144},{24,152},{32,160},{40,168},{48,176},{56,1... | collective-permute-start | bytes 67592 | tf_op jit(solution)/shard_map/ppermute | solution.py:546
  19.1 0.9 %shard_map.93 = (f32[512,128]{1,0:T(8,128)S(1)}, f32[32,128]{1,0:T(8,128)S(1)}, bf16[96,128]{1,0:T(8,128)(2,1)S(1)}) custom-call(s32[1]{0:T(128)} %bitcast.place, bf16[1024,128]{1,0:T(8,128)(2,1)S(1)} %bitcast.11, f32[7,128]{1,0:T(8,128)S(1)} %get-tuple-element.29.refs_1_.tap_ref, ...), custom_call_target="tpu_custom_call", output_to_operand_aliasing={{0}: (5, {})} | custom-call | tf_op jit(solution)/shard_map/pallas_call | solution.py:453
  20.0 1.3 %collective-permute-start.2 = (bf16[96,128]{1,0:T(8,128)(2,1)S(1)}, bf16[96,128]{1,0:T(8,128)(2,1)S(1)}, u32[]{:S(2)}, u32[]{:S(2)}) collective-permute-start(bf16[96,128]{1,0:T(8,128)(2,1)S(1)} %get-tuple-element.37.send_ref), channel_id=1, source_target_pairs={{256,384},{264,392},{272,400},{280,408},{288,416},{296,424},{304,4... | collective-permute-start | bytes 73736 | tf_op jit(solution)/shard_map/ppermute | solution.py:546
  21.3 0.0 copy-start
  21.4 0.8 %collective-permute-start.3 = (bf16[88,128]{1,0:T(8,128)(2,1)S(1)}, bf16[88,128]{1,0:T(8,128)(2,1)S(1)}, u32[]{:S(2)}, u32[]{:S(2)}) collective-permute-start(bf16[88,128]{1,0:T(8,128)(2,1)S(1)} %get-tuple-element.41), channel_id=1, source_target_pairs={{128,256},{136,264},{144,272},{152,280},{160,288},{168,296},{176,3... | collective-permute-start | bytes 67592 | tf_op jit(solution)/shard_map/ppermute | solution.py:546
  22.2 1.3 %collective-permute-start.4 = (bf16[24,128]{1,0:T(8,128)(2,1)S(1)}, bf16[24,128]{1,0:T(8,128)(2,1)S(1)}, u32[]{:S(2)}, u32[]{:S(2)}) collective-permute-start(bf16[24,128]{1,0:T(8,128)(2,1)S(1)} %get-tuple-element.42), channel_id=1, source_target_pairs={{128,384},{136,392},{144,400},{152,408},{160,416},{168,424},{176,4... | collective-permute-start | bytes 18440 | tf_op jit(solution)/shard_map/ppermute | solution.py:546
  23.5 0.2 shard_map.94.outer_ref
  23.6 6.0 %collective-permute-done.2.got_23 = bf16[96,128]{1,0:T(8,128)(2,1)S(1)} collective-permute-done((bf16[96,128]{1,0:T(8,128)(2,1)S(1)}, bf16[96,128]{1,0:T(8,128)(2,1)S(1)}, u32[]{:S(2)}, u32[]{:S(2)}) %collective-permute-start.2) | collective-permute-done | bytes 24608 | tf_op jit(solution)/shard_map/ppermute | solution.py:546
  29.6 0.6 shard_map.95.near_ref
  30.3 7.9 %collective-permute-done.4.got_13 = bf16[24,128]{1,0:T(8,128)(2,1)S(1)} collective-permute-done((bf16[24,128]{1,0:T(8,128)(2,1)S(1)}, bf16[24,128]{1,0:T(8,128)(2,1)S(1)}, u32[]{:S(2)}, u32[]{:S(2)}) %collective-permute-start.4) | collective-permute-done | bytes 6176 | tf_op jit(solution)/shard_map/ppermute | solution.py:546
  38.2 0.0 collective-permute-done.3.got_12
  38.2 0.5 shard_map.97
  38.7 0.0 copy-start.2
  38.7 12.9 %all_to_all.15 = bf16[16,32,128]{2,1,0:T(8,128)(2,1)S(1)} all-to-all(bf16[16,32,128]{2,1,0:T(8,128)(2,1)S(1)} %bitcast.15), channel_id=1, replica_groups={{0,8,16,24,32,40,48,56,64,72,80,88,96,104,112,120},{128,136,144,152,160..., dimensions={0} | all-to-all | bytes 262144 | tf_op jit(solution)/shard_map/all_to_all | solution.py:487
  51.7 0.3 shard_map.98
  52.0 9.7 %all_to_all.16 = f32[8,8,128]{2,1,0:T(8,128)S(1)} all-to-all(f32[8,8,128]{2,1,0:T(8,128)S(1)} %bitcast.18), channel_id=1, replica_groups=mesh['ctx'=64,'tp'=8] {'tp'}, dimensions={0} | all-to-all | bytes 65536 | tf_op jit(solution)/shard_map/all_to_all | solution.py:600
  61.7 0.8 %shard_map.99 = bf16[64,1024]{1,0:T(8,128)(2,1)} custom-call(f32[64,1024]{1,0:T(8,128)S(1)} %get-tuple-element.44.hidden_ref, f32[64,128]{1,0:T(8,128)S(1)} %bitcast.17, f32[1,1024]{1,0:T(1,128)S(1)} %get-tuple-element.46.gain_ref), custom_call_target="tpu_custom_call" | custom-call | tf_op jit(solution)/shard_map/pallas_call | solution.py:453
  (15 shorter events, 0.0 us)
Async XLA Ops:
  1.8 9.8 %copy-start.6 = (bf16[1024]{0:T(1024)(128)(2,1)S(1)}, bf16[1024]{0:T(1024)(128)(2,1)}, u32[]{:S(2)}) copy-start(bf16[1024]{0:T(1024)(128)(2,1)} %param.17) | copy-start | bytes 6148
  1.8 9.8 %copy-start.1 = (bf16[3,7,1024]{2,1,0:T(8,128)(2,1)S(1)}, bf16[3,7,1024]{2,1,0:T(8,128)(2,1)}, u32[]{:S(2)}) copy-start(bf16[3,7,1024]{2,1,0:T(8,128)(2,1)} %tap_ref.3) | copy-start | bytes 129028
  1.8 9.8 %copy-start.4 = (f32[64,16]{0,1:T(8,128)S(1)}, f32[64,16]{0,1:T(8,128)}, u32[]{:S(2)}) copy-start(f32[64,16]{0,1:T(8,128)} %param.14) | copy-start | bytes 12292
  1.8 9.8 %copy-start.5 = (f32[64,16]{0,1:T(8,128)S(1)}, f32[64,16]{0,1:T(8,128)}, u32[]{:S(2)}) copy-start(f32[64,16]{0,1:T(8,128)} %param.15) | copy-start | bytes 12292
  1.8 16.6 %all-to-all-start = ((bf16[16,64,128]{2,1,0:T(8,128)(2,1)}), bf16[16,64,128]{2,1,0:T(8,128)(2,1)S(1)}, u32[]{:S(2)}, u32[]{:S(2)}) async-start(bf16[16,64,128]{2,1,0:T(8,128)(2,1)} %bitcast.1), calls=%async_computation | async-start | bytes 524288 | tf_op jit(solution)/shard_map/all_to_all | solution.py:487
  7.7 3.9 %copy-start.3 = (bf16[128,64]{0,1:T(8,128)(2,1)S(1)}, bf16[128,64]{0,1:T(8,128)(2,1)}, u32[]{:S(2)}) copy-start(bf16[128,64]{0,1:T(8,128)(2,1)} %param.13) | copy-start | bytes 49156
  7.7 9.7 %collective-permute-start = (bf16[8,1024]{1,0:T(8,128)(2,1)S(1)}, bf16[8,1024]{1,0:T(8,128)(2,1)S(1)}, u32[]{:S(2)}, u32[]{:S(2)}) collective-permute-start(bf16[8,1024]{1,0:T(8,128)(2,1)S(1)} %get-tuple-element.27), channel_id=1, source_target_pairs={{0,8},{8,16},{16,24},{24,32},{32,40},{40,48},{48,56},{56,64},{64,7... | collective-permute-start | bytes 49160 | tf_op jit(solution)/shard_map/ppermute | solution.py:491
  18.4 2.9 %collective-permute-start.1 = (bf16[88,128]{1,0:T(8,128)(2,1)S(1)}, bf16[88,128]{1,0:T(8,128)(2,1)S(1)}, u32[]{:S(2)}, u32[]{:S(2)}) collective-permute-start(bf16[88,128]{1,0:T(8,128)(2,1)S(1)} %get-tuple-element.36), channel_id=1, source_target_pairs={{0,128},{8,136},{16,144},{24,152},{32,160},{40,168},{48,176},{56,1... | collective-permute-start | bytes 67592 | tf_op jit(solution)/shard_map/ppermute | solution.py:546
  20.0 9.6 %collective-permute-start.2 = (bf16[96,128]{1,0:T(8,128)(2,1)S(1)}, bf16[96,128]{1,0:T(8,128)(2,1)S(1)}, u32[]{:S(2)}, u32[]{:S(2)}) collective-permute-start(bf16[96,128]{1,0:T(8,128)(2,1)S(1)} %get-tuple-element.37.send_ref), channel_id=1, source_target_pairs={{256,384},{264,392},{272,400},{280,408},{288,416},{296,424},{304,4... | collective-permute-start | bytes 73736 | tf_op jit(solution)/shard_map/ppermute | solution.py:546
  21.3 2.1 %copy-start = (bf16[64,1024]{1,0:T(8,128)(2,1)S(1)}, bf16[64,1024]{1,0:T(8,128)(2,1)}, u32[]{:S(2)}) copy-start(bf16[64,1024]{1,0:T(8,128)(2,1)} %outer_ref.3) | copy-start | bytes 393220
  21.4 16.8 %collective-permute-start.3 = (bf16[88,128]{1,0:T(8,128)(2,1)S(1)}, bf16[88,128]{1,0:T(8,128)(2,1)S(1)}, u32[]{:S(2)}, u32[]{:S(2)}) collective-permute-start(bf16[88,128]{1,0:T(8,128)(2,1)S(1)} %get-tuple-element.41), channel_id=1, source_target_pairs={{128,256},{136,264},{144,272},{152,280},{160,288},{168,296},{176,3... | collective-permute-start | bytes 67592 | tf_op jit(solution)/shard_map/ppermute | solution.py:546
  22.2 16.0 %collective-permute-start.4 = (bf16[24,128]{1,0:T(8,128)(2,1)S(1)}, bf16[24,128]{1,0:T(8,128)(2,1)S(1)}, u32[]{:S(2)}, u32[]{:S(2)}) collective-permute-start(bf16[24,128]{1,0:T(8,128)(2,1)S(1)} %get-tuple-element.42), channel_id=1, source_target_pairs={{128,384},{136,392},{144,400},{152,408},{160,416},{168,424},{176,4... | collective-permute-start | bytes 18440 | tf_op jit(solution)/shard_map/ppermute | solution.py:546
  38.7 12.9 %copy-start.2 = (bf16[64,1024]{1,0:T(8,128)(2,1)S(1)}, bf16[64,1024]{1,0:T(8,128)(2,1)}, u32[]{:S(2)}) copy-start(bf16[64,1024]{1,0:T(8,128)(2,1)} %residual_ref.1) | copy-start | bytes 393220

commit v9 on v8

--- a/solution.py
+++ b/solution.py
@@ -67,15 +67,12 @@
     residue_ref,
     medium_ref,
     tap_ref,
-    gain_in,
     table_ref,
     step_ref,
     jump_ref,
     rest_ref,
     mine_ref,
-    gain_ref,
 ):
-    gain_ref[...] = gain_in[...].astype(F32)
     channels = tap_ref.shape[2]
     half = LANES // 2
     at, to = iota((channels, LANES), 0), iota((channels, LANES), 1)
@@ -136,6 +133,11 @@
         rest_ref[rows] = jnp.broadcast_to(jnp.exp(-rate_lanes * (block * (NEAR - 1))), (8, LANES))
 
 
+def begin_kernel(place, inner, value, outer, decay, residue, medium, taps, raw, tail, *tables):
+    pack_kernel(inner, value, outer, raw, tail)
+    tables_kernel(place, decay, residue, medium, taps, *tables)
+
+
 def featurized(tap_ref, which, lanes, padded, rows):
     total = None
     for k in range(tap_ref.shape[1]):
@@ -163,7 +165,8 @@
         out_ref[(2 * tile + 1) * rows : (2 * tile + 2) * rows] = second.astype(BF16)
 
 
-def outer_kernel(halo_ref, outer_ref, tap_ref, out_ref, padded):
+def outer_kernel(halo_ref, outer_ref, tap_ref, gain_in, out_ref, gain_ref, padded):
+    gain_ref[...] = gain_in[...].astype(F32)
     rows, channels = outer_ref.shape
     for tile in range(channels // LANES):
         lanes = tile_lanes(tile)
@@ -259,7 +262,7 @@
     send_ref[at : at + 2 * rows] = wide[(blocks - 2) * rows :].astype(BF16)
     at = at + 2 * rows
     send_ref[at : at + EDGE] = raw_ref[blocks * block - EDGE :]
-    if later:
+    if send_ref.shape[0] > at + EDGE:
         send_ref[at + EDGE :] = raw_ref[:EDGE]
     find_local(width, wide, table_ref, state_ref[...], local_ref)
 
@@ -268,19 +271,20 @@
     return lax.div(place[0], NEAR)
 
 
-def first_states_kernel(width, place, *refs):
-    raw_ref, tap_ref, table_ref, step_ref, local_ref, send_ref, padded, state_ref, end_ref = refs
-
-    @pl.when(super_block(place) == 0)
+def states_kernel(width, turn, place, raw_ref, tap_ref, table_ref, step_ref, *refs):
+    if turn > 0:
+        refs = refs[1:]
+    if turn == 1:
+        local_ref, end_ref, send_ref, padded, state_ref = refs
+    elif turn == 3:
+        local_ref, padded, state_ref, end_ref, send_ref = refs
+    else:
+        local_ref, send_ref, padded, state_ref, end_ref = refs
+
+    @pl.when(super_block(place) == turn)
     def _():
         known = (raw_ref, tap_ref, table_ref, step_ref)
-        find_states(width, False, *known, local_ref, end_ref, send_ref, padded, state_ref)
-
-
-def later_states_kernel(width, place, raw_ref, tap_ref, table_ref, step_ref, local_in, *refs):
-    @pl.when(super_block(place) > 0)
-    def _():
-        find_states(width, True, raw_ref, tap_ref, table_ref, step_ref, *refs)
+        find_states(width, turn > 0, *known, local_ref, end_ref, send_ref, padded, state_ref)
 
 
 def chain_kernel(
@@ -467,19 +471,32 @@
     pack = 8 * count
     with_width = lambda kernel: functools.partial(kernel, width)
 
+    place = lax.axis_index("ctx").reshape(1).astype(jnp.int32)
+    small = (decay_rates.T, residues.T, medium_taps.T, feature_taps)
     part = pl.BlockSpec((rows, channels), lambda i: (0, 0))
-    raw, outer_tail = pl.pallas_call(
-        pack_kernel,
+    lines = pltpu.VMEM((pack, LANES), F32)
+    raw, outer_tail, table, step, jump, rest, taps = pl.pallas_call(
+        begin_kernel,
         grid=(1,),
         in_specs=[
+            smem,
             part,
             part,
             pl.BlockSpec((HALO, channels), lambda i: (rows // HALO - 1, 0)),
+            *[pl.BlockSpec(x.shape, lambda i, n=x.ndim: (0,) * n) for x in small],
         ],
-        out_specs=[vmem, vmem],
-        out_shape=[pltpu.VMEM((NEAR * rows, LANES), BF16), pltpu.VMEM((HALO, channels), BF16)],
-        name="pack",
-    )(inner_input, value_input, outer_input)
+        out_specs=[vmem] * 7,
+        out_shape=[
+            pltpu.VMEM((NEAR * rows, LANES), BF16),
+            pltpu.VMEM((HALO, channels), BF16),
+            pltpu.VMEM((count, 7, LANES, LANES), BF16),
+            lines,
+            lines,
+            lines,
+            pltpu.VMEM((FEAT, LANES), F32),
+        ],
+        name="begin",
+    )(place, inner_input, value_input, outer_input, *small)
     neighbours = [[NEAR * f + n for n in range(NEAR)] for f in range(far)]
 
     def exchange(x):
@@ -487,66 +504,41 @@
         y = lax.all_to_all(x.reshape(slab), "ctx", 0, 0, axis_index_groups=neighbours)
         return y.reshape(x.shape)
 
-    arrived = exchange(raw)
-    halo = lax.ppermute(outer_tail, "ctx", [(i, i + 1) for i in range(size - 1)])
-    arrived, halo = lax.optimization_barrier((arrived, halo))
-    place = lax.axis_index("ctx").reshape(1).astype(jnp.int32)
-    table, step, jump, rest, taps, gain = call(
-        tables_kernel,
-        [
-            pltpu.VMEM((count, 7, LANES, LANES), BF16),
-            pltpu.VMEM((pack, LANES), F32),
-            pltpu.VMEM((pack, LANES), F32),
-            pltpu.VMEM((pack, LANES), F32),
-            pltpu.VMEM((FEAT, LANES), F32),
-            pltpu.VMEM((1, channels), F32),
-        ],
-        decay_rates.T,
-        residues.T,
-        medium_taps.T,
-        feature_taps,
-        norm_gain.reshape(1, channels),
-        scalars=(place,),
-    )
-    outer_feat = call(
-        outer_kernel,
-        pltpu.VMEM((rows, channels), F32),
-        halo,
-        outer_input,
-        feature_taps,
-        scratch=[pltpu.VMEM((tiles, HALO + rows, LANES), F32)],
-    )
     packet = pltpu.VMEM((pack // 2 + 2 * pack + EDGE, LANES), BF16)
     with_head = pltpu.VMEM((pack // 2 + 2 * pack + 2 * EDGE, LANES), BF16)
     whole = pltpu.VMEM((slab_rows, LANES), F32)
     ends = pltpu.VMEM((pack, LANES), F32)
     scratch = [pltpu.VMEM((HALO + NEAR * rows, LANES), F32), whole]
-    known = (arrived, taps, table, step)
-    local, first_packed = call(
-        with_width(first_states_kernel),
-        [whole, packet],
-        *known,
-        scalars=(place,),
-        scratch=scratch + [ends],
-    )
-    local, end, packed = call(
-        with_width(later_states_kernel),
-        [whole, ends, with_head],
-        *known,
-        local,
-        scalars=(place,),
-        scratch=scratch,
-        aliases={5: 0},
-    )
-
-    local, outer_feat = lax.optimization_barrier((local, outer_feat))
+    here = lax.axis_index("ctx") // NEAR
+    swap = lambda kept, fresh: exchange(fresh)
+    keep = lambda kept, fresh: kept
+
+    def find(turn, arrived, local, outs):
+        unread = {1: [], 3: [ends, packet]}.get(turn, [ends])
+        return call(
+            functools.partial(states_kernel, width, turn),
+            outs,
+            arrived,
+            taps,
+            table,
+            step,
+            *([] if turn == 0 else [local]),
+            scalars=(place,),
+            scratch=scratch + unread,
+            aliases={} if turn == 0 else {5: 0},
+        )
 
     def passed(x, start, end):
         pairs = [(NEAR * start + n, NEAR * end + n) for n in range(NEAR)]
         return lax.ppermute(x, "ctx", pairs)
 
+    arrived = lax.cond(here == 0, lambda x: exchange(x), lambda x: x, raw)
+    local, first_packed = find(0, arrived, None, [whole, packet])
     got_01 = passed(first_packed, 0, 1)
-    got_23 = passed(packed, 2, 3)
+    outer_tail, arrived = lax.optimization_barrier((outer_tail, arrived))
+    halo = lax.ppermute(outer_tail, "ctx", [(i, i + 1) for i in range(size - 1)])
+    arrived = lax.cond(here == 1, swap, keep, arrived, raw)
+    local, end, packed = find(1, arrived, local, [whole, ends, packet])
     state, repacked = call(
         with_width(chain_kernel),
         [pltpu.VMEM((pack // 2 + EDGE, LANES), BF16), packet],
@@ -562,6 +554,24 @@
     )
     got_13 = passed(state, 1, 3)
     got_12 = passed(repacked, 1, 2)
+    arrived = lax.cond(here == 2, swap, keep, arrived, raw)
+    local, packed = find(2, arrived, local, [whole, with_head])
+    got_23 = passed(packed, 2, 3)
+    arrived = lax.cond(here == 3, swap, keep, arrived, raw)
+    (local,) = find(3, arrived, local, [whole])
+    norm_gain, local = lax.optimization_barrier((norm_gain, local))
+    outer_feat, gain = call(
+        outer_kernel,
+        [pltpu.VMEM((rows, channels), F32), pltpu.VMEM((1, channels), F32)],
+        halo,
+        outer_input,
+        feature_taps,
+        norm_gain.reshape(1, channels),
+        scratch=[pltpu.VMEM((tiles, HALO + rows, LANES), F32)],
+    )
+
+    local, outer_feat, gain = lax.optimization_barrier((local, outer_feat, gain))
+
     near = call(
         with_width(join_kernel),
         whole,

time: 62.9 us -> 66.2 us (1.052)
  the two profiles are of different devices: /device:TPU:384 before, /device:TPU:1 now
where the time goes in v9:
time: 66.2 us; the launch traced here: 65.9 us
  blocking collectives  55 us (83%)
  starting transfers between devices  5.4 us (8%)
  Pallas kernels  4.24 us (6%)
  local copies, waits for them, and re-layouts  0.9 us (1%)
    all_to_all x2, blocking collectives, exchange(): lax.all_to_all(x.reshape(slab), 'ctx', 0, 0, axis_index_groups=neighbours)  41.9 us
    all_to_all x1, blocking collectives, on_device(): all_sums = lax.all_to_all(sums.reshape(parts, 8, LANES), 'tp', 0, 0)  13 us
    ppermute x4, starting transfers between devices, passed(): return lax.ppermute(x, 'ctx', pairs)  3.27 us
    pallas_call x10, Pallas kernels, call(): pl.pallas_call(kernel, in_specs=[smem] * len(scalars) + [vmem] * len(arra...  2.3 us
    ppermute x1, starting transfers between devices, on_device(): lax.ppermute(outer_tail, 'ctx', [(i, i + 1) for i in range(size - 1)])  2.14 us
    pallas_call x1, Pallas kernels, on_device(): pl.pallas_call(begin_kernel, grid=(1,), in_specs=[smem, part, part, pl.Bl...  1.94 us
  transfers between devices with their start and end apart: 5, of which 1 were waited for; matrix products, arithmetic and copies ran while one was open for 0% of the time, Pallas kernels for 0%

profile of v9, /device:TPU:1, one launch (start us, length us, event | category | flops | bytes accessed | tf_op | source)
XLA Modules:
  0.0 65.9 jit_solution(3775340667968777298)
XLA Ops:
  0.0 1.9 %begin.1 = (bf16[1024,128]{1,0:T(8,128)(2,1)S(1)}, bf16[8,1024]{1,0:T(8,128)(2,1)S(1)}, bf16[4,7,128,128]{3,2,1,0:T(8,128)(2,1)S(1)}, f32[32,128]{1,0:T(8,128)S(...) custom-call(s32[1]{0:T(128)} %bitcast.8.place, bf16[64,1024]{1,0:T(8,128)(2,1)} %inner.1, ...), custom_call_target="tpu_custom_call" | custom-call | tf_op jit(solution)/shard_map/begin/pallas_call | solution.py:478
  1.9 18.4 %conditional.4 = (bf16[1024,128]{1,0:T(8,128)(2,1)S(1)}) conditional(s32[]{:T(128)} %convert_element_type.15, bf16[1024,128]{1,0:T(8,128)(2,1)S(1)} %get-tuple-element.53, bf16[1024,128]{1,0:T(8,128)(2,1)S(1)} %get-tuple-element.53), branch_computations={%region_0.1_spmd, %region_1.2_spmd} | conditional | bytes 524296 | solution.py:535
  2.0 18.4 %all_to_all.26 = bf16[16,64,128]{2,1,0:T(8,128)(2,1)S(1)} all-to-all(bf16[16,64,128]{2,1,0:T(8,128)(2,1)S(1)} %bitcast.16), channel_id=1, replica_groups={{0,8,16,24,32,40,48,56,64,72,80,88,96,104,112,120},{128,136,144,152,160..., dimensions={0} | all-to-all | bytes 524288 | tf_op jit(solution)/shard_map/cond/branch_1_fun/all_to_all | solution.py:504
  20.4 0.9 %shard_map.91 = (f32[512,128]{1,0:T(8,128)S(1)}, bf16[88,128]{1,0:T(8,128)(2,1)S(1)}) custom-call(s32[1]{0:T(128)} %bitcast.8.place, bf16[1024,128]{1,0:T(8,128)(2,1)S(1)} %get-tuple-element.79.raw_ref, f32[7,128]{1,0:T(8,128)S(1)} %get-tuple-element.55.tap_ref, bf16[4,7,128,128]{3,2,1,0:T(8,128)(2,1)S(1)} %get-tuple-element.56.table_ref, ...), custom_call_target="tpu_custom_call" | custom-call | tf_op jit(solution)/shard_map/pallas_call | solution.py:457
  21.3 1.3 %collective-permute-start.1 = (bf16[88,128]{1,0:T(8,128)(2,1)S(1)}, bf16[88,128]{1,0:T(8,128)(2,1)S(1)}, u32[]{:S(2)}, u32[]{:S(2)}) collective-permute-start(bf16[88,128]{1,0:T(8,128)(2,1)S(1)} %get-tuple-element.67), channel_id=1, source_target_pairs={{0,128},{8,136},{16,144},{24,152},{32,160},{40,168},{48,176},{56,1... | collective-permute-start | bytes 67592 | tf_op jit(solution)/shard_map/ppermute | solution.py:533
  22.7 0.7 %collective-permute-start.2 = (bf16[96,128]{1,0:T(8,128)(2,1)S(1)}, bf16[96,128]{1,0:T(8,128)(2,1)S(1)}, u32[]{:S(2)}, u32[]{:S(2)}) collective-permute-start(bf16[96,128]{1,0:T(8,128)(2,1)S(1)} %get-tuple-element.68), channel_id=1, source_target_pairs={{256,384},{264,392},{272,400},{280,408},{288,416},{296,424},{304,4... | collective-permute-start | bytes 73736 | tf_op jit(solution)/shard_map/ppermute | solution.py:533
  23.4 0.1 collective-permute-done.1.got_01.got_ref
  23.5 0.7 collective-permute-start.3
  24.2 2.1 %collective-permute-start = (bf16[8,1024]{1,0:T(8,128)(2,1)S(1)}, bf16[8,1024]{1,0:T(8,128)(2,1)S(1)}, u32[]{:S(2)}, u32[]{:S(2)}) collective-permute-start(bf16[8,1024]{1,0:T(8,128)(2,1)S(1)} %get-tuple-element.62), channel_id=1, source_target_pairs={{0,8},{8,16},{16,24},{24,32},{32,40},{40,48},{48,56},{56,64},{64,7... | collective-permute-start | bytes 49160 | tf_op jit(solution)/shard_map/ppermute | solution.py:539
  26.3 0.7 %collective-permute-start.4 = (bf16[24,128]{1,0:T(8,128)(2,1)S(1)}, bf16[24,128]{1,0:T(8,128)(2,1)S(1)}, u32[]{:S(2)}, u32[]{:S(2)}) collective-permute-start(bf16[24,128]{1,0:T(8,128)(2,1)S(1)} %get-tuple-element.74), channel_id=1, source_target_pairs={{128,384},{136,392},{144,400},{152,408},{160,416},{168,424},{176,4... | collective-permute-start | bytes 18440 | tf_op jit(solution)/shard_map/ppermute | solution.py:533
  27.0 0.0 copy-start.3
  27.0 0.0 copy-start
  27.0 0.0 copy-start.1
  27.1 0.6 copy-done.3
  27.7 0.0 collective-permute-done.halo_ref
  27.7 0.2 copy-done
  27.9 0.2 shard_map.95
  28.1 0.0 collective-permute-done.2.got_23
  28.1 0.0 collective-permute-done.4.got_13
  28.2 0.0 copy-start.2
  28.2 23.6 %all_to_all.30 = bf16[16,32,128]{2,1,0:T(8,128)(2,1)S(1)} all-to-all(bf16[16,32,128]{2,1,0:T(8,128)(2,1)S(1)} %bitcast.24), channel_id=1, replica_groups={{0,8,16,24,32,40,48,56,64,72,80,88,96,104,112,120},{128,136,144,152,160..., dimensions={0} | all-to-all | bytes 262144 | tf_op jit(solution)/shard_map/all_to_all | solution.py:504
  51.8 0.3 shard_map.99
  52.1 13.0 %all_to_all.31 = f32[8,8,128]{2,1,0:T(8,128)S(1)} all-to-all(f32[8,8,128]{2,1,0:T(8,128)S(1)} %bitcast.27), channel_id=1, replica_groups=mesh['ctx'=64,'tp'=8] {'tp'}, dimensions={0} | all-to-all | bytes 65536 | tf_op jit(solution)/shard_map/all_to_all | solution.py:610
  65.1 0.8 %shard_map.100 = bf16[64,1024]{1,0:T(8,128)(2,1)} custom-call(f32[64,1024]{1,0:T(8,128)S(1)} %get-tuple-element.76.hidden_ref, f32[64,128]{1,0:T(8,128)S(1)} %bitcast.26, f32[1,1024]{1,0:T(1,128)S(1)} %get-tuple-element.78.gain_ref), custom_call_target="tpu_custom_call" | custom-call | tf_op jit(solution)/shard_map/pallas_call | solution.py:457
  (14 shorter events, 0.2 us)
Async XLA Ops:
  21.3 2.2 %collective-permute-start.1 = (bf16[88,128]{1,0:T(8,128)(2,1)S(1)}, bf16[88,128]{1,0:T(8,128)(2,1)S(1)}, u32[]{:S(2)}, u32[]{:S(2)}) collective-permute-start(bf16[88,128]{1,0:T(8,128)(2,1)S(1)} %get-tuple-element.67), channel_id=1, source_target_pairs={{0,128},{8,136},{16,144},{24,152},{32,160},{40,168},{48,176},{56,1... | collective-permute-start | bytes 67592 | tf_op jit(solution)/shard_map/ppermute | solution.py:533
  22.7 5.4 %collective-permute-start.2 = (bf16[96,128]{1,0:T(8,128)(2,1)S(1)}, bf16[96,128]{1,0:T(8,128)(2,1)S(1)}, u32[]{:S(2)}, u32[]{:S(2)}) collective-permute-start(bf16[96,128]{1,0:T(8,128)(2,1)S(1)} %get-tuple-element.68), channel_id=1, source_target_pairs={{256,384},{264,392},{272,400},{280,408},{288,416},{296,424},{304,4... | collective-permute-start | bytes 73736 | tf_op jit(solution)/shard_map/ppermute | solution.py:533
  23.5 4.6 %collective-permute-start.3 = (bf16[88,128]{1,0:T(8,128)(2,1)S(1)}, bf16[88,128]{1,0:T(8,128)(2,1)S(1)}, u32[]{:S(2)}, u32[]{:S(2)}) collective-permute-start(bf16[88,128]{1,0:T(8,128)(2,1)S(1)} %get-tuple-element.73), channel_id=1, source_target_pairs={{128,256},{136,264},{144,272},{152,280},{160,288},{168,296},{176,3... | collective-permute-start | bytes 67592 | tf_op jit(solution)/shard_map/ppermute | solution.py:533
  24.2 3.5 %collective-permute-start = (bf16[8,1024]{1,0:T(8,128)(2,1)S(1)}, bf16[8,1024]{1,0:T(8,128)(2,1)S(1)}, u32[]{:S(2)}, u32[]{:S(2)}) collective-permute-start(bf16[8,1024]{1,0:T(8,128)(2,1)S(1)} %get-tuple-element.62), channel_id=1, source_target_pairs={{0,8},{8,16},{16,24},{24,32},{32,40},{40,48},{48,56},{56,64},{64,7... | collective-permute-start | bytes 49160 | tf_op jit(solution)/shard_map/ppermute | solution.py:539
  26.3 1.8 %collective-permute-start.4 = (bf16[24,128]{1,0:T(8,128)(2,1)S(1)}, bf16[24,128]{1,0:T(8,128)(2,1)S(1)}, u32[]{:S(2)}, u32[]{:S(2)}) collective-permute-start(bf16[24,128]{1,0:T(8,128)(2,1)S(1)} %get-tuple-element.74), channel_id=1, source_target_pairs={{128,384},{136,392},{144,400},{152,408},{160,416},{168,424},{176,4... | collective-permute-start | bytes 18440 | tf_op jit(solution)/shard_map/ppermute | solution.py:533
  27.0 0.7 %copy-start.3 = (bf16[1024]{0:T(1024)(128)(2,1)S(1)}, bf16[1024]{0:T(1024)(128)(2,1)}, u32[]{:S(2)}) copy-start(bf16[1024]{0:T(1024)(128)(2,1)} %param.25) | copy-start | bytes 6148
  27.0 0.9 %copy-start = (bf16[64,1024]{1,0:T(8,128)(2,1)S(1)}, bf16[64,1024]{1,0:T(8,128)(2,1)}, u32[]{:S(2)}) copy-start(bf16[64,1024]{1,0:T(8,128)(2,1)} %outer_ref.1) | copy-start | bytes 393220
  27.0 0.9 %copy-start.1 = (bf16[3,7,1024]{2,1,0:T(8,128)(2,1)S(1)}, bf16[3,7,1024]{2,1,0:T(8,128)(2,1)}, u32[]{:S(2)}) copy-start(bf16[3,7,1024]{2,1,0:T(8,128)(2,1)} %tap_ref.1) | copy-start | bytes 129028
  28.2 23.6 %copy-start.2 = (bf16[64,1024]{1,0:T(8,128)(2,1)S(1)}, bf16[64,1024]{1,0:T(8,128)(2,1)}, u32[]{:S(2)}) copy-start(bf16[64,1024]{1,0:T(8,128)(2,1)} %residual_ref.1) | copy-start | bytes 393220

commit v10 on v9

--- a/solution.py
+++ b/solution.py
@@ -133,8 +133,13 @@
         rest_ref[rows] = jnp.broadcast_to(jnp.exp(-rate_lanes * (block * (NEAR - 1))), (8, LANES))
 
 
-def begin_kernel(place, inner, value, outer, decay, residue, medium, taps, raw, tail, *tables):
-    pack_kernel(inner, value, outer, raw, tail)
+def begin_kernel(
+    place, inner, value, outer, gain, decay, residue, medium, taps, raw, tail, outer_out, tap_out, gain_out, *tables
+):
+    outer_out[...] = outer[...]
+    tap_out[0] = taps[0].astype(F32)
+    gain_out[...] = gain[...]
+    pack_kernel(inner, value, outer.at[outer.shape[0] - HALO :], raw, tail)
     tables_kernel(place, decay, residue, medium, taps, *tables)
 
 
@@ -327,13 +332,13 @@
     return dot(two_parts(jnp.concatenate(states, 0), width), table)
 
 
-def joined(width, got, local_ref, raw_ref, tap_ref, table_ref, step_ref):
+def joined(width, got, farther, local_ref, raw_ref, tap_ref, table_ref, step_ref):
     count = table_ref.shape[0]
     rows = 8 * count
     blocks = local_ref.shape[0] // rows
     one, two, end = rows // 2, rows // 2 + rows, rows // 2 + 2 * rows
     own_slab = missing(tap_ref, got[end : end + EDGE], raw_ref[:EDGE].astype(F32))
-    incoming = unpack_state(got[:one], width)
+    incoming = unpack_state(got[:one], width) + farther
     added = to_states(table_ref, own_slab)
     zeros = jnp.zeros((8, LANES), F32)
     parts = []
@@ -351,13 +356,11 @@
     return local_ref[...] + jnp.concatenate(parts, 1).reshape(local_ref.shape)
 
 
-def join_kernel(
-    width, place, local_ref, got_01, got_23, raw_ref, tap_ref, table_ref, step_ref, out_ref
-):
-    @pl.when(lax.rem(super_block(place), 2) == 1)
+def join_kernel(width, place, local_ref, got_01, raw_ref, tap_ref, table_ref, step_ref, out_ref):
+    @pl.when(super_block(place) == 1)
     def _():
-        got = got_01[...].astype(F32) + got_23[: got_01.shape[0]].astype(F32)
-        out_ref[...] = joined(width, got, local_ref, raw_ref, tap_ref, table_ref, step_ref)
+        got = got_01[...].astype(F32)
+        out_ref[...] = joined(width, got, 0.0, local_ref, raw_ref, tap_ref, table_ref, step_ref)
 
 
 def finish_kernel(
@@ -374,8 +377,10 @@
     jump_ref,
     rest_ref,
     out_ref,
+    farther,
 ):
     here = super_block(place)
+    half = farther.shape[0] // 2
 
     @pl.when(here < 2)
     def _():
@@ -383,26 +388,20 @@
 
     @pl.when(here == 2)
     def _():
-        got = got_12[...].astype(F32)
-        total = joined(width, got, near_ref, raw_ref, tap_ref, table_ref, step_ref)
-        out_ref[...] = total.astype(BF16)
+        farther[...] = jnp.zeros_like(farther)
 
     @pl.when(here == 3)
     def _():
-        count = table_ref.shape[0]
-        rows = 8 * count
-        blocks = near_ref.shape[0] // rows
-        far_tail = got_13[rows // 2 :].astype(F32)
+        tail = got_13[half:].astype(F32)
         head = got_23[got_23.shape[0] - EDGE :].astype(F32)
-        incoming = rest_ref[...] * to_states(table_ref, missing(tap_ref, far_tail, head))
-        incoming = incoming + jump_ref[...] * unpack_state(got_13[: rows // 2], width)
-        parts = []
-        for q in range(count):
-            at = slice(8 * q, 8 * q + 8)
-            mixed = spread(width, incoming[at], step_ref[at], table_ref[q, 6], blocks)
-            parts.append(mixed.reshape(blocks, 8, LANES))
-        total = near_ref[...] + jnp.concatenate(parts, 1).reshape(near_ref.shape)
-        out_ref[...] = total.astype(BF16)
+        incoming = rest_ref[...] * to_states(table_ref, missing(tap_ref, tail, head))
+        farther[...] = incoming + jump_ref[...] * unpack_state(got_13[:half], width)
+
+    @pl.when(here > 1)
+    def _():
+        got = got_12[...].astype(F32) + got_23[: got_12.shape[0]].astype(F32)
+        known = (near_ref, raw_ref, tap_ref, table_ref, step_ref)
+        out_ref[...] = joined(width, got, farther[...], *known).astype(BF16)
 
 
 def hidden_kernel(mixed_ref, outer_ref, residual_ref, hidden_ref, sum_ref):
@@ -475,20 +474,24 @@
     small = (decay_rates.T, residues.T, medium_taps.T, feature_taps)
     part = pl.BlockSpec((rows, channels), lambda i: (0, 0))
     lines = pltpu.VMEM((pack, LANES), F32)
-    raw, outer_tail, table, step, jump, rest, taps = pl.pallas_call(
+    raw, outer_tail, outer_input, outer_taps, norm_gain, table, step, jump, rest, taps = pl.pallas_call(
         begin_kernel,
         grid=(1,),
         in_specs=[
             smem,
             part,
             part,
-            pl.BlockSpec((HALO, channels), lambda i: (rows // HALO - 1, 0)),
+            part,
+            pl.BlockSpec((channels,), lambda i: (0,)),
             *[pl.BlockSpec(x.shape, lambda i, n=x.ndim: (0,) * n) for x in small],
         ],
-        out_specs=[vmem] * 7,
+        out_specs=[vmem] * 10,
         out_shape=[
             pltpu.VMEM((NEAR * rows, LANES), BF16),
             pltpu.VMEM((HALO, channels), BF16),
+            pltpu.VMEM((rows, channels), BF16),
+            pltpu.VMEM((1, FEAT, channels), F32),
+            pltpu.VMEM((channels,), BF16),
             pltpu.VMEM((count, 7, LANES, LANES), BF16),
             lines,
             lines,
@@ -496,7 +499,7 @@
             pltpu.VMEM((FEAT, LANES), F32),
         ],
         name="begin",
-    )(place, inner_input, value_input, outer_input, *small)
+    )(place, inner_input, value_input, outer_input, norm_gain, *small)
     neighbours = [[NEAR * f + n for n in range(NEAR)] for f in range(far)]
 
     def exchange(x):
@@ -565,7 +568,7 @@
         [pltpu.VMEM((rows, channels), F32), pltpu.VMEM((1, channels), F32)],
         halo,
         outer_input,
-        feature_taps,
+        outer_taps,
         norm_gain.reshape(1, channels),
         scratch=[pltpu.VMEM((tiles, HALO + rows, LANES), F32)],
     )
@@ -577,7 +580,6 @@
         whole,
         local,
         got_01,
-        got_23,
         arrived,
         taps,
         table,
@@ -599,6 +601,7 @@
         jump,
         rest,
         scalars=(place,),
+        scratch=[ends],
     )
     hidden, sums = call(
         hidden_kernel,

time: 66.2 us -> 66.1 us (level)
  local copies, waits for them, and re-layouts: 0.9 us -> 0.03 us
    unnamed x8 -> x2, local copies, waits for them, and re-layouts: 0.88 us -> 0.01 us
  transfers between devices with their start and end apart: 5 -> 5, of which waited for: 1 -> 2; matrix products, arithmetic and copies ran while one was open for 0% -> 0% of each run, Pallas kernels for 0% -> 0%
where the time goes in v10:
time: 66.1 us; the launch traced here: 65.8 us
  blocking collectives  55.5 us (84%)
  starting transfers between devices  5.4 us (8%)
  Pallas kernels  4.29 us (6%)
    all_to_all x2, blocking collectives, exchange(): lax.all_to_all(x.reshape(slab), 'ctx', 0, 0, axis_index_groups=neighbours)  42 us
    all_to_all x1, blocking collectives, on_device(): all_sums = lax.all_to_all(sums.reshape(parts, 8, LANES), 'tp', 0, 0)  13.5 us
    ppermute x4, starting transfers between devices, passed(): return lax.ppermute(x, 'ctx', pairs)  3.27 us
    pallas_call x10, Pallas kernels, call(): pl.pallas_call(kernel, in_specs=[smem] * len(scalars) + [vmem] * len(arra...  2.28 us
    ppermute x1, starting transfers between devices, on_device(): lax.ppermute(outer_tail, 'ctx', [(i, i + 1) for i in range(size - 1)])  2.14 us
    pallas_call x1, Pallas kernels, on_device(): pl.pallas_call(begin_kernel, grid=(1,), in_specs=[smem, part, part, part,...  2.01 us
  transfers between devices with their start and end apart: 5, of which 2 were waited for; matrix products, arithmetic and copies ran while one was open for 0% of the time, Pallas kernels for 0%

profile of v10, /device:TPU:1, one launch (start us, length us, event | category | flops | bytes accessed | tf_op | source)
XLA Modules:
  0.0 65.8 jit_solution(822586876635456436)
XLA Ops:
  0.0 2.0 %begin.1 = (bf16[1024,128]{1,0:T(8,128)(2,1)S(1)}, bf16[8,1024]{1,0:T(8,128)(2,1)S(1)}, bf16[64,1024]{1,0:T(8,128)(2,1)S(1)}, f32[1,7,1024]{2,1,0:T(8,128)S(1)},...) custom-call(s32[1]{0:T(128)} %bitcast.8.place, ...), custom_call_target="tpu_custom_call" | custom-call | tf_op jit(solution)/shard_map/begin/pallas_call | solution.py:477
  2.0 18.4 %conditional.4 = (bf16[1024,128]{1,0:T(8,128)(2,1)S(1)}) conditional(s32[]{:T(128)} %convert_element_type.15, bf16[1024,128]{1,0:T(8,128)(2,1)S(1)} %get-tuple-element.57, bf16[1024,128]{1,0:T(8,128)(2,1)S(1)} %get-tuple-element.57), branch_computations={%region_0.1_spmd, %region_1.2_spmd} | conditional | bytes 524296 | solution.py:538
  2.0 18.4 %all_to_all.26 = bf16[16,64,128]{2,1,0:T(8,128)(2,1)S(1)} all-to-all(bf16[16,64,128]{2,1,0:T(8,128)(2,1)S(1)} %bitcast.16), channel_id=1, replica_groups={{0,8,16,24,32,40,48,56,64,72,80,88,96,104,112,120},{128,136,144,152,160..., dimensions={0} | all-to-all | bytes 524288 | tf_op jit(solution)/shard_map/cond/branch_1_fun/all_to_all | solution.py:507
  20.4 0.9 %shard_map.91 = (f32[512,128]{1,0:T(8,128)S(1)}, bf16[88,128]{1,0:T(8,128)(2,1)S(1)}) custom-call(s32[1]{0:T(128)} %bitcast.8.place, bf16[1024,128]{1,0:T(8,128)(2,1)S(1)} %get-tuple-element.85.raw_ref, f32[7,128]{1,0:T(8,128)S(1)} %get-tuple-element.59.tap_ref, bf16[4,7,128,128]{3,2,1,0:T(8,128)(2,1)S(1)} %get-tuple-element.60.table_ref, ...), custom_call_target="tpu_custom_call" | custom-call | tf_op jit(solution)/shard_map/pallas_call | solution.py:456
  21.4 1.3 %collective-permute-start.1 = (bf16[88,128]{1,0:T(8,128)(2,1)S(1)}, bf16[88,128]{1,0:T(8,128)(2,1)S(1)}, u32[]{:S(2)}, u32[]{:S(2)}) collective-permute-start(bf16[88,128]{1,0:T(8,128)(2,1)S(1)} %get-tuple-element.73), channel_id=1, source_target_pairs={{0,128},{8,136},{16,144},{24,152},{32,160},{40,168},{48,176},{56,1... | collective-permute-start | bytes 67592 | tf_op jit(solution)/shard_map/ppermute | solution.py:536
  22.8 0.7 %collective-permute-start.3 = (bf16[96,128]{1,0:T(8,128)(2,1)S(1)}, bf16[96,128]{1,0:T(8,128)(2,1)S(1)}, u32[]{:S(2)}, u32[]{:S(2)}) collective-permute-start(bf16[96,128]{1,0:T(8,128)(2,1)S(1)} %get-tuple-element.79), channel_id=1, source_target_pairs={{256,384},{264,392},{272,400},{280,408},{288,416},{296,424},{304,4... | collective-permute-start | bytes 73736 | tf_op jit(solution)/shard_map/ppermute | solution.py:536
  23.4 0.1 collective-permute-done.1.got_01.got_ref
  23.6 0.7 collective-permute-start.2
  24.2 2.1 %collective-permute-start = (bf16[8,1024]{1,0:T(8,128)(2,1)S(1)}, bf16[8,1024]{1,0:T(8,128)(2,1)S(1)}, u32[]{:S(2)}, u32[]{:S(2)}) collective-permute-start(bf16[8,1024]{1,0:T(8,128)(2,1)S(1)} %get-tuple-element.66), channel_id=1, source_target_pairs={{0,8},{8,16},{16,24},{24,32},{32,40},{40,48},{48,56},{56,64},{64,7... | collective-permute-start | bytes 49160 | tf_op jit(solution)/shard_map/ppermute | solution.py:542
  26.4 0.7 %collective-permute-start.4 = (bf16[24,128]{1,0:T(8,128)(2,1)S(1)}, bf16[24,128]{1,0:T(8,128)(2,1)S(1)}, u32[]{:S(2)}, u32[]{:S(2)}) collective-permute-start(bf16[24,128]{1,0:T(8,128)(2,1)S(1)} %get-tuple-element.80), channel_id=1, source_target_pairs={{128,384},{136,392},{144,400},{152,408},{160,416},{168,424},{176,4... | collective-permute-start | bytes 18440 | tf_op jit(solution)/shard_map/ppermute | solution.py:536
  27.1 0.1 collective-permute-done.halo_ref
  27.2 0.1 shard_map.95
  27.4 0.0 collective-permute-done.3.got_23
  27.4 0.0 collective-permute-done.4.got_13
  27.4 0.0 collective-permute-done.2.got_12
  27.5 0.0 copy-start
  27.5 23.6 %all_to_all.30 = bf16[16,32,128]{2,1,0:T(8,128)(2,1)S(1)} all-to-all(bf16[16,32,128]{2,1,0:T(8,128)(2,1)S(1)} %bitcast.24), channel_id=1, replica_groups={{0,8,16,24,32,40,48,56,64,72,80,88,96,104,112,120},{128,136,144,152,160..., dimensions={0} | all-to-all | bytes 262144 | tf_op jit(solution)/shard_map/all_to_all | solution.py:507
  51.1 0.0 copy-done
  51.1 0.3 shard_map.99
  51.5 13.5 %all_to_all.31 = f32[8,8,128]{2,1,0:T(8,128)S(1)} all-to-all(f32[8,8,128]{2,1,0:T(8,128)S(1)} %bitcast.27), channel_id=1, replica_groups=mesh['ctx'=64,'tp'=8] {'tp'}, dimensions={0} | all-to-all | bytes 65536 | tf_op jit(solution)/shard_map/all_to_all | solution.py:613
  65.0 0.8 %shard_map.100 = bf16[64,1024]{1,0:T(8,128)(2,1)} custom-call(f32[64,1024]{1,0:T(8,128)S(1)} %get-tuple-element.82.hidden_ref, f32[64,128]{1,0:T(8,128)S(1)} %bitcast.26, f32[1,1024]{1,0:T(1,128)S(1)} %get-tuple-element.84.gain_ref), custom_call_target="tpu_custom_call" | custom-call | tf_op jit(solution)/shard_map/pallas_call | solution.py:456
  (11 shorter events, 0.2 us)
Async XLA Ops:
  21.4 2.2 %collective-permute-start.1 = (bf16[88,128]{1,0:T(8,128)(2,1)S(1)}, bf16[88,128]{1,0:T(8,128)(2,1)S(1)}, u32[]{:S(2)}, u32[]{:S(2)}) collective-permute-start(bf16[88,128]{1,0:T(8,128)(2,1)S(1)} %get-tuple-element.73), channel_id=1, source_target_pairs={{0,128},{8,136},{16,144},{24,152},{32,160},{40,168},{48,176},{56,1... | collective-permute-start | bytes 67592 | tf_op jit(solution)/shard_map/ppermute | solution.py:536
  22.8 4.6 %collective-permute-start.3 = (bf16[96,128]{1,0:T(8,128)(2,1)S(1)}, bf16[96,128]{1,0:T(8,128)(2,1)S(1)}, u32[]{:S(2)}, u32[]{:S(2)}) collective-permute-start(bf16[96,128]{1,0:T(8,128)(2,1)S(1)} %get-tuple-element.79), channel_id=1, source_target_pairs={{256,384},{264,392},{272,400},{280,408},{288,416},{296,424},{304,4... | collective-permute-start | bytes 73736 | tf_op jit(solution)/shard_map/ppermute | solution.py:536
  23.6 3.9 %collective-permute-start.2 = (bf16[88,128]{1,0:T(8,128)(2,1)S(1)}, bf16[88,128]{1,0:T(8,128)(2,1)S(1)}, u32[]{:S(2)}, u32[]{:S(2)}) collective-permute-start(bf16[88,128]{1,0:T(8,128)(2,1)S(1)} %get-tuple-element.78), channel_id=1, source_target_pairs={{128,256},{136,264},{144,272},{152,280},{160,288},{168,296},{176,3... | collective-permute-start | bytes 67592 | tf_op jit(solution)/shard_map/ppermute | solution.py:536
  24.2 3.0 %collective-permute-start = (bf16[8,1024]{1,0:T(8,128)(2,1)S(1)}, bf16[8,1024]{1,0:T(8,128)(2,1)S(1)}, u32[]{:S(2)}, u32[]{:S(2)}) collective-permute-start(bf16[8,1024]{1,0:T(8,128)(2,1)S(1)} %get-tuple-element.66), channel_id=1, source_target_pairs={{0,8},{8,16},{16,24},{24,32},{32,40},{40,48},{48,56},{56,64},{64,7... | collective-permute-start | bytes 49160 | tf_op jit(solution)/shard_map/ppermute | solution.py:542
  26.4 1.0 %collective-permute-start.4 = (bf16[24,128]{1,0:T(8,128)(2,1)S(1)}, bf16[24,128]{1,0:T(8,128)(2,1)S(1)}, u32[]{:S(2)}, u32[]{:S(2)}) collective-permute-start(bf16[24,128]{1,0:T(8,128)(2,1)S(1)} %get-tuple-element.80), channel_id=1, source_target_pairs={{128,384},{136,392},{144,400},{152,408},{160,416},{168,424},{176,4... | collective-permute-start | bytes 18440 | tf_op jit(solution)/shard_map/ppermute | solution.py:536
  27.5 23.6 %copy-start = (bf16[64,1024]{1,0:T(8,128)(2,1)S(1)}, bf16[64,1024]{1,0:T(8,128)(2,1)}, u32[]{:S(2)}) copy-start(bf16[64,1024]{1,0:T(8,128)(2,1)} %residual_ref.1) | copy-start | bytes 393220

commit v11 on v10

--- a/solution.py
+++ b/solution.py
@@ -133,13 +133,8 @@
         rest_ref[rows] = jnp.broadcast_to(jnp.exp(-rate_lanes * (block * (NEAR - 1))), (8, LANES))
 
 
-def begin_kernel(
-    place, inner, value, outer, gain, decay, residue, medium, taps, raw, tail, outer_out, tap_out, gain_out, *tables
-):
-    outer_out[...] = outer[...]
-    tap_out[0] = taps[0].astype(F32)
-    gain_out[...] = gain[...]
-    pack_kernel(inner, value, outer.at[outer.shape[0] - HALO :], raw, tail)
+def begin_kernel(place, inner, value, outer, decay, residue, medium, taps, raw, tail, *tables):
+    pack_kernel(inner, value, outer, raw, tail)
     tables_kernel(place, decay, residue, medium, taps, *tables)
 
 
@@ -474,24 +469,20 @@
     small = (decay_rates.T, residues.T, medium_taps.T, feature_taps)
     part = pl.BlockSpec((rows, channels), lambda i: (0, 0))
     lines = pltpu.VMEM((pack, LANES), F32)
-    raw, outer_tail, outer_input, outer_taps, norm_gain, table, step, jump, rest, taps = pl.pallas_call(
+    raw, outer_tail, table, step, jump, rest, taps = pl.pallas_call(
         begin_kernel,
         grid=(1,),
         in_specs=[
             smem,
             part,
             part,
-            part,
-            pl.BlockSpec((channels,), lambda i: (0,)),
+            pl.BlockSpec((HALO, channels), lambda i: (rows // HALO - 1, 0)),
             *[pl.BlockSpec(x.shape, lambda i, n=x.ndim: (0,) * n) for x in small],
         ],
-        out_specs=[vmem] * 10,
+        out_specs=[vmem] * 7,
         out_shape=[
             pltpu.VMEM((NEAR * rows, LANES), BF16),
             pltpu.VMEM((HALO, channels), BF16),
-            pltpu.VMEM((rows, channels), BF16),
-            pltpu.VMEM((1, FEAT, channels), F32),
-            pltpu.VMEM((channels,), BF16),
             pltpu.VMEM((count, 7, LANES, LANES), BF16),
             lines,
             lines,
@@ -499,7 +490,7 @@
             pltpu.VMEM((FEAT, LANES), F32),
         ],
         name="begin",
-    )(place, inner_input, value_input, outer_input, norm_gain, *small)
+    )(place, inner_input, value_input, outer_input, *small)
     neighbours = [[NEAR * f + n for n in range(NEAR)] for f in range(far)]
 
     def exchange(x):
@@ -568,7 +559,7 @@
         [pltpu.VMEM((rows, channels), F32), pltpu.VMEM((1, channels), F32)],
         halo,
         outer_input,
-        outer_taps,
+        feature_taps,
         norm_gain.reshape(1, channels),
         scratch=[pltpu.VMEM((tiles, HALO + rows, LANES), F32)],
     )

time: 66.1 us -> 66.2 us (level)
  local copies, waits for them, and re-layouts: 0.03 us -> 0.9 us
    unnamed x2 -> x8, local copies, waits for them, and re-layouts: 0.01 us -> 0.88 us
  transfers between devices with their start and end apart: 5 -> 5, of which waited for: 2 -> 1; matrix products, arithmetic and copies ran while one was open for 0% -> 0% of each run, Pallas kernels for 0% -> 0%
where the time goes in v11:
time: 66.2 us; the launch traced here: 65.9 us
  blocking collectives  55 us (83%)
  starting transfers between devices  5.4 us (8%)
  Pallas kernels  4.24 us (6%)
  local copies, waits for them, and re-layouts  0.9 us (1%)
    all_to_all x2, blocking collectives, exchange(): lax.all_to_all(x.reshape(slab), 'ctx', 0, 0, axis_index_groups=neighbours)  41.9 us
    all_to_all x1, blocking collectives, on_device(): all_sums = lax.all_to_all(sums.reshape(parts, 8, LANES), 'tp', 0, 0)  13 us
    ppermute x4, starting transfers between devices, passed(): return lax.ppermute(x, 'ctx', pairs)  3.27 us
    pallas_call x10, Pallas kernels, call(): pl.pallas_call(kernel, in_specs=[smem] * len(scalars) + [vmem] * len(arra...  2.3 us
    ppermute x1, starting transfers between devices, on_device(): lax.ppermute(outer_tail, 'ctx', [(i, i + 1) for i in range(size - 1)])  2.14 us
    pallas_call x1, Pallas kernels, on_device(): pl.pallas_call(begin_kernel, grid=(1,), in_specs=[smem, part, part, pl.Bl...  1.94 us
  transfers between devices with their start and end apart: 5, of which 1 were waited for; matrix products, arithmetic and copies ran while one was open for 0% of the time, Pallas kernels for 0%

profile of v11, /device:TPU:1, one launch (start us, length us, event | category | flops | bytes accessed | tf_op | source)
XLA Modules:
  0.0 65.9 jit_solution(3280019266620549503)
XLA Ops:
  0.0 1.9 %begin.1 = (bf16[1024,128]{1,0:T(8,128)(2,1)S(1)}, bf16[8,1024]{1,0:T(8,128)(2,1)S(1)}, bf16[4,7,128,128]{3,2,1,0:T(8,128)(2,1)S(1)}, f32[32,128]{1,0:T(8,128)S(...) custom-call(s32[1]{0:T(128)} %bitcast.8.place, bf16[64,1024]{1,0:T(8,128)(2,1)} %inner.1, ...), custom_call_target="tpu_custom_call" | custom-call | tf_op jit(solution)/shard_map/begin/pallas_call | solution.py:472
  1.9 18.4 %conditional.4 = (bf16[1024,128]{1,0:T(8,128)(2,1)S(1)}) conditional(s32[]{:T(128)} %convert_element_type.15, bf16[1024,128]{1,0:T(8,128)(2,1)S(1)} %get-tuple-element.53, bf16[1024,128]{1,0:T(8,128)(2,1)S(1)} %get-tuple-element.53), branch_computations={%region_0.1_spmd, %region_1.2_spmd} | conditional | bytes 524296 | solution.py:529
  2.0 18.4 %all_to_all.26 = bf16[16,64,128]{2,1,0:T(8,128)(2,1)S(1)} all-to-all(bf16[16,64,128]{2,1,0:T(8,128)(2,1)S(1)} %bitcast.16), channel_id=1, replica_groups={{0,8,16,24,32,40,48,56,64,72,80,88,96,104,112,120},{128,136,144,152,160..., dimensions={0} | all-to-all | bytes 524288 | tf_op jit(solution)/shard_map/cond/branch_1_fun/all_to_all | solution.py:498
  20.4 0.9 %shard_map.91 = (f32[512,128]{1,0:T(8,128)S(1)}, bf16[88,128]{1,0:T(8,128)(2,1)S(1)}) custom-call(s32[1]{0:T(128)} %bitcast.8.place, bf16[1024,128]{1,0:T(8,128)(2,1)S(1)} %get-tuple-element.79.raw_ref, f32[7,128]{1,0:T(8,128)S(1)} %get-tuple-element.55.tap_ref, bf16[4,7,128,128]{3,2,1,0:T(8,128)(2,1)S(1)} %get-tuple-element.56.table_ref, ...), custom_call_target="tpu_custom_call" | custom-call | tf_op jit(solution)/shard_map/pallas_call | solution.py:451
  21.3 1.3 %collective-permute-start.1 = (bf16[88,128]{1,0:T(8,128)(2,1)S(1)}, bf16[88,128]{1,0:T(8,128)(2,1)S(1)}, u32[]{:S(2)}, u32[]{:S(2)}) collective-permute-start(bf16[88,128]{1,0:T(8,128)(2,1)S(1)} %get-tuple-element.67), channel_id=1, source_target_pairs={{0,128},{8,136},{16,144},{24,152},{32,160},{40,168},{48,176},{56,1... | collective-permute-start | bytes 67592 | tf_op jit(solution)/shard_map/ppermute | solution.py:527
  22.7 0.7 %collective-permute-start.3 = (bf16[96,128]{1,0:T(8,128)(2,1)S(1)}, bf16[96,128]{1,0:T(8,128)(2,1)S(1)}, u32[]{:S(2)}, u32[]{:S(2)}) collective-permute-start(bf16[96,128]{1,0:T(8,128)(2,1)S(1)} %get-tuple-element.73), channel_id=1, source_target_pairs={{256,384},{264,392},{272,400},{280,408},{288,416},{296,424},{304,4... | collective-permute-start | bytes 73736 | tf_op jit(solution)/shard_map/ppermute | solution.py:527
  23.4 0.1 collective-permute-done.1.got_01.got_ref
  23.5 0.7 collective-permute-start.2
  24.2 2.1 %collective-permute-start = (bf16[8,1024]{1,0:T(8,128)(2,1)S(1)}, bf16[8,1024]{1,0:T(8,128)(2,1)S(1)}, u32[]{:S(2)}, u32[]{:S(2)}) collective-permute-start(bf16[8,1024]{1,0:T(8,128)(2,1)S(1)} %get-tuple-element.62), channel_id=1, source_target_pairs={{0,8},{8,16},{16,24},{24,32},{32,40},{40,48},{48,56},{56,64},{64,7... | collective-permute-start | bytes 49160 | tf_op jit(solution)/shard_map/ppermute | solution.py:533
  26.3 0.7 %collective-permute-start.4 = (bf16[24,128]{1,0:T(8,128)(2,1)S(1)}, bf16[24,128]{1,0:T(8,128)(2,1)S(1)}, u32[]{:S(2)}, u32[]{:S(2)}) collective-permute-start(bf16[24,128]{1,0:T(8,128)(2,1)S(1)} %get-tuple-element.74), channel_id=1, source_target_pairs={{128,384},{136,392},{144,400},{152,408},{160,416},{168,424},{176,4... | collective-permute-start | bytes 18440 | tf_op jit(solution)/shard_map/ppermute | solution.py:527
  27.0 0.0 copy-start.3
  27.0 0.0 copy-start
  27.0 0.0 copy-start.1
  27.1 0.6 copy-done.3
  27.7 0.0 collective-permute-done.halo_ref
  27.7 0.2 copy-done
  27.9 0.2 shard_map.95
  28.1 0.0 collective-permute-done.3.got_23
  28.1 0.0 collective-permute-done.4.got_13
  28.2 0.0 copy-start.2
  28.2 23.6 %all_to_all.30 = bf16[16,32,128]{2,1,0:T(8,128)(2,1)S(1)} all-to-all(bf16[16,32,128]{2,1,0:T(8,128)(2,1)S(1)} %bitcast.24), channel_id=1, replica_groups={{0,8,16,24,32,40,48,56,64,72,80,88,96,104,112,120},{128,136,144,152,160..., dimensions={0} | all-to-all | bytes 262144 | tf_op jit(solution)/shard_map/all_to_all | solution.py:498
  51.8 0.3 shard_map.99
  52.1 13.0 %all_to_all.31 = f32[8,8,128]{2,1,0:T(8,128)S(1)} all-to-all(f32[8,8,128]{2,1,0:T(8,128)S(1)} %bitcast.27), channel_id=1, replica_groups=mesh['ctx'=64,'tp'=8] {'tp'}, dimensions={0} | all-to-all | bytes 65536 | tf_op jit(solution)/shard_map/all_to_all | solution.py:604
  65.1 0.8 %shard_map.100 = bf16[64,1024]{1,0:T(8,128)(2,1)} custom-call(f32[64,1024]{1,0:T(8,128)S(1)} %get-tuple-element.76.hidden_ref, f32[64,128]{1,0:T(8,128)S(1)} %bitcast.26, f32[1,1024]{1,0:T(1,128)S(1)} %get-tuple-element.78.gain_ref), custom_call_target="tpu_custom_call" | custom-call | tf_op jit(solution)/shard_map/pallas_call | solution.py:451
  (14 shorter events, 0.2 us)
Async XLA Ops:
  21.3 2.2 %collective-permute-start.1 = (bf16[88,128]{1,0:T(8,128)(2,1)S(1)}, bf16[88,128]{1,0:T(8,128)(2,1)S(1)}, u32[]{:S(2)}, u32[]{:S(2)}) collective-permute-start(bf16[88,128]{1,0:T(8,128)(2,1)S(1)} %get-tuple-element.67), channel_id=1, source_target_pairs={{0,128},{8,136},{16,144},{24,152},{32,160},{40,168},{48,176},{56,1... | collective-permute-start | bytes 67592 | tf_op jit(solution)/shard_map/ppermute | solution.py:527
  22.7 5.4 %collective-permute-start.3 = (bf16[96,128]{1,0:T(8,128)(2,1)S(1)}, bf16[96,128]{1,0:T(8,128)(2,1)S(1)}, u32[]{:S(2)}, u32[]{:S(2)}) collective-permute-start(bf16[96,128]{1,0:T(8,128)(2,1)S(1)} %get-tuple-element.73), channel_id=1, source_target_pairs={{256,384},{264,392},{272,400},{280,408},{288,416},{296,424},{304,4... | collective-permute-start | bytes 73736 | tf_op jit(solution)/shard_map/ppermute | solution.py:527
  23.5 4.6 %collective-permute-start.2 = (bf16[88,128]{1,0:T(8,128)(2,1)S(1)}, bf16[88,128]{1,0:T(8,128)(2,1)S(1)}, u32[]{:S(2)}, u32[]{:S(2)}) collective-permute-start(bf16[88,128]{1,0:T(8,128)(2,1)S(1)} %get-tuple-element.72), channel_id=1, source_target_pairs={{128,256},{136,264},{144,272},{152,280},{160,288},{168,296},{176,3... | collective-permute-start | bytes 67592 | tf_op jit(solution)/shard_map/ppermute | solution.py:527
  24.2 3.5 %collective-permute-start = (bf16[8,1024]{1,0:T(8,128)(2,1)S(1)}, bf16[8,1024]{1,0:T(8,128)(2,1)S(1)}, u32[]{:S(2)}, u32[]{:S(2)}) collective-permute-start(bf16[8,1024]{1,0:T(8,128)(2,1)S(1)} %get-tuple-element.62), channel_id=1, source_target_pairs={{0,8},{8,16},{16,24},{24,32},{32,40},{40,48},{48,56},{56,64},{64,7... | collective-permute-start | bytes 49160 | tf_op jit(solution)/shard_map/ppermute | solution.py:533
  26.3 1.8 %collective-permute-start.4 = (bf16[24,128]{1,0:T(8,128)(2,1)S(1)}, bf16[24,128]{1,0:T(8,128)(2,1)S(1)}, u32[]{:S(2)}, u32[]{:S(2)}) collective-permute-start(bf16[24,128]{1,0:T(8,128)(2,1)S(1)} %get-tuple-element.74), channel_id=1, source_target_pairs={{128,384},{136,392},{144,400},{152,408},{160,416},{168,424},{176,4... | collective-permute-start | bytes 18440 | tf_op jit(solution)/shard_map/ppermute | solution.py:527
  27.0 0.7 %copy-start.3 = (bf16[1024]{0:T(1024)(128)(2,1)S(1)}, bf16[1024]{0:T(1024)(128)(2,1)}, u32[]{:S(2)}) copy-start(bf16[1024]{0:T(1024)(128)(2,1)} %param.25) | copy-start | bytes 6148
  27.0 0.9 %copy-start = (bf16[64,1024]{1,0:T(8,128)(2,1)S(1)}, bf16[64,1024]{1,0:T(8,128)(2,1)}, u32[]{:S(2)}) copy-start(bf16[64,1024]{1,0:T(8,128)(2,1)} %outer_ref.1) | copy-start | bytes 393220
  27.0 0.9 %copy-start.1 = (bf16[3,7,1024]{2,1,0:T(8,128)(2,1)S(1)}, bf16[3,7,1024]{2,1,0:T(8,128)(2,1)}, u32[]{:S(2)}) copy-start(bf16[3,7,1024]{2,1,0:T(8,128)(2,1)} %tap_ref.1) | copy-start | bytes 129028
  28.2 23.6 %copy-start.2 = (bf16[64,1024]{1,0:T(8,128)(2,1)S(1)}, bf16[64,1024]{1,0:T(8,128)(2,1)}, u32[]{:S(2)}) copy-start(bf16[64,1024]{1,0:T(8,128)(2,1)} %residual_ref.1) | copy-start | bytes 393220
